TPU v7x, 32 devices: a whole 2x2x4 slice. The times are simulated.
32 devices in a mesh: fsdp: 4 (over y, x), req: 8 (over z, core).
Axes of the slice: x: 2, y: 2, z: 4, core: 2. Of those that a mesh axis runs over, the one named last changes fastest.
Arguments:
- x_prompt: bfloat16 [8, 256, 2048], P('req', 'fsdp')
- x_suffix: bfloat16 [8, 4, 256, 2048], P('req', 'fsdp')
- norm_gain: float32 [2048], replicated, may hold values from 0.1 to 1.9
- w_query: bfloat16 [2048, 1024], P('fsdp', 'req')
- w_key: bfloat16 [2048, 512], P('fsdp', 'req')
- w_value: bfloat16 [2048, 512], P('fsdp', 'req'), may hold values from -0.125 to 0.125
- query_gain: float32 [128], replicated
- key_gain: float32 [128], replicated
- adapter_down: bfloat16 [8, 16, 2048], P('fsdp'), may hold values from -0.125 to 0.125
- adapter_up: bfloat16 [8, 16, 1024], P('fsdp'), may hold values from -1.5 to 1.5
- prompt_len: int32 [8], P('req'), may hold values from 64 to 256, as said below
- member_count: int32 [8], P('req'), may hold values from 2 to 4, as said below
- suffix_len: int32 [8, 4], P('req', 'fsdp'), may hold values from 128 to 256, as said below
- adapter_id: int32 [8, 4], P('req'), may hold values from 0 to 7
- holder_slot: int32 [8], replicated, may hold values from 0 to 7, each once
Outputs:
- prompt_out: bfloat16 [8, 256, 1024], P('req', 'fsdp')
- suffix_out: bfloat16 [8, 4, 256, 1024], P('req', 'fsdp')
Inputs may be any that keep to these rules, and one draw needn't show every extreme that they name: `prompt_len`: some group's prompt has exactly 256 positions. `member_count`: some group is full. `suffix_len`: some member's suffix has exactly 256 tokens. `holder_slot`: each adapter has its own storage row.
All inputs are finite; a program needn't handle non-finite values.
Results may differ from a plain program's by a relative error of at most 0.0055.
The roundings to bfloat16 on the way count: a program that leaves them out, or rounds other values in their place, can miss the bound.
Values may be sent and summed in bfloat16 or wider, within the bound.
No kernel may reach another device: no remote copies, remote signals or barrier semaphores. Data moves between devices by JAX's collectives and lax.ppermute only.
A program may use at most 64 MiB of HBM per device.

v0:
```python
import jax
import jax.numpy as jnp
from jax import lax
from jax.sharding import PartitionSpec as P

epsilon = 1e-06
rope_base = 1000000.0
masked_low = -1e30


def norm_rows(values, gain_vector):
    return (
        values
        * lax.rsqrt(jnp.mean(values * values, axis=-1, keepdims=True) + epsilon)
        * gain_vector
    )


def rotate(heads_in, positions):
    half_dim = heads_in.shape[-1] // 2
    frequency = rope_base ** (-jnp.arange(half_dim).astype(jnp.float32) / half_dim)
    angles = positions.astype(jnp.float32)[:, None] * frequency[None, :]
    cosine = jnp.cos(angles)[:, None, :]
    sine = jnp.sin(angles)[:, None, :]
    first_half = heads_in[..., :half_dim]
    second_half = heads_in[..., half_dim:]
    return jnp.concatenate(
        [first_half * cosine - second_half * sine, second_half * cosine + first_half * sine],
        axis=-1,
    )


def shape_heads(flat_rows, gain_vector, positions, head_dim):
    per_head = flat_rows.reshape(flat_rows.shape[0], flat_rows.shape[1] // head_dim, head_dim)
    return rotate(norm_rows(per_head, gain_vector), positions)


def update(carried, scores, allowed, value_heads, pattern):
    running, denominator, summed_output = carried
    masked = jnp.where(allowed, scores, masked_low)
    newest = jnp.maximum(running, jnp.max(masked, axis=-1))
    weights = jnp.where(allowed, jnp.exp(scores - newest[..., None]), 0.0)
    factor = jnp.exp(running - newest)
    denominator = denominator * factor + jnp.sum(weights, axis=-1)
    summed_output = summed_output * factor[..., None] + jnp.einsum(
        pattern, weights.astype(jnp.bfloat16), value_heads, preferred_element_type=jnp.float32
    )
    return (newest, denominator, summed_output)


def shards(
    x_prompt,
    x_suffix,
    norm_gain,
    w_query,
    w_key,
    w_value,
    query_gain,
    key_gain,
    adapter_down,
    adapter_up,
    prompt_len,
    member_count,
    suffix_len,
    adapter_id,
    holder_slot,
):
    fsdp_rank = lax.axis_index("fsdp")
    req_count = lax.axis_size("req")
    pr_rows = x_prompt.shape[1]
    mem_dev = x_suffix.shape[1]
    suf_rows = x_suffix.shape[2]
    model_width = x_prompt.shape[2]
    head_dim = query_gain.shape[0]
    q_cols = w_query.shape[1] * req_count
    kv_cols = w_key.shape[1] * req_count
    kv_heads = kv_cols // head_dim
    group_size = q_cols // kv_cols
    row_count = pr_rows + mem_dev * suf_rows
    prompt_total = prompt_len[0]
    tokens = jnp.concatenate(
        [x_prompt[0], x_suffix[0].reshape(mem_dev * suf_rows, model_width)], axis=0
    )
    normed = norm_rows(tokens.astype(jnp.float32), norm_gain).astype(jnp.bfloat16)
    full_q, full_k, full_v = (
        lax.all_gather(w_query, "req", axis=1, tiled=True),
        lax.all_gather(w_key, "req", axis=1, tiled=True),
        lax.all_gather(w_value, "req", axis=1, tiled=True),
    )
    pieces = (
        lax.all_gather(full_q, "fsdp", axis=0, tiled=True),
        lax.all_gather(full_k, "fsdp", axis=0, tiled=True),
        lax.all_gather(full_v, "fsdp", axis=0, tiled=True),
    )
    base_q, base_k, base_v = tuple(
        (
            jnp.dot(normed, weight_piece, preferred_element_type=jnp.float32)
            for weight_piece in pieces
        )
    )
    member_ids = adapter_id[0]
    store_rows = holder_slot.shape[0]
    lookup = jnp.where(
        member_ids[:, None] == jnp.arange(store_rows)[None, :], holder_slot[None, :], 0
    )
    storage = jnp.sum(lookup, axis=1)
    store_down, store_up = (
        lax.all_gather(adapter_down, "fsdp", axis=0, tiled=True),
        lax.all_gather(adapter_up, "fsdp", axis=0, tiled=True),
    )
    mine = lax.dynamic_slice_in_dim(storage, fsdp_rank * mem_dev, mem_dev)
    select_down_matrix = jnp.take(store_down, mine, axis=0)
    select_up_matrix = jnp.take(store_up, mine, axis=0)
    suffix_input_rows = normed[pr_rows:].reshape(mem_dev, suf_rows, model_width)
    reduced_rank_rows = jnp.einsum(
        "bve,bfe->bvf", suffix_input_rows, select_down_matrix, preferred_element_type=jnp.float32
    ).astype(jnp.bfloat16)
    adapter_delta = jnp.einsum(
        "wge,wet->wgt", reduced_rank_rows, select_up_matrix, preferred_element_type=jnp.float32
    )
    query_full = jnp.concatenate(
        [base_q[:pr_rows], base_q[pr_rows:] + adapter_delta.reshape(mem_dev * suf_rows, q_cols)],
        axis=0,
    )
    prompt_pos = fsdp_rank * pr_rows + jnp.arange(pr_rows)
    suffix_pos = prompt_total + jnp.tile(jnp.arange(suf_rows), mem_dev)
    positions = jnp.concatenate([prompt_pos, suffix_pos])
    queries = (
        shape_heads(query_full, query_gain, positions, head_dim)
        .astype(jnp.bfloat16)
        .reshape(row_count, kv_heads, group_size, head_dim)
    )
    key_heads = shape_heads(base_k, key_gain, positions, head_dim).astype(jnp.bfloat16)
    value_heads = base_v.astype(jnp.bfloat16).reshape(row_count, kv_heads, head_dim)
    limits = jnp.concatenate([prompt_pos, jnp.full((mem_dev * suf_rows,), 2**30, jnp.int32)])
    score_scale = head_dim ** (-0.5)
    start_state = (
        jnp.full((row_count, kv_heads, group_size), masked_low, jnp.float32),
        jnp.zeros((row_count, kv_heads, group_size), jnp.float32),
        jnp.zeros((row_count, kv_heads, group_size, head_dim), jnp.float32),
    )
    prompt_k_flat = key_heads[:pr_rows].reshape(pr_rows, kv_cols)
    prompt_v_flat = value_heads[:pr_rows].reshape(pr_rows, kv_cols)
    piece_keys = lax.all_gather(prompt_k_flat, "fsdp", axis=0, tiled=True)
    piece_values = lax.all_gather(prompt_v_flat, "fsdp", axis=0, tiled=True)
    piece_rows = piece_keys.shape[0]
    key_pos = jnp.arange(piece_rows)
    allowed = (key_pos[None, :] < prompt_total) & (key_pos[None, :] <= limits[:, None])
    scores = (
        jnp.einsum(
            "rkgd,nkd->rkgn",
            queries,
            piece_keys.reshape(piece_rows, kv_heads, head_dim),
            preferred_element_type=jnp.float32,
        )
        * score_scale
    )
    carried = update(
        start_state,
        scores,
        allowed[:, None, None, :],
        piece_values.reshape(piece_rows, kv_heads, head_dim),
        "rkgn,nkd->rkgd",
    )
    suffix_state = tuple(
        (
            state_part[pr_rows:].reshape((mem_dev, suf_rows) + state_part.shape[1:])
            for state_part in carried
        )
    )
    suffix_q = queries[pr_rows:].reshape(mem_dev, suf_rows, kv_heads, group_size, head_dim)
    suffix_k = key_heads[pr_rows:].reshape(mem_dev, suf_rows, kv_heads, head_dim)
    suffix_v = value_heads[pr_rows:].reshape(mem_dev, suf_rows, kv_heads, head_dim)
    own_scores = (
        jnp.einsum("mskgd,mtkd->mskgt", suffix_q, suffix_k, preferred_element_type=jnp.float32)
        * score_scale
    )
    causal = jnp.arange(suf_rows)[None, :] <= jnp.arange(suf_rows)[:, None]
    suffix_state = update(
        suffix_state, own_scores, causal[None, :, None, None, :], suffix_v, "mskgt,mtkd->mskgd"
    )
    denominator = jnp.concatenate(
        [carried[1][:pr_rows], suffix_state[1].reshape(mem_dev * suf_rows, kv_heads, group_size)],
        axis=0,
    )
    summed_output = jnp.concatenate(
        [
            carried[2][:pr_rows],
            suffix_state[2].reshape(mem_dev * suf_rows, kv_heads, group_size, head_dim),
        ],
        axis=0,
    )
    attended = (summed_output / denominator[..., None]).reshape(row_count, q_cols)
    member_index = fsdp_rank * mem_dev + jnp.arange(mem_dev)
    suffix_ok = (member_index < member_count[0])[:, None] & (
        jnp.arange(suf_rows)[None, :] < suffix_len[0][:, None]
    )
    valid_rows = jnp.concatenate([prompt_pos < prompt_total, suffix_ok.reshape(mem_dev * suf_rows)])
    result = jnp.where(valid_rows[:, None], attended, 0.0).astype(jnp.bfloat16)
    return (result[:pr_rows][None], result[pr_rows:].reshape(1, mem_dev, suf_rows, q_cols))


def solution(mesh):
    return jax.shard_map(
        shards,
        mesh=mesh,
        in_specs=(
            P("req", "fsdp", None),
            P("req", "fsdp", None, None),
            P(),
            P("fsdp", "req"),
            P("fsdp", "req"),
            P("fsdp", "req"),
            P(),
            P(),
            P("fsdp", None, None),
            P("fsdp", None, None),
            P("req"),
            P("req"),
            P("req", "fsdp"),
            P("req", None),
            P(),
        ),
        out_specs=(P("req", "fsdp", None), P("req", "fsdp", None, None)),
        check_vma=False,
    )
```

profile of v0, /device:TPU:0, one launch (start us, length us, event | category | flops | bytes accessed | tf_op | source)
XLA Modules:
  0.0 200.5 jit_solution(7296874157899483863)
XLA Ops:
  7.3 0.7 all-gather.7.cloned.1.call-update
  8.0 18.0 %all_gather.37 = bf16[512,512]{0,1:T(8,128)(2,1)} all-gather(bf16[512,64]{0,1:T(8,128)(2,1)} %param.20), channel_id=1, replica_groups=mesh['fsdp'=4,'req'=8] {'req'}, dimensions={1}, use_global_device_ids=true | all-gather | bytes 589824 | tf_op jit(solution)/shard_map/all_gather | solution.py:88
  26.1 17.6 %all_gather.30 = bf16[512,512]{0,1:T(8,128)(2,1)} all-gather(bf16[512,64]{0,1:T(8,128)(2,1)} %param.19), channel_id=1, replica_groups=mesh['fsdp'=4,'req'=8] {'req'}, dimensions={1}, use_global_device_ids=true | all-gather | bytes 589824 | tf_op jit(solution)/shard_map/all_gather | solution.py:87
  43.8 0.5 all-gather.9.cloned.1.call-update
  44.3 0.2 select_reduce_fusion
  44.5 0.6 dynamic_slice.3
  49.0 10.7 %all_gather.36 = bf16[8,16,1024]{2,1,0:T(8,128)(2,1)} all-gather(bf16[2,16,1024]{2,1,0:T(8,128)(2,1)S(1)} %copy-done.7), channel_id=1, replica_groups=mesh['fsdp'=4,'req'=8] {'fsdp'}, dimensions={0}, use_global_device_ids=true | all-gather | bytes 327680 | tf_op jit(solution)/shard_map/all_gather | solution.py:109
  59.7 0.4 fusion
  60.1 15.3 %all_gather.35 = bf16[8,16,2048]{2,1,0:T(8,128)(2,1)} all-gather(bf16[2,16,2048]{2,1,0:T(8,128)(2,1)S(1)} %copy-done.6), channel_id=1, replica_groups=mesh['fsdp'=4,'req'=8] {'fsdp'}, dimensions={0}, use_global_device_ids=true | all-gather | bytes 655360 | tf_op jit(solution)/shard_map/all_gather | solution.py:108
  75.8 0.6 multiply_cosine_fusion
  76.5 0.4 fusion.2
  76.9 2.0 %all-gather.11.cloned.1.call-done = bf16[2048,512]{0,1:T(8,128)(2,1)} async-done(((bf16[512,512]{0,1:T(8,128)(2,1)}), bf16[2048,512]{0,1:T(8,128)(2,1)}) %all-gather.11.cloned.1.call-update) | async-done | bytes 2097168 | tf_op jit(solution)/shard_map/all_gather | solution.py:93
  78.9 2.5 %convolution_convert_fusion = bf16[320,512]{1,0:T(8,128)(2,1)S(1)} fusion(bf16[320,2048]{1,0:T(8,128)(2,1)S(1)} %fusion.2, bf16[2048,512]{0,1:T(8,128)(2,1)} %all-gather.11.cloned.1.call-done), kind=kOutput, calls=%fused_computation.37 | convolution fusion | flops 671252480 | bytes 3735552 | tf_op jit(solution)/shard_map/dot_general | solution.py:97
  81.4 0.9 copy.124
  82.2 33.7 %all-gather.5.cloned.1.call-done = bf16[2048,512]{0,1:T(8,128)(2,1)} async-done(((bf16[512,512]{0,1:T(8,128)(2,1)}), bf16[2048,512]{0,1:T(8,128)(2,1)}) %all-gather.5.cloned.1.call-update) | async-done | bytes 2097168 | tf_op jit(solution)/shard_map/all_gather | solution.py:92
  115.9 2.5 %fusion.64 = f32[320,512]{1,0:T(8,128)S(1)} fusion(bf16[320,2048]{1,0:T(8,128)(2,1)S(1)} %fusion.2, bf16[2048,512]{0,1:T(8,128)(2,1)} %all-gather.5.cloned.1.call-done), kind=kOutput, calls=%fused_computation.109 | convolution fusion | flops 671088640 | bytes 4063232 | tf_op jit(solution)/shard_map/dot_general | solution.py:97
  118.4 0.2 reshape.286
  118.6 0.4 multiply_reduce_fusion.1
  119.2 0.2 fusion.31
  119.4 0.3 subtract_convert_fusion.1
  119.8 10.2 %all_gather.32 = bf16[256,512]{1,0:T(8,128)(2,1)S(1)} all-gather(bf16[64,512]{1,0:T(8,128)(2,1)S(1)} %copy_bitcast_fusion), channel_id=1, replica_groups=mesh['fsdp'=4,'req'=8] {'fsdp'}, dimensions={0}, use_global_device_ids=true | all-gather | bytes 327680 | tf_op jit(solution)/shard_map/all_gather | solution.py:144
  130.1 0.9 copy.97
  130.9 10.5 %all_gather.39 = bf16[256,512]{1,0:T(8,128)(2,1)S(1)} all-gather(bf16[64,512]{1,0:T(8,128)(2,1)S(1)} %slice-done), channel_id=1, replica_groups=mesh['fsdp'=4,'req'=8] {'fsdp'}, dimensions={0}, use_global_device_ids=true | all-gather | bytes 327680 | tf_op jit(solution)/shard_map/all_gather | solution.py:145
  141.5 0.8 reshape.290
  142.2 30.4 %all-gather.9.cloned.1.call-done = bf16[2048,1024]{1,0:T(8,128)(2,1)} async-done(((bf16[512,1024]{1,0:T(8,128)(2,1)}), bf16[2048,1024]{1,0:T(8,128)(2,1)}) %all-gather.9.cloned.1.call-update) | async-done | bytes 4194320 | tf_op jit(solution)/shard_map/all_gather | solution.py:91
  172.6 4.8 %fusion.65 = f32[320,1024]{1,0:T(8,128)} fusion(bf16[320,2048]{1,0:T(8,128)(2,1)S(1)} %fusion.2, bf16[2048,1024]{1,0:T(8,128)(2,1)} %all-gather.9.cloned.1.call-done), kind=kOutput, calls=%fused_computation.110 | convolution fusion | flops 1342177280 | bytes 6815744 | tf_op jit(solution)/shard_map/dot_general | solution.py:97
  177.4 1.7 slice.99
  179.1 2.2 %convolution_add_fusion = f32[256,1024]{1,0:T(8,128)S(1)} fusion(bf16[320,2048]{1,0:T(8,128)(2,1)S(1)} %fusion.2, f32[320,1024]{1,0:T(8,128)} %fusion.65, bf16[8,16,2048]{2,1,0:T(8,128)(2,1)} %all_gather.35, s32[]{:T(128)} %bitcast.10, pred[]{:T(512)} %bitcast.9, bf16[8,16,1024]{2,1,0:T(8,128)(2,1)} %all_gather.36), kind=kOutput, calls=%fused_computation.25 | convolution fusion | flops 25481216 | bytes 3246080 | tf_op jit(solution)/shard_map/wge,wet->wgt/dot_general | solution.py:118
  181.3 1.1 maximum_bitcast_fusion
  182.4 0.3 copy.128
  182.7 0.4 multiply_reduce_fusion
  183.2 0.2 copy.99
  183.4 0.4 multiply_multiply_fusion
  183.8 0.6 subtract_convert_fusion
  184.5 0.3 pad_maximum_fusion.1
  185.0 0.5 copy-done.3
  185.4 1.0 fusion.3
  186.4 1.1 fusion.9
  187.6 0.6 fusion.6
  188.3 0.5 fusion.11
  188.8 0.9 fusion.15
  189.8 1.0 fusion.21
  190.7 0.3 copy.109
  191.1 0.2 copy.123
  191.4 0.5 fusion.14
  191.9 0.2 slice_bitcast_fusion
  192.1 0.8 copy.111
  192.9 1.0 copy.112
  (62 shorter events, 1.5 us)
Async XLA Ops:
  7.2 37.1 %copy-start.11 = (s32[8]{0:T(128)S(1)}, s32[8]{0:T(128)}, u32[]{:S(2)}) copy-start(s32[8]{0:T(128)} %param.29) | copy-start | bytes 100
  7.2 37.1 %copy-start.12 = (s32[1,4]{1,0:T(1,128)S(1)}, s32[1,4]{1,0:T(1,128)}, u32[]{:S(2)}) copy-start(s32[1,4]{1,0:T(1,128)} %param.28) | copy-start | bytes 52
  7.2 41.8 %copy-start.7 = (bf16[2,16,1024]{2,1,0:T(8,128)(2,1)S(1)}, bf16[2,16,1024]{2,1,0:T(8,128)(2,1)}, u32[]{:S(2)}) copy-start(bf16[2,16,1024]{2,1,0:T(8,128)(2,1)} %param.24) | copy-start | bytes 196612
  7.2 52.5 %copy-start = (bf16[1,1,256,2048]{3,2,1,0:T(8,128)(2,1)S(1)}, bf16[1,1,256,2048]{3,2,1,0:T(8,128)(2,1)}, u32[]{:S(2)}) copy-start(bf16[1,1,256,2048]{3,2,1,0:T(8,128)(2,1)} %param.16) | copy-start | bytes 3145732
  7.2 52.5 %copy-start.1 = (bf16[1,64,2048]{2,1,0:T(8,128)(2,1)S(1)}, bf16[1,64,2048]{2,1,0:T(8,128)(2,1)}, u32[]{:S(2)}) copy-start(bf16[1,64,2048]{2,1,0:T(8,128)(2,1)} %param.15) | copy-start | bytes 786436
  7.2 36.6 %all-gather.7.cloned.1.call-start = ((), (), s32[]{:S(2)}) async-start(), calls=%async_computation.1 | async-start | bytes 1179648 | tf_op jit(solution)/shard_map/all_gather | solution.py:86
  7.9 70.9 %all-gather.11.cloned.1.call-start = ((), (), s32[]{:S(2)}) async-start(), calls=%async_computation.3 | async-start | bytes 2621440 | tf_op jit(solution)/shard_map/all_gather | solution.py:93
  26.0 34.1 %copy-start.6 = (bf16[2,16,2048]{2,1,0:T(8,128)(2,1)S(1)}, bf16[2,16,2048]{2,1,0:T(8,128)(2,1)}, u32[]{:S(2)}) copy-start(bf16[2,16,2048]{2,1,0:T(8,128)(2,1)} %param.23) | copy-start | bytes 393220
  26.0 89.9 %all-gather.5.cloned.1.call-start = ((), (), s32[]{:S(2)}) async-start(), calls=%async_computation | async-start | bytes 2621440 | tf_op jit(solution)/shard_map/all_gather | solution.py:92
  43.7 32.8 %copy-start.8 = (f32[2048]{0:T(1024)S(1)}, f32[2048]{0:T(1024)}, u32[]{:S(2)}) copy-start(f32[2048]{0:T(1024)} %param.17) | copy-start | bytes 24580
  43.7 128.9 %all-gather.9.cloned.1.call-start = ((), (), s32[]{:S(2)}) async-start(), calls=%async_computation.2 | async-start | bytes 5242880 | tf_op jit(solution)/shard_map/all_gather | solution.py:91
  81.4 0.9 copy-start.4
  118.4 0.8 copy-start.9
  119.4 11.5 %slice-start = ((bf16[320,512]{1,0:T(8,128)(2,1)}), bf16[64,512]{1,0:T(8,128)(2,1)S(1)}, s32[]{:S(2)}) async-start(bf16[320,512]{1,0:T(8,128)(2,1)} %copy-done.4), calls=%async_computation.4 | async-start | bytes 131072 | tf_op jit(solution)/shard_map/slice | solution.py:143
  182.4 1.0 copy-start.10
  184.5 1.0 copy-start.3
  187.6 1.2 copy-start.5
  188.8 1.0 copy-start.2
Sparse Core Ops, SparseCore 0:
  9.6 29.3 all-gather.6
  40.9 37.9 all-gather.10
  80.7 35.1 all-gather.4
  117.6 54.9 all-gather.8
where the time goes:
time: 201 us; the launch traced here: 200 us
  blocking collectives  82.4 us (41%)
  waiting for transfers between devices  67.3 us (33%)
  between operations  18.2 us (9%)
  matrix products  15.3 us (8%)
  local copies, waits for them, and re-layouts  8.99 us (4%)
  other arithmetic  8.1 us (4%)
    all_gather x1, waiting for transfers between devices, shards(): lax.all_gather(full_k, 'fsdp', axis=0, tiled=True)  33.7 us
    all_gather x1, waiting for transfers between devices, shards(): lax.all_gather(full_q, 'fsdp', axis=0, tiled=True)  30.4 us
    all_gather x1, blocking collectives, shards(): lax.all_gather(w_value, 'req', axis=1, tiled=True)  18 us
    all_gather x1, blocking collectives, shards(): lax.all_gather(w_key, 'req', axis=1, tiled=True)  17.6 us
    all_gather x1, blocking collectives, shards(): lax.all_gather(adapter_down, 'fsdp', axis=0, tiled=True)  15.3 us
    all_gather x1, blocking collectives, shards(): lax.all_gather(adapter_up, 'fsdp', axis=0, tiled=True)  10.7 us
    all_gather x1, blocking collectives, shards(): piece_values = lax.all_gather(prompt_v_flat, 'fsdp', axis=0, tiled=True)  10.5 us
    all_gather x1, blocking collectives, shards(): piece_keys = lax.all_gather(prompt_k_flat, 'fsdp', axis=0, tiled=True)  10.2 us
  transfers between devices with their start and end apart: 4, of which 3 were waited for; matrix products, arithmetic and copies ran while one was open for 6% of the time, Pallas kernels for 0%

commit v1 on v0

--- a/solution.py
+++ b/solution.py
@@ -1,6 +1,10 @@
+import functools
+
 import jax
 import jax.numpy as jnp
 from jax import lax
+from jax.experimental import pallas as pl
+from jax.experimental.pallas import tpu as pltpu
 from jax.sharding import PartitionSpec as P
 
 epsilon = 1e-06
@@ -48,7 +52,7 @@
     return (newest, denominator, summed_output)
 
 
-def shards(
+def shards_general(
     x_prompt,
     x_suffix,
     norm_gain,
@@ -200,6 +204,442 @@
     return (result[:pr_rows][None], result[pr_rows:].reshape(1, mem_dev, suf_rows, q_cols))
 
 
+axes = ("fsdp", "req")
+any_space = pl.BlockSpec(memory_space=pl.ANY)
+in_vmem = pl.BlockSpec(memory_space=pltpu.VMEM)
+in_smem = pl.BlockSpec(memory_space=pltpu.SMEM)
+nt_dims = (((1,), (1,)), ((), ()))
+
+
+def device_number(x, y, z, core):
+    return (y * 2 + x) * 8 + z * 2 + core
+
+
+def pairs(target):
+    return [
+        (device_number(x, y, z, core), device_number(*target(x, y, z, core)))
+        for y in range(2)
+        for x in range(2)
+        for z in range(4)
+        for core in range(2)
+    ]
+
+
+first_hop = pairs(lambda x, y, z, c: (1 - x, y, z, c) if c == 0 else (x, 1 - y, z, c))
+second_hop = pairs(lambda x, y, z, c: (x, 1 - y, z, c) if c == 0 else (1 - x, y, z, c))
+ring_hop = pairs(lambda x, y, z, c: (x, y, (z + 1) % 4, c))
+core_swap = pairs(lambda x, y, z, c: (x, y, z, 1 - c))
+x_swap = pairs(lambda x, y, z, c: (1 - x, y, z, c))
+y_swap = pairs(lambda x, y, z, c: (x, 1 - y, z, c))
+xy_swap = pairs(lambda x, y, z, c: (1 - x, 1 - y, z, c))
+
+
+def permute(value, hop):
+    return lax.ppermute(value, axes, hop)
+
+
+def place():
+    fsdp_rank = lax.axis_index("fsdp")
+    req_rank = lax.axis_index("req")
+    return fsdp_rank, lax.rem(fsdp_rank, 2), fsdp_rank // 2, req_rank // 2, lax.rem(req_rank, 2)
+
+
+def slice_owner(kind, parity):
+    rank, x, y, _, _ = place()
+    if kind == 0:
+        return rank
+    x_side = rank + 1 - 2 * x
+    y_side = rank + 2 - 4 * y
+    if kind == 1:
+        return (1 - parity) * x_side + parity * y_side
+    if kind == 2:
+        return (1 - parity) * y_side + parity * x_side
+    return 3 - rank
+
+
+def pack_kernel(key_ref, value_ref, query_ref, down_ref, up_ref, own_ref, kv_ref, q_ref):
+    core = lax.rem(lax.axis_index("req"), 2)
+    half = key_ref.shape[0]
+    depth = key_ref.shape[1]
+    rank = down_ref.shape[1]
+    own_ref[0:half, :] = key_ref[...]
+    own_ref[half : 2 * half, :] = value_ref[...]
+    kv_ref[0:half, :] = key_ref[...]
+    kv_ref[half : 2 * half, :] = value_ref[...]
+    turned = query_ref[...].T
+    own_ref[2 * half : 4 * half, :] = turned
+    q_ref[...] = turned
+    row = 4 * half
+    for source in (down_ref, up_ref):
+        for part in range(source.shape[2] // depth):
+            own_ref[row : row + rank, :] = source[core, :, part * depth : (part + 1) * depth]
+            row += rank
+
+
+def copy_blocks(sources, parts, sems, target):
+    copies = []
+    _, _, _, z, core = place()
+    for step, (group, row, rows) in enumerate(parts):
+        home = lax.rem(z + 4 - step, 4)
+        started = []
+        for side in range(2):
+            parity = core if side == 0 else 1 - core
+            for kind in range(4):
+                copy = pltpu.make_async_copy(
+                    sources[group][side][kind].at[pl.ds(row, rows), :],
+                    target(home, parity, slice_owner(kind, parity)),
+                    sems.at[step, side * 4 + kind],
+                )
+                copy.start()
+                started.append(copy)
+        copies.append((home, started))
+    return copies
+
+
+def project_kv(*refs, rank_size):
+    (x_ref, cos_ref, sin_ref, gain_ref, slot_ref), refs = refs[:5], refs[5:]
+    own = (refs[0:4], refs[4:8])
+    far = (refs[8:12], refs[12:16])
+    shared_ref, key_ref, value_ref, low_ref, up_ref, weights, store, sems, store_sems = refs[16:]
+    depth = own[0][0].shape[1]
+    rows = 128
+    pr_rows = shared_ref.shape[0]
+    kv_cols = key_ref.shape[1]
+    parts = [(0, 0, rows)] + [(1, rows * s, rows) for s in range(3)]
+
+    def target(home, parity, owner):
+        return weights.at[
+            home,
+            pl.ds(pl.multiple_of(parity * rows, rows), rows),
+            pl.ds(pl.multiple_of(owner * depth, depth), depth),
+        ]
+
+    copies = copy_blocks((own, far), parts, sems, target)
+    _, _, _, _, core = place()
+    store_copies = []
+    for side in range(2):
+        parity = core if side == 0 else 1 - core
+        for kind in range(4):
+            copy = pltpu.make_async_copy(
+                own[side][kind].at[pl.ds(2 * rows, store.shape[1]), :],
+                store.at[slice_owner(kind, parity) * 2 + parity],
+                store_sems.at[side * 4 + kind],
+            )
+            copy.start()
+            store_copies.append(copy)
+    cosine = cos_ref[...]
+    sine = sin_ref[...]
+    low_gain = gain_ref[:, 0:64]
+    high_gain = gain_ref[:, 64:128]
+    for home, started in copies:
+        for copy in started:
+            copy.wait()
+        both = lax.dot_general(
+            x_ref[...], weights[home], nt_dims, preferred_element_type=jnp.float32
+        )
+        low, high = both[:, 0:64], both[:, 128:192]
+        square = jnp.sum(low * low, axis=-1, keepdims=True) + jnp.sum(
+            high * high, axis=-1, keepdims=True
+        )
+        scale = lax.rsqrt(square * (1.0 / 128.0) + epsilon)
+        low = low * scale * low_gain
+        high = high * scale * high_gain
+        keys = jnp.concatenate(
+            [low * cosine - high * sine, high * cosine + low * sine], axis=-1
+        ).astype(jnp.bfloat16)
+        values = jnp.concatenate([both[:, 64:128], both[:, 192:256]], axis=-1).astype(jnp.bfloat16)
+        at_head = pl.ds(pl.multiple_of(home * 128, 128), 128)
+        shared_ref[:, at_head] = keys[:pr_rows]
+        shared_ref[:, pl.ds(pl.multiple_of(home * 128 + kv_cols, 128), 128)] = values[:pr_rows]
+        key_ref[:, at_head] = keys[pr_rows:]
+        value_ref[:, at_head] = values[pr_rows:]
+    for copy in store_copies:
+        copy.wait()
+    slot = slot_ref[0]
+    total = jnp.zeros((x_ref.shape[0] - pr_rows, rank_size), jnp.float32)
+    for part in range(x_ref.shape[1] // depth):
+        total += lax.dot_general(
+            x_ref[pr_rows:, part * depth : (part + 1) * depth],
+            store[slot, part * rank_size : (part + 1) * rank_size, :],
+            nt_dims,
+            preferred_element_type=jnp.float32,
+        )
+    low_ref[...] = total.astype(jnp.bfloat16)
+    row = (x_ref.shape[1] // depth) * rank_size
+    for part in range(up_ref.shape[1] // depth):
+        up_ref[:, part * depth : (part + 1) * depth] = store[slot, row : row + rank_size, :]
+        row += rank_size
+
+
+def attend_kernel(*refs):
+    (x_ref, cos_ref, sin_ref, gain_ref, info_ref, low_ref, up_ref, key_ref, value_ref), refs = (
+        refs[:9],
+        refs[9:],
+    )
+    own = (refs[0:4], refs[4:8])
+    far = (refs[8:12], refs[12:16])
+    shared_parts = refs[16:20]
+    prompt_out, suffix_out, weights, shared, sems, shared_sems = refs[20:]
+    depth = own[0][0].shape[1]
+    rows = 128
+    pr_rows = prompt_out.shape[0]
+    suf_rows = suffix_out.shape[0]
+    row_count = pr_rows + suf_rows
+    kv_cols = key_ref.shape[1]
+    fsdp_rank, x, y, _, _ = place()
+    parts = [(0, rows, rows)] + [(1, rows * s, rows) for s in range(3)]
+
+    def target(home, parity, owner):
+        return weights.at[
+            home,
+            pl.ds(pl.multiple_of(parity * rows, rows), rows),
+            pl.ds(pl.multiple_of(owner * depth, depth), depth),
+        ]
+
+    copies = copy_blocks((own, far), parts, sems, target)
+    owners = (fsdp_rank, fsdp_rank + 1 - 2 * x, fsdp_rank + 2 - 4 * y, 3 - fsdp_rank)
+    shared_copies = []
+    for index, owner in enumerate(owners):
+        copy = pltpu.make_async_copy(
+            shared_parts[index],
+            shared.at[pl.ds(pl.multiple_of(owner * pr_rows, pr_rows), pr_rows), :],
+            shared_sems.at[index],
+        )
+        copy.start()
+        shared_copies.append(copy)
+    for copy in shared_copies:
+        copy.wait()
+    prompt_total = info_ref[0]
+    member_ok = info_ref[1]
+    suffix_total = info_ref[2]
+    prompt_keys = shared.shape[0]
+    row = lax.broadcasted_iota(jnp.int32, (row_count, prompt_keys), 0)
+    column = lax.broadcasted_iota(jnp.int32, (row_count, prompt_keys), 1)
+    limit = jnp.where(row < pr_rows, fsdp_rank * pr_rows + row, jnp.int32(2**30))
+    see_prompt = (column < prompt_total) & (column <= limit)
+    see_own = lax.broadcasted_iota(jnp.int32, (suf_rows, suf_rows), 1) <= (
+        lax.broadcasted_iota(jnp.int32, (suf_rows, suf_rows), 0)
+    )
+    row = lax.broadcasted_iota(jnp.int32, (row_count, 1), 0)
+    prompt_ok = (row < pr_rows) & (fsdp_rank * pr_rows + row < prompt_total)
+    suffix_ok = (row >= pr_rows) & (row - pr_rows < suffix_total) & (member_ok > 0)
+    row_ok = prompt_ok | suffix_ok
+    score_scale = 128 ** (-0.5)
+    for home, started in copies:
+        for copy in started:
+            copy.wait()
+        both = lax.dot_general(
+            x_ref[...], weights[home], nt_dims, preferred_element_type=jnp.float32
+        )
+        at_pair = pl.ds(pl.multiple_of(home * 256, 256), 256)
+        delta = jnp.dot(low_ref[...], up_ref[:, at_pair], preferred_element_type=jnp.float32)
+        both = jnp.concatenate([both[:pr_rows], both[pr_rows:] + delta], axis=0)
+        at_head = pl.ds(pl.multiple_of(home * 128, 128), 128)
+        p_keys = shared[:, at_head]
+        p_values = shared[:, pl.ds(pl.multiple_of(home * 128 + kv_cols, 128), 128)]
+        s_keys = key_ref[:, at_head]
+        s_values = value_ref[:, at_head]
+        for head in range(2):
+            query = both[:, head * 128 : head * 128 + 128]
+            scale = lax.rsqrt(jnp.mean(query * query, axis=-1, keepdims=True) + epsilon)
+            query = query * scale * gain_ref[...]
+            query = query * cos_ref[...] + pltpu.roll(query, 64, 1) * sin_ref[...]
+            query = query.astype(jnp.bfloat16)
+            p_scores = lax.dot_general(
+                query, p_keys, nt_dims, preferred_element_type=jnp.float32
+            )
+            p_scores = jnp.where(see_prompt, p_scores * score_scale, masked_low)
+            s_scores = lax.dot_general(
+                query[pr_rows:], s_keys, nt_dims, preferred_element_type=jnp.float32
+            )
+            s_scores = jnp.where(see_own, s_scores * score_scale, masked_low)
+            p_top = jnp.max(p_scores, axis=-1, keepdims=True)
+            s_top = jnp.max(s_scores, axis=-1, keepdims=True)
+            s_top = jnp.maximum(p_top[pr_rows:], s_top)
+            top = jnp.concatenate([p_top[:pr_rows], s_top], axis=0)
+            p_weights = jnp.exp(p_scores - top)
+            s_weights = jnp.exp(s_scores - s_top)
+            p_total = jnp.sum(p_weights, axis=-1, keepdims=True)
+            s_total = jnp.sum(s_weights, axis=-1, keepdims=True)
+            p_sum = jnp.dot(
+                p_weights.astype(jnp.bfloat16), p_values, preferred_element_type=jnp.float32
+            )
+            s_sum = jnp.dot(
+                s_weights.astype(jnp.bfloat16), s_values, preferred_element_type=jnp.float32
+            )
+            p_result = jnp.where(row_ok[:pr_rows], p_sum[:pr_rows] / p_total[:pr_rows], 0.0)
+            s_result = (p_sum[pr_rows:] + s_sum) / (p_total[pr_rows:] + s_total)
+            s_result = jnp.where(row_ok[pr_rows:], s_result, 0.0)
+            at_query = pl.ds(pl.multiple_of(home * 256 + head * 128, 128), 128)
+            prompt_out[:, at_query] = p_result.astype(jnp.bfloat16)
+            suffix_out[:, at_query] = s_result.astype(jnp.bfloat16)
+
+
+def spread(block):
+    side = permute(block, first_hop)
+    other = permute(block, second_hop)
+    corner = permute(side, second_hop)
+    mine = (block, side, other, corner)
+    return mine + tuple(permute(part, core_swap) for part in mine)
+
+
+def rope_tables(positions, half_dim):
+    frequency = rope_base ** (-jnp.arange(half_dim).astype(jnp.float32) / half_dim)
+    angles = positions.astype(jnp.float32)[:, None] * frequency[None, :]
+    return jnp.cos(angles), jnp.sin(angles)
+
+
+def shards_torus(
+    x_prompt,
+    x_suffix,
+    norm_gain,
+    w_query,
+    w_key,
+    w_value,
+    query_gain,
+    key_gain,
+    adapter_down,
+    adapter_up,
+    prompt_len,
+    member_count,
+    suffix_len,
+    adapter_id,
+    holder_slot,
+):
+    bf16 = jnp.bfloat16
+    fsdp_rank = lax.axis_index("fsdp")
+    pr_rows, model_width = x_prompt.shape[1:]
+    suf_rows = x_suffix.shape[2]
+    row_count = pr_rows + suf_rows
+    depth = w_query.shape[0]
+    rank_size = adapter_down.shape[1]
+    q_cols = adapter_up.shape[2]
+    kv_cols = w_key.shape[1] * 8
+    store_rows = (model_width + q_cols) // depth * rank_size
+
+    own, kv_near, q_near = pl.pallas_call(
+        pack_kernel,
+        out_shape=(
+            jax.ShapeDtypeStruct((256 + store_rows, depth), bf16),
+            jax.ShapeDtypeStruct((128, depth), bf16),
+            jax.ShapeDtypeStruct((128, depth), bf16),
+        ),
+        name="pack",
+    )(w_key.T, w_value.T, w_query, adapter_down, adapter_up)
+
+    def ring(block):
+        steps = []
+        for _ in range(3):
+            block = permute(block, ring_hop)
+            steps.append(block)
+        return jnp.concatenate(steps, axis=0)
+
+    own_blocks = spread(own)
+    kv_blocks = spread(ring(kv_near))
+    q_blocks = spread(ring(q_near))
+
+    tokens = jnp.concatenate([x_prompt[0], x_suffix[0, 0]], axis=0)
+    normed = norm_rows(tokens.astype(jnp.float32), norm_gain).astype(bf16)
+    prompt_pos = fsdp_rank * pr_rows + jnp.arange(pr_rows)
+    suffix_pos = prompt_len[0] + jnp.arange(suf_rows)
+    cosine, sine = rope_tables(jnp.concatenate([prompt_pos, suffix_pos]), 64)
+    lookup = jnp.where(
+        adapter_id[0][:, None] == jnp.arange(holder_slot.shape[0])[None, :], holder_slot[None, :], 0
+    )
+    storage = jnp.sum(lookup, axis=1)
+    mine = lax.dynamic_slice_in_dim(storage, fsdp_rank, 1)
+    info = jnp.stack(
+        [
+            prompt_len[0],
+            (fsdp_rank < member_count[0]).astype(jnp.int32),
+            suffix_len[0, 0],
+        ]
+    )
+
+    shared, s_keys, s_values, low, up = pl.pallas_call(
+        functools.partial(project_kv, rank_size=rank_size),
+        out_shape=(
+            jax.ShapeDtypeStruct((pr_rows, 2 * kv_cols), bf16),
+            jax.ShapeDtypeStruct((suf_rows, kv_cols), bf16),
+            jax.ShapeDtypeStruct((suf_rows, kv_cols), bf16),
+            jax.ShapeDtypeStruct((suf_rows, rank_size), bf16),
+            jax.ShapeDtypeStruct((rank_size, q_cols), bf16),
+        ),
+        in_specs=[in_vmem] * 4 + [in_smem] + [any_space] * 16,
+        scratch_shapes=[
+            pltpu.VMEM((4, 256, model_width), bf16),
+            pltpu.VMEM((8, store_rows, depth), bf16),
+            pltpu.SemaphoreType.DMA((4, 8)),
+            pltpu.SemaphoreType.DMA((8,)),
+        ],
+        compiler_params=pltpu.CompilerParams(vmem_limit_bytes=32 << 20),
+        cost_estimate=pl.CostEstimate(
+            flops=2 * row_count * model_width * 2 * kv_cols,
+            bytes_accessed=8 << 20,
+            transcendentals=0,
+        ),
+        name="project_kv",
+    )(normed, cosine, sine, key_gain[None, :], mine, *own_blocks, *kv_blocks)
+
+    shared_blocks = (
+        shared,
+        permute(shared, x_swap),
+        permute(shared, y_swap),
+        permute(shared, xy_swap),
+    )
+    cos_pair = jnp.concatenate([cosine, cosine], axis=1)
+    sin_pair = jnp.concatenate([-sine, sine], axis=1)
+    prompt_res, suffix_res = pl.pallas_call(
+        attend_kernel,
+        out_shape=(
+            jax.ShapeDtypeStruct((pr_rows, q_cols), bf16),
+            jax.ShapeDtypeStruct((suf_rows, q_cols), bf16),
+        ),
+        in_specs=[in_vmem] * 4 + [in_smem] + [in_vmem] * 4 + [any_space] * 20,
+        scratch_shapes=[
+            pltpu.VMEM((4, 256, model_width), bf16),
+            pltpu.VMEM((4 * pr_rows, 2 * kv_cols), bf16),
+            pltpu.SemaphoreType.DMA((4, 8)),
+            pltpu.SemaphoreType.DMA((4,)),
+        ],
+        compiler_params=pltpu.CompilerParams(vmem_limit_bytes=40 << 20),
+        cost_estimate=pl.CostEstimate(
+            flops=2 * row_count * model_width * q_cols,
+            bytes_accessed=8 << 20,
+            transcendentals=0,
+        ),
+        name="attend",
+    )(
+        normed,
+        cos_pair,
+        sin_pair,
+        query_gain[None, :],
+        info,
+        low,
+        up,
+        s_keys,
+        s_values,
+        *own_blocks,
+        *q_blocks,
+        *shared_blocks,
+    )
+    return prompt_res[None], suffix_res[None, None]
+
+
+def shards(*operands):
+    x_suffix, w_query, w_key, query_gain = operands[1], operands[3], operands[4], operands[6]
+    head_dim = query_gain.shape[0]
+    fits = (
+        (lax.axis_size("fsdp"), lax.axis_size("req")) == (4, 8)
+        and head_dim == 128
+        and w_query.shape[1] == head_dim
+        and 2 * w_key.shape[1] == head_dim
+        and x_suffix.shape[1] == 1
+        and operands[8].shape[0] == 2
+    )
+    return shards_torus(*operands) if fits else shards_general(*operands)
+
+
 def solution(mesh):
     return jax.shard_map(
         shards,

time: 201 us -> 96.6 us (0.48)
  blocking collectives: 82.4 us -> 0 us
  waiting for transfers between devices: 67.3 us -> 31.6 us
  starting transfers between devices: 0.16 us -> 22.4 us
  Pallas kernels: 0 us -> 22.1 us
  matrix products: 15.3 us -> 0 us
  between operations: 18.2 us -> 2.94 us
  local copies, waits for them, and re-layouts: 8.99 us -> 13.2 us
  other arithmetic: 8.1 us -> 3.92 us
    all_gather x6 -> x0, blocking collectives: 82.4 us -> none  [the longest x1 18 us: shards(): lax.all_gather(w_value, 'req', axis=1, tiled=True)]
    all_gather x4 -> x0, waiting for transfers between devices: 66.1 us -> none  [the longest x1 33.7 us: shards(): lax.all_gather(full_k, 'fsdp', axis=0, tiled=True)]
    ppermute x0 -> x30, waiting for transfers between devices: none -> 31.6 us  [permute(): return lax.ppermute(value, axes, hop)]
    ppermute x0 -> x30, starting transfers between devices: none -> 22.4 us  [permute(): return lax.ppermute(value, axes, hop)]
    pallas_call x0 -> x3, Pallas kernels: none -> 22.1 us  [the longest x1 12.6 us: shards_torus(): pl.pallas_call(attend_kernel, out_shape=(jax.ShapeDtypeStruct((pr_rows, q...]
    dot_general x8 -> x0, matrix products: 15.3 us -> none  [the longest x3 9.71 us: shards(): jnp.dot(normed, weight_piece, preferred_element_type=jnp.float32)]
    unnamed x29 -> x48, local copies, waits for them, and re-layouts: 2.63 us -> 11.4 us
  transfers between devices with their start and end apart: 4 -> 30, of which waited for: 3 -> 11; matrix products, arithmetic and copies ran while one was open for 6% -> 9% of each run, Pallas kernels for 0% -> 8%
where the time goes in v1:
time: 96.6 us; the launch traced here: 96.2 us
  waiting for transfers between devices  31.6 us (33%)
  starting transfers between devices  22.4 us (23%)
  Pallas kernels  22.1 us (23%)
  local copies, waits for them, and re-layouts  13.2 us (14%)
  other arithmetic  3.92 us (4%)
  between operations  2.94 us (3%)
    ppermute x30, waiting for transfers between devices, permute(): return lax.ppermute(value, axes, hop)  31.6 us
    ppermute x30, starting transfers between devices, permute(): return lax.ppermute(value, axes, hop)  22.4 us
    pallas_call x1, Pallas kernels, shards_torus(): pl.pallas_call(attend_kernel, out_shape=(jax.ShapeDtypeStruct((pr_rows, q...  12.6 us
    unnamed x48, local copies, waits for them, and re-layouts  11.4 us
    pallas_call x1, Pallas kernels, shards_torus(): pl.pallas_call(functools.partial(project_kv, rank_size=rank_size), out_sh...  7.58 us
  transfers between devices with their start and end apart: 30, of which 11 were waited for; matrix products, arithmetic and copies ran while one was open for 9% of the time, Pallas kernels for 8%

profile of v1, /device:TPU:0, one launch (start us, length us, event | category | flops | bytes accessed | tf_op | source)
XLA Modules:
  0.0 96.2 jit_solution(17530281545522706211)
XLA Ops:
  0.6 1.9 %pack.1 = (bf16[352,512]{1,0:T(8,128)(2,1)}, bf16[128,512]{1,0:T(8,128)(2,1)}, bf16[128,512]{1,0:T(8,128)(2,1)}) custom-call(bf16[64,512]{1,0:T(8,128)(2,1)} %bitcast.22, bf16[64,512]{1,0:T(8,128)(2,1)} %bitcast.23, bf16[512,128]{1,0:T(8,128)(2,1)} %query_ref.1, bf16[2,16,2048]{2,1,0:T(8,128)(2,1)} %down_ref.1, bf16[2,16,1024]{2,1,0:T(8,128)(2,1)} %up_ref.1), custom_call_target="tpu_custom_call" | custom-call | tf_op jit(solution)/shard_map/pack/pallas_call | solution.py:520
  2.5 3.0 %collective-permute-start.7 = (bf16[128,512]{1,0:T(8,128)(2,1)}, bf16[128,512]{1,0:T(8,128)(2,1)S(1)}, u32[]{:S(2)}, u32[]{:S(2)}) collective-permute-start(bf16[128,512]{1,0:T(8,128)(2,1)} %get-tuple-element.13), channel_id=1, source_target_pairs={{0,2},{1,3},{2,4},{3,5},{4,6},{5,7},{6,0},{7,1},{8,10},{9,11},{10,... | collective-permute-start | bytes 393224 | tf_op jit(solution)/shard_map/ppermute | solution.py:238
  5.6 1.6 %collective-permute-start.17 = (bf16[128,512]{1,0:T(8,128)(2,1)}, bf16[128,512]{1,0:T(8,128)(2,1)S(1)}, u32[]{:S(2)}, u32[]{:S(2)}) collective-permute-start(bf16[128,512]{1,0:T(8,128)(2,1)} %get-tuple-element.18), channel_id=1, source_target_pairs={{0,2},{1,3},{2,4},{3,5},{4,6},{5,7},{6,0},{7,1},{8,10},{9,11},{10,... | collective-permute-start | bytes 393224 | tf_op jit(solution)/shard_map/ppermute | solution.py:238
  7.1 5.0 %collective-permute-done.7 = bf16[128,512]{1,0:T(8,128)(2,1)S(1)} collective-permute-done((bf16[128,512]{1,0:T(8,128)(2,1)}, bf16[128,512]{1,0:T(8,128)(2,1)S(1)}, u32[]{:S(2)}, u32[]{:S(2)}) %collective-permute-start.7) | collective-permute-done | bytes 131104 | tf_op jit(solution)/shard_map/ppermute | solution.py:238
  12.2 1.7 %collective-permute-start = (bf16[352,512]{1,0:T(8,128)(2,1)}, bf16[352,512]{1,0:T(8,128)(2,1)S(1)}, u32[]{:S(2)}, u32[]{:S(2)}) collective-permute-start(bf16[352,512]{1,0:T(8,128)(2,1)} %get-tuple-element.12.refs_5_.refs_9_), channel_id=1, source_target_pairs={{0,8},{1,17},{2,10},{3,19},{4,12},{5,21},{6,14},{7,23},{8,0},{9,25... | collective-permute-start | bytes 1081352 | tf_op jit(solution)/shard_map/ppermute | solution.py:238
  13.9 1.5 %collective-permute-start.1 = (bf16[352,512]{1,0:T(8,128)(2,1)}, bf16[352,512]{1,0:T(8,128)(2,1)S(1)}, u32[]{:S(2)}, u32[]{:S(2)}) collective-permute-start(bf16[352,512]{1,0:T(8,128)(2,1)} %get-tuple-element.12.refs_5_.refs_9_), channel_id=1, source_target_pairs={{0,16},{1,9},{2,18},{3,11},{4,20},{5,13},{6,22},{7,15},{8,24},{9,1... | collective-permute-start | bytes 1081352 | tf_op jit(solution)/shard_map/ppermute | solution.py:238
  15.4 1.4 %collective-permute-start.18 = (bf16[128,512]{1,0:T(8,128)(2,1)S(1)}, bf16[128,512]{1,0:T(8,128)(2,1)S(1)}, u32[]{:S(2)}, u32[]{:S(2)}) collective-permute-start(bf16[128,512]{1,0:T(8,128)(2,1)S(1)} %collective-permute-done.17), channel_id=1, source_target_pairs={{0,2},{1,3},{2,4},{3,5},{4,6},{5,7},{6,0},{7,1},{8,10},{9,11},{10,... | collective-permute-start | bytes 393224 | tf_op jit(solution)/shard_map/ppermute | solution.py:238
  16.8 1.7 %fusion = f32[320]{0:T(512)S(1)} fusion(bf16[256,2048]{1,0:T(8,128)(2,1)} %bitcast.18, bf16[64,2048]{1,0:T(8,128)(2,1)} %bitcast.20), kind=kLoop, calls=%fused_computation.2 | loop fusion | flops 3931840 | bytes 1312000 | tf_op jit(solution)/shard_map/reduce_sum | solution.py:18
  18.9 1.2 %collective-permute-start.9 = (bf16[128,512]{1,0:T(8,128)(2,1)S(1)}, bf16[128,512]{1,0:T(8,128)(2,1)S(1)}, u32[]{:S(2)}, u32[]{:S(2)}) collective-permute-start(bf16[128,512]{1,0:T(8,128)(2,1)S(1)} %collective-permute-done.8), channel_id=1, source_target_pairs={{0,2},{1,3},{2,4},{3,5},{4,6},{5,7},{6,0},{7,1},{8,10},{9,11},{10,... | collective-permute-start | bytes 393224 | tf_op jit(solution)/shard_map/ppermute | solution.py:238
  20.1 0.7 constant_dynamic-update-slice_fusion.2
  20.8 2.8 %collective-permute-done.18 = bf16[128,512]{1,0:T(8,128)(2,1)S(1)} collective-permute-done((bf16[128,512]{1,0:T(8,128)(2,1)S(1)}, bf16[128,512]{1,0:T(8,128)(2,1)S(1)}, u32[]{:S(2)}, u32[]{:S(2)}) %collective-permute-start.18) | collective-permute-done | bytes 131104 | tf_op jit(solution)/shard_map/ppermute | solution.py:238
  23.6 0.7 constant_dynamic-update-slice_fusion.1
  24.2 0.5 collective-permute-start.2
  24.7 1.4 %collective-permute-done.9 = bf16[128,512]{1,0:T(8,128)(2,1)S(1)} collective-permute-done((bf16[128,512]{1,0:T(8,128)(2,1)S(1)}, bf16[128,512]{1,0:T(8,128)(2,1)S(1)}, u32[]{:S(2)}, u32[]{:S(2)}) %collective-permute-start.9) | collective-permute-done | bytes 131104 | tf_op jit(solution)/shard_map/ppermute | solution.py:238
  26.2 0.7 constant_dynamic-update-slice_fusion.refs_13_
  26.9 3.7 %collective-permute-done.19 = bf16[128,512]{1,0:T(8,128)(2,1)S(1)} collective-permute-done((bf16[128,512]{1,0:T(8,128)(2,1)S(1)}, bf16[128,512]{1,0:T(8,128)(2,1)S(1)}, u32[]{:S(2)}, u32[]{:S(2)}) %collective-permute-start.19) | collective-permute-done | bytes 131104 | tf_op jit(solution)/shard_map/ppermute | solution.py:238
  30.5 0.5 collective-permute-start.10
  31.0 0.7 constant_dynamic-update-slice_fusion.5
  31.7 0.7 constant_dynamic-update-slice_fusion.4
  32.4 0.7 constant_dynamic-update-slice_fusion.3.refs_17_
  33.0 1.6 %collective-permute-start.11 = (bf16[384,512]{1,0:T(8,128)(2,1)}, bf16[384,512]{1,0:T(8,128)(2,1)}, u32[]{:S(2)}, u32[]{:S(2)}) collective-permute-start(bf16[384,512]{1,0:T(8,128)(2,1)} %constant_dynamic-update-slice_fusion.refs_13_), channel_id=1, source_target_pairs={{0,16},{1,9},{2,18},{3,11},{4,20},{5,13},{6,22},{7,15},{8,24},{9,1... | collective-permute-start | bytes 1179656 | tf_op jit(solution)/shard_map/ppermute | solution.py:238
  34.6 0.7 copy-done.1
  35.9 0.7 copy-done.4
  36.6 1.5 %collective-permute-start.21 = (bf16[384,512]{1,0:T(8,128)(2,1)}, bf16[384,512]{1,0:T(8,128)(2,1)}, u32[]{:S(2)}, u32[]{:S(2)}) collective-permute-start(bf16[384,512]{1,0:T(8,128)(2,1)} %constant_dynamic-update-slice_fusion.3.refs_17_), channel_id=1, source_target_pairs={{0,16},{1,9},{2,18},{3,11},{4,20},{5,13},{6,22},{7,15},{8,24},{9,1... | collective-permute-start | bytes 1179656 | tf_op jit(solution)/shard_map/ppermute | solution.py:238
  38.1 4.1 %collective-permute-done.10.refs_14_ = bf16[384,512]{1,0:T(8,128)(2,1)} collective-permute-done((bf16[384,512]{1,0:T(8,128)(2,1)}, bf16[384,512]{1,0:T(8,128)(2,1)}, u32[]{:S(2)}, u32[]{:S(2)}) %collective-permute-start.10) | collective-permute-done | bytes 393248 | tf_op jit(solution)/shard_map/ppermute | solution.py:238
  42.6 1.0 %collective-permute-done.11.refs_15_ = bf16[384,512]{1,0:T(8,128)(2,1)} collective-permute-done((bf16[384,512]{1,0:T(8,128)(2,1)}, bf16[384,512]{1,0:T(8,128)(2,1)}, u32[]{:S(2)}, u32[]{:S(2)}) %collective-permute-start.11) | collective-permute-done | bytes 393248 | tf_op jit(solution)/shard_map/ppermute | solution.py:238
  43.7 0.5 collective-permute-start.14
  44.8 5.8 %collective-permute-done.20.refs_18_ = bf16[384,512]{1,0:T(8,128)(2,1)} collective-permute-done((bf16[384,512]{1,0:T(8,128)(2,1)}, bf16[384,512]{1,0:T(8,128)(2,1)}, u32[]{:S(2)}, u32[]{:S(2)}) %collective-permute-start.20) | collective-permute-done | bytes 393248 | tf_op jit(solution)/shard_map/ppermute | solution.py:238
  51.2 2.6 %collective-permute-done.12.refs_16_ = bf16[384,512]{1,0:T(8,128)(2,1)} collective-permute-done((bf16[384,512]{1,0:T(8,128)(2,1)}, bf16[384,512]{1,0:T(8,128)(2,1)}, u32[]{:S(2)}, u32[]{:S(2)}) %collective-permute-start.12) | collective-permute-done | bytes 393248 | tf_op jit(solution)/shard_map/ppermute | solution.py:238
  53.8 1.7 %collective-permute-start.16 = (bf16[384,512]{1,0:T(8,128)(2,1)}, bf16[384,512]{1,0:T(8,128)(2,1)}, u32[]{:S(2)}, u32[]{:S(2)}) collective-permute-start(bf16[384,512]{1,0:T(8,128)(2,1)} %collective-permute-done.12.refs_16_), channel_id=1, source_target_pairs={{0,1},{1,0},{2,3},{3,2},{4,5},{5,4},{6,7},{7,6},{8,9},{9,8},{10,11... | collective-permute-start | bytes 1179656 | tf_op jit(solution)/shard_map/ppermute | solution.py:238
  55.6 0.7 copy-done.7
  56.3 0.8 copy-done.10
  57.6 1.3 %fusion.3 = (f32[320,64]{1,0:T(8,128)}, f32[320,64]{1,0:T(8,128)S(1)}, f32[320,64]{1,0:T(8,128)S(1)}) fusion(f32[64]{0:T(128)S(1)} %multiply_power_fusion, f32[320]{0:T(512)S(1)} %add_convert_fusion), kind=kLoop, calls=%fused_computation.10 | loop fusion | flops 40960 | bytes 247296 | tf_op jit(solution)/shard_map/neg | solution.py:591
  58.9 0.7 copy-done.12
  59.7 0.5 collective-permute-start.26
  61.7 0.6 dynamic_slice.3.refs_4_
  62.3 1.0 %copy-done.2 = bf16[352,512]{1,0:T(8,128)(2,1)S(1)} copy-done((bf16[352,512]{1,0:T(8,128)(2,1)S(1)}, bf16[352,512]{1,0:T(8,128)(2,1)}, u32[]{:S(2)}) %copy-start.2) | copy-done | bytes 360472
  63.2 1.0 %copy-done.5 = bf16[352,512]{1,0:T(8,128)(2,1)S(1)} copy-done((bf16[352,512]{1,0:T(8,128)(2,1)S(1)}, bf16[352,512]{1,0:T(8,128)(2,1)}, u32[]{:S(2)}) %copy-start.5) | copy-done | bytes 360472
  64.2 1.0 %copy-done.8 = bf16[352,512]{1,0:T(8,128)(2,1)S(1)} copy-done((bf16[352,512]{1,0:T(8,128)(2,1)S(1)}, bf16[352,512]{1,0:T(8,128)(2,1)}, u32[]{:S(2)}) %copy-start.8) | copy-done | bytes 360472
  65.2 1.0 %copy-done.11 = bf16[384,512]{1,0:T(8,128)(2,1)S(1)} copy-done((bf16[384,512]{1,0:T(8,128)(2,1)S(1)}, bf16[384,512]{1,0:T(8,128)(2,1)}, u32[]{:S(2)}) %copy-start.11) | copy-done | bytes 393240
  66.2 1.0 %copy-done.13 = bf16[384,512]{1,0:T(8,128)(2,1)S(1)} copy-done((bf16[384,512]{1,0:T(8,128)(2,1)S(1)}, bf16[384,512]{1,0:T(8,128)(2,1)}, u32[]{:S(2)}) %copy-start.13) | copy-done | bytes 393240
  67.2 7.6 %project_kv.1 = (bf16[64,1024]{1,0:T(8,128)(2,1)S(1)}, bf16[256,512]{1,0:T(8,128)(2,1)S(1)}, bf16[256,512]{1,0:T(8,128)(2,1)S(1)}, bf16[256,16]{1,0:T(8,128)(2,1)S(1)}, bf16[16,1024]{1,0:T(8,128)(2,1)S(1)}) custom-call(bf16[320,2048]{1,0:T(8,128)(2,1)S(1)} %fusion.2.refs_0_, f32[320,64]{1,0:T(8,128)S(1)} %get-tuple-element.24.refs_1_, ...), custom_call_target="tpu_custom_call" | custom-call | flops 1342177280 | bytes 8388608 | tf_op jit(solution)/shard_map/project_kv/pallas_call | solution.py:559
  74.8 0.6 collective-permute-start.27
  75.4 1.5 %collective-permute-start.28 = (bf16[64,1024]{1,0:T(8,128)(2,1)S(1)}, bf16[64,1024]{1,0:T(8,128)(2,1)S(1)}, u32[]{:S(2)}, u32[]{:S(2)}) collective-permute-start(bf16[64,1024]{1,0:T(8,128)(2,1)S(1)} %get-tuple-element.19.refs_25_), channel_id=1, source_target_pairs={{0,16},{1,17},{2,18},{3,19},{4,20},{5,21},{6,22},{7,23},{8,24},{9,... | collective-permute-start | bytes 393224 | tf_op jit(solution)/shard_map/ppermute | solution.py:238
  76.9 1.4 %collective-permute-start.29 = (bf16[64,1024]{1,0:T(8,128)(2,1)S(1)}, bf16[64,1024]{1,0:T(8,128)(2,1)S(1)}, u32[]{:S(2)}, u32[]{:S(2)}) collective-permute-start(bf16[64,1024]{1,0:T(8,128)(2,1)S(1)} %get-tuple-element.19.refs_25_), channel_id=1, source_target_pairs={{0,24},{1,25},{2,26},{3,27},{4,28},{5,29},{6,30},{7,31},{8,16},{9,... | collective-permute-start | bytes 393224 | tf_op jit(solution)/shard_map/ppermute | solution.py:238
  78.6 2.6 %collective-permute-done.27.refs_26_ = bf16[64,1024]{1,0:T(8,128)(2,1)S(1)} collective-permute-done((bf16[64,1024]{1,0:T(8,128)(2,1)S(1)}, bf16[64,1024]{1,0:T(8,128)(2,1)S(1)}, u32[]{:S(2)}, u32[]{:S(2)}) %collective-permute-start.27) | collective-permute-done | bytes 131104 | tf_op jit(solution)/shard_map/ppermute | solution.py:238
  81.2 2.1 %collective-permute-done.28.refs_27_ = bf16[64,1024]{1,0:T(8,128)(2,1)S(1)} collective-permute-done((bf16[64,1024]{1,0:T(8,128)(2,1)S(1)}, bf16[64,1024]{1,0:T(8,128)(2,1)S(1)}, u32[]{:S(2)}, u32[]{:S(2)}) %collective-permute-start.28) | collective-permute-done | bytes 131104 | tf_op jit(solution)/shard_map/ppermute | solution.py:238
  83.4 12.6 %attend.1 = (bf16[64,1024]{1,0:T(8,128)(2,1)}, bf16[256,1024]{1,0:T(8,128)(2,1)}) custom-call(bf16[320,2048]{1,0:T(8,128)(2,1)S(1)} %fusion.2.refs_0_, f32[320,128]{1,0:T(8,128)S(1)} %get-tuple-element.25.refs_1_, f32[320,128]{1,0:T(8,128)S(1)} %get-tuple-element.26.refs_2_, f32[1,128]{1,0:T(1,128)S(1)} %bitcast.17, s32[3]{0:T(128)S(1)} %pad_add_fusion.refs_4_, ...), custom_call_target="tpu_custom_call" | custom-call | flops 1342177280 | bytes 8388608 | tf_op jit(solution)/shard_map/attend/pallas_call | solution.py:592
  (77 shorter events, 2.9 us)
Async XLA Ops:
  2.5 9.6 %collective-permute-start.7 = (bf16[128,512]{1,0:T(8,128)(2,1)}, bf16[128,512]{1,0:T(8,128)(2,1)S(1)}, u32[]{:S(2)}, u32[]{:S(2)}) collective-permute-start(bf16[128,512]{1,0:T(8,128)(2,1)} %get-tuple-element.13), channel_id=1, source_target_pairs={{0,2},{1,3},{2,4},{3,5},{4,6},{5,7},{6,0},{7,1},{8,10},{9,11},{10,... | collective-permute-start | bytes 393224 | tf_op jit(solution)/shard_map/ppermute | solution.py:238
  5.6 9.8 %collective-permute-start.17 = (bf16[128,512]{1,0:T(8,128)(2,1)}, bf16[128,512]{1,0:T(8,128)(2,1)S(1)}, u32[]{:S(2)}, u32[]{:S(2)}) collective-permute-start(bf16[128,512]{1,0:T(8,128)(2,1)} %get-tuple-element.18), channel_id=1, source_target_pairs={{0,2},{1,3},{2,4},{3,5},{4,6},{5,7},{6,0},{7,1},{8,10},{9,11},{10,... | collective-permute-start | bytes 393224 | tf_op jit(solution)/shard_map/ppermute | solution.py:238
  12.1 6.8 %collective-permute-start.8 = (bf16[128,512]{1,0:T(8,128)(2,1)S(1)}, bf16[128,512]{1,0:T(8,128)(2,1)S(1)}, u32[]{:S(2)}, u32[]{:S(2)}) collective-permute-start(bf16[128,512]{1,0:T(8,128)(2,1)S(1)} %collective-permute-done.7), channel_id=1, source_target_pairs={{0,2},{1,3},{2,4},{3,5},{4,6},{5,7},{6,0},{7,1},{8,10},{9,11},{10,... | collective-permute-start | bytes 393224 | tf_op jit(solution)/shard_map/ppermute | solution.py:238
  12.2 12.1 %collective-permute-start = (bf16[352,512]{1,0:T(8,128)(2,1)}, bf16[352,512]{1,0:T(8,128)(2,1)S(1)}, u32[]{:S(2)}, u32[]{:S(2)}) collective-permute-start(bf16[352,512]{1,0:T(8,128)(2,1)} %get-tuple-element.12.refs_5_.refs_9_), channel_id=1, source_target_pairs={{0,8},{1,17},{2,10},{3,19},{4,12},{5,21},{6,14},{7,23},{8,0},{9,25... | collective-permute-start | bytes 1081352 | tf_op jit(solution)/shard_map/ppermute | solution.py:238
  13.9 10.9 %collective-permute-start.1 = (bf16[352,512]{1,0:T(8,128)(2,1)}, bf16[352,512]{1,0:T(8,128)(2,1)S(1)}, u32[]{:S(2)}, u32[]{:S(2)}) collective-permute-start(bf16[352,512]{1,0:T(8,128)(2,1)} %get-tuple-element.12.refs_5_.refs_9_), channel_id=1, source_target_pairs={{0,16},{1,9},{2,18},{3,11},{4,20},{5,13},{6,22},{7,15},{8,24},{9,1... | collective-permute-start | bytes 1081352 | tf_op jit(solution)/shard_map/ppermute | solution.py:238
  15.4 17.7 %collective-permute-start.3 = (bf16[352,512]{1,0:T(8,128)(2,1)}, bf16[352,512]{1,0:T(8,128)(2,1)S(1)}, u32[]{:S(2)}, u32[]{:S(2)}) collective-permute-start(bf16[352,512]{1,0:T(8,128)(2,1)} %get-tuple-element.12.refs_5_.refs_9_), channel_id=1, source_target_pairs={{0,1},{1,0},{2,3},{3,2},{4,5},{5,4},{6,7},{7,6},{8,9},{9,8},{10,11... | collective-permute-start | bytes 1081352 | tf_op jit(solution)/shard_map/ppermute | solution.py:238
  15.4 8.2 %collective-permute-start.18 = (bf16[128,512]{1,0:T(8,128)(2,1)S(1)}, bf16[128,512]{1,0:T(8,128)(2,1)S(1)}, u32[]{:S(2)}, u32[]{:S(2)}) collective-permute-start(bf16[128,512]{1,0:T(8,128)(2,1)S(1)} %collective-permute-done.17), channel_id=1, source_target_pairs={{0,2},{1,3},{2,4},{3,5},{4,6},{5,7},{6,0},{7,1},{8,10},{9,11},{10,... | collective-permute-start | bytes 393224 | tf_op jit(solution)/shard_map/ppermute | solution.py:238
  16.7 25.5 %copy-start.16 = (bf16[1,1,256,2048]{3,2,1,0:T(8,128)(2,1)S(1)}, bf16[1,1,256,2048]{3,2,1,0:T(8,128)(2,1)}, u32[]{:S(2)}) copy-start(bf16[1,1,256,2048]{3,2,1,0:T(8,128)(2,1)} %param.16) | copy-start | bytes 3145732
  16.8 25.5 %copy-start.17 = (bf16[1,64,2048]{2,1,0:T(8,128)(2,1)S(1)}, bf16[1,64,2048]{2,1,0:T(8,128)(2,1)}, u32[]{:S(2)}) copy-start(bf16[1,64,2048]{2,1,0:T(8,128)(2,1)} %param.15) | copy-start | bytes 786436
  16.8 25.5 %copy-start.19 = (f32[2048]{0:T(1024)S(1)}, f32[2048]{0:T(1024)}, u32[]{:S(2)}) copy-start(f32[2048]{0:T(1024)} %param.17) | copy-start | bytes 24580
  18.9 7.3 %collective-permute-start.9 = (bf16[128,512]{1,0:T(8,128)(2,1)S(1)}, bf16[128,512]{1,0:T(8,128)(2,1)S(1)}, u32[]{:S(2)}, u32[]{:S(2)}) collective-permute-start(bf16[128,512]{1,0:T(8,128)(2,1)S(1)} %collective-permute-done.8), channel_id=1, source_target_pairs={{0,2},{1,3},{2,4},{3,5},{4,6},{5,7},{6,0},{7,1},{8,10},{9,11},{10,... | collective-permute-start | bytes 393224 | tf_op jit(solution)/shard_map/ppermute | solution.py:238
  23.6 6.9 %collective-permute-start.19 = (bf16[128,512]{1,0:T(8,128)(2,1)S(1)}, bf16[128,512]{1,0:T(8,128)(2,1)S(1)}, u32[]{:S(2)}, u32[]{:S(2)}) collective-permute-start(bf16[128,512]{1,0:T(8,128)(2,1)S(1)} %collective-permute-done.18), channel_id=1, source_target_pairs={{0,2},{1,3},{2,4},{3,5},{4,6},{5,7},{6,0},{7,1},{8,10},{9,11},{10,... | collective-permute-start | bytes 393224 | tf_op jit(solution)/shard_map/ppermute | solution.py:238
  24.2 10.4 %collective-permute-start.2 = (bf16[352,512]{1,0:T(8,128)(2,1)S(1)}, bf16[352,512]{1,0:T(8,128)(2,1)S(1)}, u32[]{:S(2)}, u32[]{:S(2)}) collective-permute-start(bf16[352,512]{1,0:T(8,128)(2,1)S(1)} %collective-permute-done.refs_6_.refs_10_), channel_id=1, source_target_pairs={{0,16},{1,9},{2,18},{3,11},{4,20},{5,13},{6,22},{7,15},{8,24},{9,1... | collective-permute-start | bytes 1081352 | tf_op jit(solution)/shard_map/ppermute | solution.py:238
  24.7 9.9 %collective-permute-start.4 = (bf16[352,512]{1,0:T(8,128)(2,1)S(1)}, bf16[352,512]{1,0:T(8,128)(2,1)S(1)}, u32[]{:S(2)}, u32[]{:S(2)}) collective-permute-start(bf16[352,512]{1,0:T(8,128)(2,1)S(1)} %collective-permute-done.refs_6_.refs_10_), channel_id=1, source_target_pairs={{0,1},{1,0},{2,3},{3,2},{4,5},{5,4},{6,7},{7,6},{8,9},{9,8},{10,11... | collective-permute-start | bytes 1081352 | tf_op jit(solution)/shard_map/ppermute | solution.py:238
  26.2 9.7 %collective-permute-start.5 = (bf16[352,512]{1,0:T(8,128)(2,1)S(1)}, bf16[352,512]{1,0:T(8,128)(2,1)S(1)}, u32[]{:S(2)}, u32[]{:S(2)}) collective-permute-start(bf16[352,512]{1,0:T(8,128)(2,1)S(1)} %collective-permute-done.1.refs_7_.refs_11_), channel_id=1, source_target_pairs={{0,1},{1,0},{2,3},{3,2},{4,5},{5,4},{6,7},{7,6},{8,9},{9,8},{10,11... | collective-permute-start | bytes 1081352 | tf_op jit(solution)/shard_map/ppermute | solution.py:238
  30.5 11.7 %collective-permute-start.10 = (bf16[384,512]{1,0:T(8,128)(2,1)}, bf16[384,512]{1,0:T(8,128)(2,1)}, u32[]{:S(2)}, u32[]{:S(2)}) collective-permute-start(bf16[384,512]{1,0:T(8,128)(2,1)} %constant_dynamic-update-slice_fusion.refs_13_), channel_id=1, source_target_pairs={{0,8},{1,17},{2,10},{3,19},{4,12},{5,21},{6,14},{7,23},{8,0},{9,25... | collective-permute-start | bytes 1179656 | tf_op jit(solution)/shard_map/ppermute | solution.py:238
  33.0 27.2 %copy-start.20 = (s32[8]{0:T(128)S(1)}, s32[8]{0:T(128)}, u32[]{:S(2)}) copy-start(s32[8]{0:T(128)} %param.29) | copy-start | bytes 100
  33.0 27.2 %copy-start.21 = (s32[1,4]{1,0:T(1,128)S(1)}, s32[1,4]{1,0:T(1,128)}, u32[]{:S(2)}) copy-start(s32[1,4]{1,0:T(1,128)} %param.28) | copy-start | bytes 52
  33.0 29.2 %copy-start = (bf16[352,512]{1,0:T(8,128)(2,1)S(1)}, bf16[352,512]{1,0:T(8,128)(2,1)}, u32[]{:S(2)}) copy-start(bf16[352,512]{1,0:T(8,128)(2,1)} %get-tuple-element.12.refs_5_.refs_9_) | copy-start | bytes 1081348
  33.0 29.2 %copy-start.14 = (f32[128]{0:T(128)S(1)}, f32[128]{0:T(128)}, u32[]{:S(2)}) copy-start(f32[128]{0:T(128)} %param.22) | copy-start | bytes 1540
  33.0 10.6 %collective-permute-start.11 = (bf16[384,512]{1,0:T(8,128)(2,1)}, bf16[384,512]{1,0:T(8,128)(2,1)}, u32[]{:S(2)}, u32[]{:S(2)}) collective-permute-start(bf16[384,512]{1,0:T(8,128)(2,1)} %constant_dynamic-update-slice_fusion.refs_13_), channel_id=1, source_target_pairs={{0,16},{1,9},{2,18},{3,11},{4,20},{5,13},{6,22},{7,15},{8,24},{9,1... | collective-permute-start | bytes 1179656 | tf_op jit(solution)/shard_map/ppermute | solution.py:238
  34.6 9.0 %collective-permute-start.13 = (bf16[384,512]{1,0:T(8,128)(2,1)}, bf16[384,512]{1,0:T(8,128)(2,1)}, u32[]{:S(2)}, u32[]{:S(2)}) collective-permute-start(bf16[384,512]{1,0:T(8,128)(2,1)} %constant_dynamic-update-slice_fusion.refs_13_), channel_id=1, source_target_pairs={{0,1},{1,0},{2,3},{3,2},{4,5},{5,4},{6,7},{7,6},{8,9},{9,8},{10,11... | collective-permute-start | bytes 1179656 | tf_op jit(solution)/shard_map/ppermute | solution.py:238
  35.4 15.3 %collective-permute-start.20 = (bf16[384,512]{1,0:T(8,128)(2,1)}, bf16[384,512]{1,0:T(8,128)(2,1)}, u32[]{:S(2)}, u32[]{:S(2)}) collective-permute-start(bf16[384,512]{1,0:T(8,128)(2,1)} %constant_dynamic-update-slice_fusion.3.refs_17_), channel_id=1, source_target_pairs={{0,8},{1,17},{2,10},{3,19},{4,12},{5,21},{6,14},{7,23},{8,0},{9,25... | collective-permute-start | bytes 1179656 | tf_op jit(solution)/shard_map/ppermute | solution.py:238
  36.6 14.0 %collective-permute-start.21 = (bf16[384,512]{1,0:T(8,128)(2,1)}, bf16[384,512]{1,0:T(8,128)(2,1)}, u32[]{:S(2)}, u32[]{:S(2)}) collective-permute-start(bf16[384,512]{1,0:T(8,128)(2,1)} %constant_dynamic-update-slice_fusion.3.refs_17_), channel_id=1, source_target_pairs={{0,16},{1,9},{2,18},{3,11},{4,20},{5,13},{6,22},{7,15},{8,24},{9,1... | collective-permute-start | bytes 1179656 | tf_op jit(solution)/shard_map/ppermute | solution.py:238
  42.2 11.6 %collective-permute-start.12 = (bf16[384,512]{1,0:T(8,128)(2,1)}, bf16[384,512]{1,0:T(8,128)(2,1)}, u32[]{:S(2)}, u32[]{:S(2)}) collective-permute-start(bf16[384,512]{1,0:T(8,128)(2,1)} %collective-permute-done.10.refs_14_), channel_id=1, source_target_pairs={{0,16},{1,9},{2,18},{3,11},{4,20},{5,13},{6,22},{7,15},{8,24},{9,1... | collective-permute-start | bytes 1179656 | tf_op jit(solution)/shard_map/ppermute | solution.py:238
  43.7 11.9 %collective-permute-start.6 = (bf16[352,512]{1,0:T(8,128)(2,1)S(1)}, bf16[352,512]{1,0:T(8,128)(2,1)S(1)}, u32[]{:S(2)}, u32[]{:S(2)}) collective-permute-start(bf16[352,512]{1,0:T(8,128)(2,1)S(1)} %collective-permute-done.2.refs_8_.refs_12_), channel_id=1, source_target_pairs={{0,1},{1,0},{2,3},{3,2},{4,5},{5,4},{6,7},{7,6},{8,9},{9,8},{10,11... | collective-permute-start | bytes 1081352 | tf_op jit(solution)/shard_map/ppermute | solution.py:238
  43.7 12.7 %collective-permute-start.14 = (bf16[384,512]{1,0:T(8,128)(2,1)}, bf16[384,512]{1,0:T(8,128)(2,1)S(1)}, u32[]{:S(2)}, u32[]{:S(2)}) collective-permute-start(bf16[384,512]{1,0:T(8,128)(2,1)} %collective-permute-done.10.refs_14_), channel_id=1, source_target_pairs={{0,1},{1,0},{2,3},{3,2},{4,5},{5,4},{6,7},{7,6},{8,9},{9,8},{10,11... | collective-permute-start | bytes 1179656 | tf_op jit(solution)/shard_map/ppermute | solution.py:238
  50.7 8.3 %collective-permute-start.15 = (bf16[384,512]{1,0:T(8,128)(2,1)}, bf16[384,512]{1,0:T(8,128)(2,1)S(1)}, u32[]{:S(2)}, u32[]{:S(2)}) collective-permute-start(bf16[384,512]{1,0:T(8,128)(2,1)} %collective-permute-done.11.refs_15_), channel_id=1, source_target_pairs={{0,1},{1,0},{2,3},{3,2},{4,5},{5,4},{6,7},{7,6},{8,9},{9,8},{10,11... | collective-permute-start | bytes 1179656 | tf_op jit(solution)/shard_map/ppermute | solution.py:238
  50.7 9.0 %collective-permute-start.22 = (bf16[384,512]{1,0:T(8,128)(2,1)}, bf16[384,512]{1,0:T(8,128)(2,1)}, u32[]{:S(2)}, u32[]{:S(2)}) collective-permute-start(bf16[384,512]{1,0:T(8,128)(2,1)} %collective-permute-done.20.refs_18_), channel_id=1, source_target_pairs={{0,16},{1,9},{2,18},{3,11},{4,20},{5,13},{6,22},{7,15},{8,24},{9,1... | collective-permute-start | bytes 1179656 | tf_op jit(solution)/shard_map/ppermute | solution.py:238
  53.8 8.4 %collective-permute-start.16 = (bf16[384,512]{1,0:T(8,128)(2,1)}, bf16[384,512]{1,0:T(8,128)(2,1)}, u32[]{:S(2)}, u32[]{:S(2)}) collective-permute-start(bf16[384,512]{1,0:T(8,128)(2,1)} %collective-permute-done.12.refs_16_), channel_id=1, source_target_pairs={{0,1},{1,0},{2,3},{3,2},{4,5},{5,4},{6,7},{7,6},{8,9},{9,8},{10,11... | collective-permute-start | bytes 1179656 | tf_op jit(solution)/shard_map/ppermute | solution.py:238
  56.3 19.1 %collective-permute-start.23 = (bf16[384,512]{1,0:T(8,128)(2,1)}, bf16[384,512]{1,0:T(8,128)(2,1)}, u32[]{:S(2)}, u32[]{:S(2)}) collective-permute-start(bf16[384,512]{1,0:T(8,128)(2,1)} %constant_dynamic-update-slice_fusion.3.refs_17_), channel_id=1, source_target_pairs={{0,1},{1,0},{2,3},{3,2},{4,5},{5,4},{6,7},{7,6},{8,9},{9,8},{10,11... | collective-permute-start | bytes 1179656 | tf_op jit(solution)/shard_map/ppermute | solution.py:238
  56.3 0.8 copy-start.10
  57.1 19.8 %collective-permute-start.24 = (bf16[384,512]{1,0:T(8,128)(2,1)}, bf16[384,512]{1,0:T(8,128)(2,1)}, u32[]{:S(2)}, u32[]{:S(2)}) collective-permute-start(bf16[384,512]{1,0:T(8,128)(2,1)} %collective-permute-done.20.refs_18_), channel_id=1, source_target_pairs={{0,1},{1,0},{2,3},{3,2},{4,5},{5,4},{6,7},{7,6},{8,9},{9,8},{10,11... | collective-permute-start | bytes 1179656 | tf_op jit(solution)/shard_map/ppermute | solution.py:238
  59.7 18.9 %collective-permute-start.25 = (bf16[384,512]{1,0:T(8,128)(2,1)}, bf16[384,512]{1,0:T(8,128)(2,1)}, u32[]{:S(2)}, u32[]{:S(2)}) collective-permute-start(bf16[384,512]{1,0:T(8,128)(2,1)} %collective-permute-done.21.refs_19_), channel_id=1, source_target_pairs={{0,1},{1,0},{2,3},{3,2},{4,5},{5,4},{6,7},{7,6},{8,9},{9,8},{10,11... | collective-permute-start | bytes 1179656 | tf_op jit(solution)/shard_map/ppermute | solution.py:238
  59.7 18.9 %collective-permute-start.26 = (bf16[384,512]{1,0:T(8,128)(2,1)}, bf16[384,512]{1,0:T(8,128)(2,1)}, u32[]{:S(2)}, u32[]{:S(2)}) collective-permute-start(bf16[384,512]{1,0:T(8,128)(2,1)} %collective-permute-done.22.refs_20_), channel_id=1, source_target_pairs={{0,1},{1,0},{2,3},{3,2},{4,5},{5,4},{6,7},{7,6},{8,9},{9,8},{10,11... | collective-permute-start | bytes 1179656 | tf_op jit(solution)/shard_map/ppermute | solution.py:238
  62.3 1.0 %copy-start.2 = (bf16[352,512]{1,0:T(8,128)(2,1)S(1)}, bf16[352,512]{1,0:T(8,128)(2,1)}, u32[]{:S(2)}) copy-start(bf16[352,512]{1,0:T(8,128)(2,1)} %copy-done.1) | copy-start | bytes 1081348
  63.2 1.0 %copy-start.5 = (bf16[352,512]{1,0:T(8,128)(2,1)S(1)}, bf16[352,512]{1,0:T(8,128)(2,1)}, u32[]{:S(2)}) copy-start(bf16[352,512]{1,0:T(8,128)(2,1)} %copy-done.4) | copy-start | bytes 1081348
  64.2 1.0 %copy-start.8 = (bf16[352,512]{1,0:T(8,128)(2,1)S(1)}, bf16[352,512]{1,0:T(8,128)(2,1)}, u32[]{:S(2)}) copy-start(bf16[352,512]{1,0:T(8,128)(2,1)} %copy-done.7) | copy-start | bytes 1081348
  65.2 1.0 %copy-start.11 = (bf16[384,512]{1,0:T(8,128)(2,1)S(1)}, bf16[384,512]{1,0:T(8,128)(2,1)}, u32[]{:S(2)}) copy-start(bf16[384,512]{1,0:T(8,128)(2,1)} %copy-done.10) | copy-start | bytes 1179652
  66.2 1.0 %copy-start.13 = (bf16[384,512]{1,0:T(8,128)(2,1)S(1)}, bf16[384,512]{1,0:T(8,128)(2,1)}, u32[]{:S(2)}) copy-start(bf16[384,512]{1,0:T(8,128)(2,1)} %copy-done.12) | copy-start | bytes 1179652
  67.2 11.2 %copy-start.18 = (f32[320,64]{1,0:T(8,128)S(1)}, f32[320,64]{1,0:T(8,128)}, u32[]{:S(2)}) copy-start(f32[320,64]{1,0:T(8,128)} %get-tuple-element.22) | copy-start | bytes 245764
  67.2 16.2 %copy-start.3 = (bf16[352,512]{1,0:T(8,128)(2,1)S(1)}, bf16[352,512]{1,0:T(8,128)(2,1)}, u32[]{:S(2)}) copy-start(bf16[352,512]{1,0:T(8,128)(2,1)} %copy-done.1) | copy-start | bytes 1081348
  67.2 16.2 %copy-start.6 = (bf16[352,512]{1,0:T(8,128)(2,1)S(1)}, bf16[352,512]{1,0:T(8,128)(2,1)}, u32[]{:S(2)}) copy-start(bf16[352,512]{1,0:T(8,128)(2,1)} %copy-done.4) | copy-start | bytes 1081348
  67.2 16.2 %copy-start.9 = (bf16[352,512]{1,0:T(8,128)(2,1)S(1)}, bf16[352,512]{1,0:T(8,128)(2,1)}, u32[]{:S(2)}) copy-start(bf16[352,512]{1,0:T(8,128)(2,1)} %copy-done.7) | copy-start | bytes 1081348
  67.2 16.2 %copy-start.15 = (f32[128]{0:T(128)S(1)}, f32[128]{0:T(128)}, u32[]{:S(2)}) copy-start(f32[128]{0:T(128)} %param.21) | copy-start | bytes 1540
  74.8 6.4 %collective-permute-start.27 = (bf16[64,1024]{1,0:T(8,128)(2,1)S(1)}, bf16[64,1024]{1,0:T(8,128)(2,1)S(1)}, u32[]{:S(2)}, u32[]{:S(2)}) collective-permute-start(bf16[64,1024]{1,0:T(8,128)(2,1)S(1)} %get-tuple-element.19.refs_25_), channel_id=1, source_target_pairs={{0,8},{1,9},{2,10},{3,11},{4,12},{5,13},{6,14},{7,15},{8,0},{9,1},... | collective-permute-start | bytes 393224 | tf_op jit(solution)/shard_map/ppermute | solution.py:238
  75.4 7.9 %collective-permute-start.28 = (bf16[64,1024]{1,0:T(8,128)(2,1)S(1)}, bf16[64,1024]{1,0:T(8,128)(2,1)S(1)}, u32[]{:S(2)}, u32[]{:S(2)}) collective-permute-start(bf16[64,1024]{1,0:T(8,128)(2,1)S(1)} %get-tuple-element.19.refs_25_), channel_id=1, source_target_pairs={{0,16},{1,17},{2,18},{3,19},{4,20},{5,21},{6,22},{7,23},{8,24},{9,... | collective-permute-start | bytes 393224 | tf_op jit(solution)/shard_map/ppermute | solution.py:238
  76.9 6.4 %collective-permute-start.29 = (bf16[64,1024]{1,0:T(8,128)(2,1)S(1)}, bf16[64,1024]{1,0:T(8,128)(2,1)S(1)}, u32[]{:S(2)}, u32[]{:S(2)}) collective-permute-start(bf16[64,1024]{1,0:T(8,128)(2,1)S(1)} %get-tuple-element.19.refs_25_), channel_id=1, source_target_pairs={{0,24},{1,25},{2,26},{3,27},{4,28},{5,29},{6,30},{7,31},{8,16},{9,... | collective-permute-start | bytes 393224 | tf_op jit(solution)/shard_map/ppermute | solution.py:238
  (4 other events, 3.0 us)

commit v2 on v0

--- a/solution.py
+++ b/solution.py
@@ -1,6 +1,10 @@
+import functools
+
 import jax
 import jax.numpy as jnp
 from jax import lax
+from jax.experimental import pallas as pl
+from jax.experimental.pallas import tpu as pltpu
 from jax.sharding import PartitionSpec as P
 
 epsilon = 1e-06
@@ -48,7 +52,7 @@
     return (newest, denominator, summed_output)
 
 
-def shards(
+def shards_general(
     x_prompt,
     x_suffix,
     norm_gain,
@@ -200,6 +204,524 @@
     return (result[:pr_rows][None], result[pr_rows:].reshape(1, mem_dev, suf_rows, q_cols))
 
 
+axes = ("fsdp", "req")
+in_smem = pl.BlockSpec(memory_space=pltpu.SMEM)
+in_vmem = pl.BlockSpec(memory_space=pltpu.VMEM)
+in_hbm = pl.BlockSpec(memory_space=pltpu.HBM)
+in_any = pl.BlockSpec(memory_space=pl.ANY)
+nt_dims = (((1,), (1,)), ((), ()))
+log2_e = 1.4426950408889634
+head = 128
+
+
+def device_number(x, y, z, core):
+    return (y * 2 + x) * 8 + z * 2 + core
+
+
+def pairs(target):
+    return [
+        (device_number(x, y, z, core), device_number(*target(x, y, z, core)))
+        for y in range(2)
+        for x in range(2)
+        for z in range(4)
+        for core in range(2)
+    ]
+
+
+first_hop = pairs(lambda x, y, z, c: (1 - x, y, z, c) if c == 0 else (x, 1 - y, z, c))
+second_hop = pairs(lambda x, y, z, c: (x, 1 - y, z, c) if c == 0 else (1 - x, y, z, c))
+ring_hop = pairs(lambda x, y, z, c: (x, y, (z + 1) % 4, c))
+ring_back = pairs(lambda x, y, z, c: (x, y, (z + 3) % 4, c))
+core_swap = pairs(lambda x, y, z, c: (x, y, z, 1 - c))
+
+
+def permute(value, hop):
+    return lax.ppermute(value, axes, hop)
+
+
+def together(*values):
+    return lax.optimization_barrier(values)
+
+
+def slice_owners():
+    rank = lax.axis_index("fsdp")
+    core = lax.rem(lax.axis_index("req"), 2)
+    x_side = rank + 1 - 2 * lax.rem(rank, 2)
+    y_side = rank + 2 - 4 * (rank // 2)
+    return (
+        rank,
+        (1 - core) * x_side + core * y_side,
+        (1 - core) * y_side + core * x_side,
+        3 - rank,
+    )
+
+
+def block_refs(refs):
+    near, corner = refs[4:6]
+    rows = corner.shape[0]
+    theirs = tuple(near.at[part * rows : (part + 1) * rows, :] for part in range(3)) + (corner,)
+    return tuple(refs[0:4]), theirs
+
+
+def homes(steps):
+    z = lax.axis_index("req") // 2
+    return [lax.rem(z + 4 - step, 4) for step in steps]
+
+
+def pack_kernel(
+    key_ref, value_ref, query_ref, down_ref, up_ref, prompt_ref, own_ref, near_ref, buffers, sems
+):
+    core = lax.rem(lax.axis_index("req"), 2)
+    half, depth = key_ref.shape
+    rank = down_ref.shape[1]
+    pr_rows, width = prompt_ref.shape
+    query_buf, down_buf, up_buf = buffers
+    tail = own_ref.shape[0] - pr_rows * (width // depth)
+    copies = [
+        pltpu.make_async_copy(query_ref, query_buf, sems.at[0]),
+        pltpu.make_async_copy(down_ref, down_buf, sems.at[1]),
+        pltpu.make_async_copy(up_ref, up_buf, sems.at[2]),
+        pltpu.make_async_copy(key_ref, near_ref.at[pl.ds(0, half), :], sems.at[3]),
+        pltpu.make_async_copy(value_ref, near_ref.at[pl.ds(half, half), :], sems.at[4]),
+    ]
+    for part in range(width // depth):
+        copies.append(
+            pltpu.make_async_copy(
+                prompt_ref.at[:, pl.ds(part * depth, depth)],
+                own_ref.at[pl.ds(tail + part * pr_rows, pr_rows), :],
+                sems.at[5 + part],
+            )
+        )
+    for copy in copies:
+        copy.start()
+    for copy in copies:
+        copy.wait()
+    near_ref[2 * half : 4 * half, :] = query_buf[...].T
+    own_ref[0 : 4 * half, :] = near_ref[...]
+    row = 4 * half
+    for source in (down_buf, up_buf):
+        for part in range(source.shape[2] // depth):
+            own_ref[row : row + rank, :] = source[core, :, part * depth : (part + 1) * depth]
+            row += rank
+
+
+def norm_kernel(own_ref, side_ref, other_ref, corner_ref, suffix_ref, gain_ref, out_ref, *, tail):
+    slices, _, depth = out_ref.shape
+    width = slices * depth
+    pr_rows = (own_ref.shape[0] - tail) // slices
+    owners = slice_owners()
+    row = 0
+    for source in (side_ref, other_ref, corner_ref, own_ref):
+        square = None
+        for part in range(slices):
+            start = tail + part * pr_rows
+            values = source[start : start + pr_rows, :].astype(jnp.float32)
+            added = jnp.sum(values * values, axis=-1, keepdims=True)
+            square = added if square is None else square + added
+        scale = lax.rsqrt(square * (1.0 / width) + epsilon)
+        for index, owner in enumerate(owners):
+            start = pl.multiple_of(tail + owner * pr_rows, 16)
+            gain = gain_ref[:, pl.ds(pl.multiple_of(owner * depth, depth), depth)]
+            values = source[pl.ds(start, pr_rows), :].astype(jnp.float32)
+            out_ref[index, row : row + pr_rows, :] = (values * scale * gain).astype(jnp.bfloat16)
+        row += pr_rows
+    values = suffix_ref[...].astype(jnp.float32)
+    scale = lax.rsqrt(jnp.mean(values * values, axis=-1, keepdims=True) + epsilon)
+    for index, owner in enumerate(owners):
+        at_slice = pl.ds(pl.multiple_of(owner * depth, depth), depth)
+        part = suffix_ref[:, at_slice].astype(jnp.float32) * scale * gain_ref[:, at_slice]
+        out_ref[index, row:, :] = part.astype(jnp.bfloat16)
+
+
+def project(x_ref, rows, weight_blocks):
+    total = None
+    for index, block in enumerate(weight_blocks):
+        part = lax.dot_general(
+            x_ref[index, rows, :], block, nt_dims, preferred_element_type=jnp.float32
+        )
+        total = part if total is None else total + part
+    return total
+
+
+def adapter_kernel(x_ref, slot_ref, *refs, first_row):
+    mine, theirs = block_refs(refs[:6])
+    low_ref, up_ref = refs[6:]
+    slices, _, depth = x_ref.shape
+    rank_size = up_ref.shape[0] // 8
+    owners = slice_owners()
+    core = lax.rem(lax.axis_index("req"), 2)
+    low = None
+    for owner in range(slices):
+        index = jnp.where(
+            owner == owners[0],
+            0,
+            jnp.where(owner == owners[1], 1, jnp.where(owner == owners[2], 2, 3)),
+        )
+        row = 2 * head + owner * rank_size
+        down = jnp.concatenate(
+            [block[row : row + rank_size, :] for block in mine + theirs], axis=0
+        )
+        part = lax.dot_general(
+            x_ref[index, first_row:, :], down, nt_dims, preferred_element_type=jnp.float32
+        )
+        low = part if low is None else low + part
+    column = lax.broadcasted_iota(jnp.int32, low.shape, 1) // rank_size
+    keep = jnp.zeros(low.shape, jnp.bool_)
+    for side in range(2):
+        parity = core if side == 0 else 1 - core
+        for index, owner in enumerate(owners):
+            held = owner * 2 + parity
+            keep = keep | ((column == side * 4 + index) & (held == slot_ref[0]))
+    low_ref[...] = jnp.where(keep, low, 0.0).astype(jnp.bfloat16)
+    for part in range(up_ref.shape[1] // depth):
+        row = 2 * head + (slices + part) * rank_size
+        for index, block in enumerate(mine + theirs):
+            up_ref[index * rank_size : (index + 1) * rank_size, part * depth : (part + 1) * depth] = (
+                block[row : row + rank_size, :]
+            )
+
+
+def attend_kernel(*refs, steps, first):
+    (info_ref, x_ref, cos_ref, sin_ref, q_gain_ref, k_gain_ref, low_ref, up_ref), refs = (
+        refs[:8],
+        refs[8:],
+    )
+    mine, theirs = block_refs(refs[:6])
+    refs = refs[6:] if first else refs[8:]
+    prompt_out, suffix_out, prompt_buf, suffix_buf, sems = refs
+    pr_rows = prompt_buf.shape[0]
+    suf_rows = suffix_buf.shape[0]
+    prompt_keys = 4 * pr_rows
+    first_query = prompt_keys - pr_rows
+    count = len(steps)
+    core = lax.rem(lax.axis_index("req"), 2)
+    owners = slice_owners()
+    rank = owners[0]
+
+    def stacked(start):
+        return [
+            jnp.concatenate(
+                [
+                    block[step * 2 * head + start : step * 2 * head + start + head, :]
+                    for block in (m, t)
+                    for step in range(count)
+                ],
+                axis=0,
+            )
+            for m, t in zip(mine, theirs)
+        ]
+
+    kv_raw = project(x_ref, slice(None), stacked(0))
+    q_raw = project(x_ref, slice(first_query, None), stacked(head))
+    prompt_total = info_ref[0]
+    member_ok = info_ref[1]
+    suffix_total = info_ref[2]
+
+    def key_positions(rows):
+        column = lax.broadcasted_iota(jnp.int32, (rows, prompt_keys), 1)
+        part = column // pr_rows
+        owner = jnp.where(
+            part == 0,
+            owners[1],
+            jnp.where(part == 1, owners[2], jnp.where(part == 2, owners[3], rank)),
+        )
+        return owner * pr_rows + column - part * pr_rows
+
+    suffix_sees = jnp.where(key_positions(1) < prompt_total, 0.0, masked_low)
+    row = lax.broadcasted_iota(jnp.int32, (pr_rows, prompt_keys), 0) + rank * pr_rows
+    position = key_positions(pr_rows)
+    prompt_sees = jnp.where((position < prompt_total) & (position <= row), 0.0, masked_low)
+    prompt_sees = jnp.concatenate([prompt_sees, prompt_sees], axis=0)
+    own_sees = jnp.where(
+        lax.broadcasted_iota(jnp.int32, (suf_rows, suf_rows), 1)
+        <= lax.broadcasted_iota(jnp.int32, (suf_rows, suf_rows), 0),
+        0.0,
+        masked_low,
+    )
+    prompt_ok = (
+        lax.broadcasted_iota(jnp.int32, (pr_rows, 1), 0) + rank * pr_rows < prompt_total
+    )
+    suffix_ok = (lax.broadcasted_iota(jnp.int32, (suf_rows, 1), 0) < suffix_total) & (
+        member_ok > 0
+    )
+    factor = head ** (-0.5) * log2_e
+    half = head // 2
+    cosine, minus_sine = cos_ref[:, 0:half], sin_ref[:, 0:half]
+    q_cos, q_sin = cos_ref[first_query:, :], sin_ref[first_query:, :]
+    low_gain, high_gain = k_gain_ref[:, 0:half], k_gain_ref[:, half:head]
+    copies = []
+    for index, home in enumerate(homes(steps)):
+        own_part = kv_raw[:, index * head : (index + 1) * head]
+        other_part = kv_raw[:, (count + index) * head : (count + index + 1) * head]
+        lower = jnp.where(core == 0, own_part, other_part)
+        upper = jnp.where(core == 0, other_part, own_part)
+        low, high = lower[:, 0:half], upper[:, 0:half]
+        square = jnp.sum(low * low + high * high, axis=-1, keepdims=True)
+        scale = lax.rsqrt(square * (1.0 / head) + epsilon)
+        low = low * scale * low_gain
+        high = high * scale * high_gain
+        keys = jnp.concatenate(
+            [low * cosine + high * minus_sine, high * cosine - low * minus_sine], axis=-1
+        ).astype(jnp.bfloat16)
+        values = jnp.concatenate([lower[:, half:head], upper[:, half:head]], axis=-1)
+        values = values.astype(jnp.bfloat16)
+        queries = []
+        for side in range(2):
+            parity = core if side == 0 else 1 - core
+            at_query = pl.ds(pl.multiple_of((2 * home + parity) * head, head), head)
+            delta = jnp.dot(low_ref[...], up_ref[:, at_query], preferred_element_type=jnp.float32)
+            place = (side * count + index) * head
+            query = q_raw[:, place : place + head]
+            query = jnp.concatenate([query[:pr_rows], query[pr_rows:] + delta], axis=0)
+            scale = lax.rsqrt(jnp.mean(query * query, axis=-1, keepdims=True) + epsilon)
+            query = query * scale * q_gain_ref[...]
+            query = query * q_cos + pltpu.roll(query, half, 1) * q_sin
+            queries.append(query.astype(jnp.bfloat16))
+        scores = lax.dot_general(
+            jnp.concatenate([query[:pr_rows] for query in queries], axis=0),
+            keys[:prompt_keys],
+            nt_dims,
+            preferred_element_type=jnp.float32,
+        )
+        scores = scores * factor + prompt_sees
+        weights = jnp.exp2(scores - jnp.max(scores, axis=-1, keepdims=True))
+        total = jnp.sum(weights, axis=-1, keepdims=True)
+        summed = jnp.dot(
+            weights.astype(jnp.bfloat16), values[:prompt_keys], preferred_element_type=jnp.float32
+        )
+        summed = summed / total
+        for side in range(2):
+            parity = core if side == 0 else 1 - core
+            at_side = pl.ds(pl.multiple_of((2 * index + parity) * head, head), head)
+            prompt_buf[:, at_side] = jnp.where(
+                prompt_ok, summed[side * pr_rows : (side + 1) * pr_rows], 0.0
+            ).astype(jnp.bfloat16)
+            scores = lax.dot_general(
+                queries[side][pr_rows:], keys, nt_dims, preferred_element_type=jnp.float32
+            )
+            p_scores = scores[:, :prompt_keys] * factor + suffix_sees
+            s_scores = scores[:, prompt_keys:] * factor + own_sees
+            top = jnp.maximum(
+                jnp.max(p_scores, axis=-1, keepdims=True),
+                jnp.max(s_scores, axis=-1, keepdims=True),
+            )
+            weights = jnp.concatenate(
+                [jnp.exp2(p_scores - top), jnp.exp2(s_scores - top)], axis=-1
+            )
+            total = jnp.sum(weights, axis=-1, keepdims=True)
+            result = jnp.dot(
+                weights.astype(jnp.bfloat16), values, preferred_element_type=jnp.float32
+            )
+            result = jnp.where(suffix_ok, result / total, 0.0)
+            suffix_buf[:, at_side] = result.astype(jnp.bfloat16)
+        at_pair = pl.ds(pl.multiple_of(home * 2 * head, 2 * head), 2 * head)
+        for number, (buffer, out) in enumerate(((prompt_buf, prompt_out), (suffix_buf, suffix_out))):
+            copy = pltpu.make_async_copy(
+                buffer.at[:, pl.ds(index * 2 * head, 2 * head)],
+                out.at[:, at_pair],
+                sems.at[2 * index + number],
+            )
+            copy.start()
+            copies.append(copy)
+    for copy in copies:
+        copy.wait()
+
+
+def shards_torus(
+    x_prompt,
+    x_suffix,
+    norm_gain,
+    w_query,
+    w_key,
+    w_value,
+    query_gain,
+    key_gain,
+    adapter_down,
+    adapter_up,
+    prompt_len,
+    member_count,
+    suffix_len,
+    adapter_id,
+    holder_slot,
+):
+    bf16 = jnp.bfloat16
+    fsdp_rank = lax.axis_index("fsdp")
+    pr_rows, model_width = x_prompt.shape[1:]
+    suf_rows = x_suffix.shape[2]
+    row_count = 4 * pr_rows + suf_rows
+    depth = w_query.shape[0]
+    slices = model_width // depth
+    rank_size = adapter_down.shape[1]
+    q_cols = adapter_up.shape[2]
+    store_rows = (model_width + q_cols) // depth * rank_size
+    tail = 2 * head + store_rows
+    small = pltpu.CompilerParams(vmem_limit_bytes=12 << 20)
+
+    def cost(flops, size):
+        return pl.CostEstimate(flops=flops, bytes_accessed=size, transcendentals=0)
+
+    own, near = pl.pallas_call(
+        pack_kernel,
+        out_shape=(
+            jax.ShapeDtypeStruct((tail + slices * pr_rows, depth), bf16),
+            jax.ShapeDtypeStruct((2 * head, depth), bf16),
+        ),
+        in_specs=[in_hbm] * 6,
+        scratch_shapes=[
+            (
+                pltpu.VMEM(w_query.shape, bf16),
+                pltpu.VMEM(adapter_down.shape, bf16),
+                pltpu.VMEM(adapter_up.shape, bf16),
+            ),
+            pltpu.SemaphoreType.DMA((5 + slices,)),
+        ],
+        compiler_params=small,
+        name="pack",
+    )(
+        *(
+            pltpu.with_memory_space_constraint(operand, pltpu.HBM)
+            for operand in (w_key.T, w_value.T, w_query, adapter_down, adapter_up, x_prompt[0])
+        )
+    )
+
+    key_owners = slice_owners()
+    prompt_pos = [owner * pr_rows + jnp.arange(pr_rows) for owner in key_owners]
+    suffix_pos = prompt_len[0] + jnp.arange(suf_rows)
+    positions = jnp.concatenate(prompt_pos[1:] + prompt_pos[:1] + [suffix_pos])
+    half_dim = head // 2
+    frequency = rope_base ** (-jnp.arange(half_dim).astype(jnp.float32) / half_dim)
+    angles = positions.astype(jnp.float32)[:, None] * frequency[None, :]
+    cosine, sine = jnp.cos(angles), jnp.sin(angles)
+    cos_pair = jnp.concatenate([cosine, cosine], axis=1)
+    sin_pair = jnp.concatenate([-sine, sine], axis=1)
+    member = lax.dynamic_slice_in_dim(adapter_id[0], fsdp_rank, 1)
+    slot = jnp.sum(
+        jnp.where(member == jnp.arange(holder_slot.shape[0]), holder_slot, 0), keepdims=True
+    )
+    info = jnp.stack(
+        [
+            prompt_len[0],
+            (fsdp_rank < member_count[0]).astype(jnp.int32),
+            suffix_len[0, 0],
+        ]
+    )
+
+    def swapped(*blocks, rows=None):
+        return permute(jnp.concatenate([block[:rows] for block in blocks], axis=0), core_swap)
+
+    own_side = permute(own, first_hop)
+    own_other = permute(own, second_hop)
+    step_one = permute(near, ring_hop)
+    step_three = permute(near, ring_back)
+    own, own_side, own_other, step_one, step_three, cos_pair, sin_pair, slot, info = together(
+        own, own_side, own_other, step_one, step_three, cos_pair, sin_pair, slot, info
+    )
+
+    own_corner = permute(own_side, second_hop)
+    along = permute(jnp.concatenate([step_one, own_side[: 2 * head]], axis=0), ring_hop)
+    step_two, one_side = along[: 2 * head], along[2 * head :]
+    three_side = permute(step_three, first_hop)
+    far = jnp.concatenate([step_one, step_three], axis=0)
+    far_other = permute(far, second_hop)
+    own_near = swapped(own, own_other, own_side, rows=tail)
+    own, own_side, own_other, own_corner, step_two, far, one_side, three_side, far_other, own_near = (
+        together(
+            own, own_side, own_other, own_corner, step_two,
+            far, one_side, three_side, far_other, own_near,
+        )
+    )
+
+    far_side = jnp.concatenate([one_side, three_side], axis=0)
+    one_corner = permute(own_corner[: 2 * head], ring_hop)
+    three_corner = permute(three_side, second_hop)
+    two_side = permute(step_two, first_hop)
+    two_other = permute(step_two, second_hop)
+    own_blocks = (own, own_side, own_other, own_corner, own_near, swapped(own_corner, rows=tail))
+    far_near = swapped(far, far_other, far_side)
+
+    normed = pl.pallas_call(
+        functools.partial(norm_kernel, tail=tail),
+        out_shape=jax.ShapeDtypeStruct((slices, row_count, depth), bf16),
+        compiler_params=small,
+        cost_estimate=cost(0, row_count * model_width * 4),
+        name="norm_rows",
+    )(own, own_side, own_other, own_corner, x_suffix[0, 0], norm_gain[None, :])
+
+    low, up = pl.pallas_call(
+        functools.partial(adapter_kernel, first_row=4 * pr_rows),
+        out_shape=(
+            jax.ShapeDtypeStruct((suf_rows, 8 * rank_size), bf16),
+            jax.ShapeDtypeStruct((8 * rank_size, q_cols), bf16),
+        ),
+        in_specs=[in_vmem, in_smem] + [in_vmem] * 6,
+        compiler_params=small,
+        cost_estimate=cost(2 * suf_rows * model_width * 8 * rank_size, 2 << 20),
+        name="adapter",
+    )(normed, slot, *own_blocks)
+
+    def attend(steps, blocks, results):
+        count = len(steps)
+        return pl.pallas_call(
+            functools.partial(attend_kernel, steps=steps, first=not results),
+            out_shape=(
+                jax.ShapeDtypeStruct((pr_rows, q_cols), bf16),
+                jax.ShapeDtypeStruct((suf_rows, q_cols), bf16),
+            ),
+            in_specs=[in_smem] + [in_vmem] * 13 + [in_any] * len(results),
+            out_specs=[in_any] * 2,
+            scratch_shapes=[
+                pltpu.VMEM((pr_rows, 2 * head * count), bf16),
+                pltpu.VMEM((suf_rows, 2 * head * count), bf16),
+                pltpu.SemaphoreType.DMA((2 * count,)),
+            ],
+            input_output_aliases={14: 0, 15: 1} if results else {},
+            compiler_params=small,
+            cost_estimate=cost(2 * row_count * model_width * 512 * count, count << 20),
+            name="attend",
+        )(
+            info,
+            normed,
+            cos_pair,
+            sin_pair,
+            query_gain[None, :],
+            key_gain[None, :],
+            low,
+            up,
+            *blocks,
+            *results,
+        )
+
+    results = attend((0,), own_blocks, ())
+    one_corner, three_corner, step_two, two_side, two_other, far_near, *results = together(
+        one_corner, three_corner, step_two, two_side, two_other, far_near, *results
+    )
+    far_corner = jnp.concatenate([one_corner, three_corner], axis=0)
+
+    two_corner = permute(two_side, second_hop)
+    far_blocks = (far, far_side, far_other, far_corner, far_near, swapped(far_corner))
+    two_near = swapped(step_two, two_other, two_side)
+    two_corner, two_near, *results = together(
+        two_corner, two_near, *attend((1, 3), far_blocks, results)
+    )
+    two_blocks = (step_two, two_side, two_other, two_corner, two_near, swapped(two_corner))
+    prompt_res, suffix_res = attend((2,), two_blocks, results)
+    return prompt_res[None], suffix_res[None, None]
+
+
+def shards(*operands):
+    x_suffix, w_query, w_key, query_gain = operands[1], operands[3], operands[4], operands[6]
+    head_dim = query_gain.shape[0]
+    fits = (
+        (lax.axis_size("fsdp"), lax.axis_size("req")) == (4, 8)
+        and head_dim == 128
+        and w_query.shape[1] == head_dim
+        and 2 * w_key.shape[1] == head_dim
+        and x_suffix.shape[1] == 1
+        and operands[8].shape[0] == 2
+    )
+    return shards_torus(*operands) if fits else shards_general(*operands)
+
+
 def solution(mesh):
     return jax.shard_map(
         shards,

time: 201 us -> 68.5 us (0.34)
  blocking collectives: 82.4 us -> 0 us
  waiting for transfers between devices: 67.3 us -> 23.8 us
  starting transfers between devices: 0.16 us -> 20.1 us
  Pallas kernels: 0 us -> 16.7 us
  matrix products: 15.3 us -> 0 us
  between operations: 18.2 us -> 3.06 us
  local copies, waits for them, and re-layouts: 8.99 us -> 0.94 us
  other arithmetic: 8.1 us -> 3.69 us
    all_gather x6 -> x0, blocking collectives: 82.4 us -> none  [the longest x1 18 us: shards(): lax.all_gather(w_value, 'req', axis=1, tiled=True)]
    all_gather x4 -> x0, waiting for transfers between devices: 66.1 us -> none  [the longest x1 33.7 us: shards(): lax.all_gather(full_k, 'fsdp', axis=0, tiled=True)]
    ppermute x0 -> x19, waiting for transfers between devices: none -> 23.8 us  [permute(): return lax.ppermute(value, axes, hop)]
    ppermute x0 -> x19, starting transfers between devices: none -> 20.1 us  [permute(): return lax.ppermute(value, axes, hop)]
    pallas_call x0 -> x6, Pallas kernels: none -> 16.7 us  [the longest x3 13.2 us: attend(): pl.pallas_call(functools.partial(attend_kernel, steps=steps, first=not re...]
    dot_general x8 -> x0, matrix products: 15.3 us -> none  [the longest x3 9.71 us: shards(): jnp.dot(normed, weight_piece, preferred_element_type=jnp.float32)]
    unnamed x29 -> x12, local copies, waits for them, and re-layouts: 2.63 us -> 0.07 us
  transfers between devices with their start and end apart: 4 -> 19, of which waited for: 3 -> 8; matrix products, arithmetic and copies ran while one was open for 6% -> 6% of each run, Pallas kernels for 0% -> 17%
where the time goes in v2:
time: 68.5 us; the launch traced here: 68.3 us
  waiting for transfers between devices  23.8 us (35%)
  starting transfers between devices  20.1 us (29%)
  Pallas kernels  16.7 us (24%)
  other arithmetic  3.69 us (5%)
  between operations  3.06 us (4%)
  local copies, waits for them, and re-layouts  0.94 us (1%)
    ppermute x19, waiting for transfers between devices, permute(): return lax.ppermute(value, axes, hop)  23.8 us
    ppermute x19, starting transfers between devices, permute(): return lax.ppermute(value, axes, hop)  20.1 us
    pallas_call x3, Pallas kernels, attend(): pl.pallas_call(functools.partial(attend_kernel, steps=steps, first=not re...  13.2 us
    reduce_sum x1, other arithmetic, shards_torus(): jnp.sum(jnp.where(member == jnp.arange(holder_slot.shape[0]), holder_slot...  2.02 us
  transfers between devices with their start and end apart: 19, of which 8 were waited for; matrix products, arithmetic and copies ran while one was open for 6% of the time, Pallas kernels for 17%

profile of v2, /device:TPU:0, one launch (start us, length us, event | category | flops | bytes accessed | tf_op | source)
XLA Modules:
  0.0 68.3 jit_solution(9638022233072045782)
XLA Ops:
  0.6 0.0 copy-start
  0.6 1.3 %pack.1 = (bf16[608,512]{1,0:T(8,128)(2,1)S(1)}, bf16[256,512]{1,0:T(8,128)(2,1)S(1)}) custom-call(bf16[64,512]{1,0:T(8,128)(2,1)} %bitcast.29, bf16[64,512]{1,0:T(8,128)(2,1)} %bitcast.30, bf16[512,128]{1,0:T(8,128)(2,1)} %query_ref.1, bf16[2,16,2048]{2,1,0:T(8,128)(2,1)} %down_ref.1, bf16[2,16,1024]{2,1,0:T(8,128)(2,1)} %up_ref.1, bf16[64,2048]{1,0:T(8,128)(2,1)} %bitcast.27), custom_call_target="tpu_custom_call" | custom-call | tf_op jit(solution)/shard_map/pack/pallas_call | solution.py:563
  2.0 3.0 %collective-permute-start = (bf16[608,512]{1,0:T(8,128)(2,1)S(1)}, bf16[608,512]{1,0:T(8,128)(2,1)S(1)}, u32[]{:S(2)}, u32[]{:S(2)}) collective-permute-start(bf16[608,512]{1,0:T(8,128)(2,1)S(1)} %get-tuple-element.51.own_ref.refs_0_.refs_8_), channel_id=1, source_target_pairs={{0,8},{1,17},{2,10},{3,19},{4,12},{5,21},{6,14},{7,23},{8,0},{9,25... | collective-permute-start | bytes 1867784 | tf_op jit(solution)/shard_map/ppermute | solution.py:239
  5.0 1.5 %collective-permute-start.1 = (bf16[608,512]{1,0:T(8,128)(2,1)S(1)}, bf16[608,512]{1,0:T(8,128)(2,1)S(1)}, u32[]{:S(2)}, u32[]{:S(2)}) collective-permute-start(bf16[608,512]{1,0:T(8,128)(2,1)S(1)} %get-tuple-element.51.own_ref.refs_0_.refs_8_), channel_id=1, source_target_pairs={{0,16},{1,9},{2,18},{3,11},{4,20},{5,13},{6,22},{7,15},{8,24},{9,1... | collective-permute-start | bytes 1867784 | tf_op jit(solution)/shard_map/ppermute | solution.py:239
  6.5 1.6 %collective-permute-start.2 = (bf16[256,512]{1,0:T(8,128)(2,1)S(1)}, bf16[256,512]{1,0:T(8,128)(2,1)S(1)}, u32[]{:S(2)}, u32[]{:S(2)}) collective-permute-start(bf16[256,512]{1,0:T(8,128)(2,1)S(1)} %get-tuple-element.44), channel_id=1, source_target_pairs={{0,2},{1,3},{2,4},{3,5},{4,6},{5,7},{6,0},{7,1},{8,10},{9,11},{10,... | collective-permute-start | bytes 786440 | tf_op jit(solution)/shard_map/ppermute | solution.py:239
  8.1 2.2 %collective-permute-start.3 = (bf16[256,512]{1,0:T(8,128)(2,1)S(1)}, bf16[256,512]{1,0:T(8,128)(2,1)S(1)}, u32[]{:S(2)}, u32[]{:S(2)}) collective-permute-start(bf16[256,512]{1,0:T(8,128)(2,1)S(1)} %get-tuple-element.44), channel_id=1, source_target_pairs={{0,6},{1,7},{2,0},{3,1},{4,2},{5,3},{6,4},{7,5},{8,14},{9,15},{10,... | collective-permute-start | bytes 786440 | tf_op jit(solution)/shard_map/ppermute | solution.py:239
  11.0 0.6 constant_dynamic-slice_fusion
  11.6 2.0 %fusion.1 = s32[]{:T(128)} fusion(s32[8]{0:T(128)} %param.29, s32[]{:T(128)} %bitcast.4), kind=kLoop, calls=%fused_computation.16 | loop fusion | flops 23 | bytes 40 | tf_op jit(solution)/shard_map/reduce_sum | solution.py:598
  13.6 0.1 concatenate.35
  15.0 1.0 %fusion = (f32[512,64]{1,0:T(8,128)S(1)}, f32[512,64]{1,0:T(8,128)S(1)}, f32[512,64]{1,0:T(8,128)S(1)}) fusion(f32[64]{0:T(128)S(1)} %multiply_power_fusion, f32[512]{0:T(512)S(1)} %convert_element_type.15), kind=kLoop, calls=%fused_computation.9 | loop fusion | flops 65536 | bytes 395520 | tf_op jit(solution)/shard_map/neg | solution.py:596
  16.0 0.1 pad_add_fusion.refs_0_
  16.1 0.1 pad_maximum_fusion.5.refs_2_
  16.3 0.1 pad_maximum_fusion.6.refs_3_
  16.4 1.2 %collective-permute-done.2 = bf16[256,512]{1,0:T(8,128)(2,1)S(1)} collective-permute-done((bf16[256,512]{1,0:T(8,128)(2,1)S(1)}, bf16[256,512]{1,0:T(8,128)(2,1)S(1)}, u32[]{:S(2)}, u32[]{:S(2)}) %collective-permute-start.2) | collective-permute-done | bytes 262176 | tf_op jit(solution)/shard_map/ppermute | solution.py:239
  17.6 3.3 %collective-permute-done.3 = bf16[256,512]{1,0:T(8,128)(2,1)S(1)} collective-permute-done((bf16[256,512]{1,0:T(8,128)(2,1)S(1)}, bf16[256,512]{1,0:T(8,128)(2,1)S(1)}, u32[]{:S(2)}, u32[]{:S(2)}) %collective-permute-start.3) | collective-permute-done | bytes 262176 | tf_op jit(solution)/shard_map/ppermute | solution.py:239
  20.9 0.0 collective-permute-done.side_ref.refs_1_.refs_9_
  21.0 0.1 pad_maximum_fusion.1
  21.1 0.1 collective-permute-start.8
  21.2 1.2 %collective-permute-start.5 = (bf16[512,512]{1,0:T(8,128)(2,1)S(1)}, bf16[512,512]{1,0:T(8,128)(2,1)S(1)}, u32[]{:S(2)}, u32[]{:S(2)}) collective-permute-start(bf16[512,512]{1,0:T(8,128)(2,1)S(1)} %pad_maximum_fusion.3), channel_id=1, source_target_pairs={{0,2},{1,3},{2,4},{3,5},{4,6},{5,7},{6,0},{7,1},{8,10},{9,11},{10,... | collective-permute-start | bytes 1572872 | tf_op jit(solution)/shard_map/ppermute | solution.py:239
  22.4 0.5 collective-permute-start.4
  23.0 1.6 %collective-permute-start.7 = (bf16[512,512]{1,0:T(8,128)(2,1)S(1)}, bf16[512,512]{1,0:T(8,128)(2,1)S(1)}, u32[]{:S(2)}, u32[]{:S(2)}) collective-permute-start(bf16[512,512]{1,0:T(8,128)(2,1)S(1)} %constant_dynamic-update-slice_fusion.refs_8_), channel_id=1, source_target_pairs={{0,16},{1,9},{2,18},{3,11},{4,20},{5,13},{6,22},{7,15},{8,24},{9,1... | collective-permute-start | bytes 1572872 | tf_op jit(solution)/shard_map/ppermute | solution.py:239
  24.6 1.4 %collective-permute-start.6 = (bf16[256,512]{1,0:T(8,128)(2,1)S(1)}, bf16[256,512]{1,0:T(8,128)(2,1)S(1)}, u32[]{:S(2)}, u32[]{:S(2)}) collective-permute-start(bf16[256,512]{1,0:T(8,128)(2,1)S(1)} %collective-permute-done.3), channel_id=1, source_target_pairs={{0,8},{1,17},{2,10},{3,19},{4,12},{5,21},{6,14},{7,23},{8,0},{9,25... | collective-permute-start | bytes 786440 | tf_op jit(solution)/shard_map/ppermute | solution.py:239
  26.0 11.4 %collective-permute-done.5 = bf16[512,512]{1,0:T(8,128)(2,1)S(1)} collective-permute-done((bf16[512,512]{1,0:T(8,128)(2,1)S(1)}, bf16[512,512]{1,0:T(8,128)(2,1)S(1)}, u32[]{:S(2)}, u32[]{:S(2)}) %collective-permute-start.5) | collective-permute-done | bytes 524320 | tf_op jit(solution)/shard_map/ppermute | solution.py:239
  37.5 3.7 %collective-permute-done.7.refs_10_ = bf16[512,512]{1,0:T(8,128)(2,1)S(1)} collective-permute-done((bf16[512,512]{1,0:T(8,128)(2,1)S(1)}, bf16[512,512]{1,0:T(8,128)(2,1)S(1)}, u32[]{:S(2)}, u32[]{:S(2)}) %collective-permute-start.7) | collective-permute-done | bytes 524320 | tf_op jit(solution)/shard_map/ppermute | solution.py:239
  41.1 0.0 copy-start.2
  41.1 0.1 pad_maximum_fusion
  41.2 0.1 collective-permute-start.14
  41.4 0.6 collective-permute-start.9
  41.9 0.6 collective-permute-start.11
  42.5 1.6 %collective-permute-start.10 = (bf16[256,512]{1,0:T(8,128)(2,1)S(1)}, bf16[256,512]{1,0:T(8,128)(2,1)S(1)}, u32[]{:S(2)}, u32[]{:S(2)}) collective-permute-start(bf16[256,512]{1,0:T(8,128)(2,1)S(1)} %slice.31), channel_id=1, source_target_pairs={{0,2},{1,3},{2,4},{3,5},{4,6},{5,7},{6,0},{7,1},{8,10},{9,11},{10,... | collective-permute-start | bytes 786440 | tf_op jit(solution)/shard_map/ppermute | solution.py:239
  44.1 1.5 %collective-permute-start.12 = (bf16[256,512]{1,0:T(8,128)(2,1)S(1)}, bf16[256,512]{1,0:T(8,128)(2,1)S(1)}, u32[]{:S(2)}, u32[]{:S(2)}) collective-permute-start(bf16[256,512]{1,0:T(8,128)(2,1)S(1)} %get-tuple-element.68.refs_8_), channel_id=1, source_target_pairs={{0,8},{1,17},{2,10},{3,19},{4,12},{5,21},{6,14},{7,23},{8,0},{9,25... | collective-permute-start | bytes 786440 | tf_op jit(solution)/shard_map/ppermute | solution.py:239
  45.6 1.4 %collective-permute-start.13 = (bf16[256,512]{1,0:T(8,128)(2,1)S(1)}, bf16[256,512]{1,0:T(8,128)(2,1)S(1)}, u32[]{:S(2)}, u32[]{:S(2)}) collective-permute-start(bf16[256,512]{1,0:T(8,128)(2,1)S(1)} %get-tuple-element.68.refs_8_), channel_id=1, source_target_pairs={{0,16},{1,9},{2,18},{3,11},{4,20},{5,13},{6,22},{7,15},{8,24},{9,1... | collective-permute-start | bytes 786440 | tf_op jit(solution)/shard_map/ppermute | solution.py:239
  47.0 1.0 %norm_rows.1.x_ref.refs_1_ = bf16[4,512,512]{2,1,0:T(8,128)(2,1)S(1)} custom-call(bf16[608,512]{1,0:T(8,128)(2,1)S(1)} %get-tuple-element.51.own_ref.refs_0_.refs_8_, bf16[608,512]{1,0:T(8,128)(2,1)S(1)} %collective-permute-done.side_ref.refs_1_.refs_9_, bf16[608,512]{1,0:T(8,128)(2,1)S(1)} %collective-permute-done.1.other_ref.refs_2_.refs_10_, ...), custom_call_target="tpu_custom_call" | custom-call | bytes 4194304 | tf_op jit(solution)/shard_map/norm_rows/pallas_call | solution.py:642
  48.0 0.0 copy-start.3
  48.0 0.0 copy-start.4
  48.0 1.1 %adapter.1 = (bf16[256,128]{1,0:T(8,128)(2,1)S(1)}, bf16[128,1024]{1,0:T(8,128)(2,1)S(1)}) custom-call(bf16[4,512,512]{2,1,0:T(8,128)(2,1)S(1)} %norm_rows.1.x_ref.refs_1_, s32[1]{0:T(128)} %bitcast.5.slot_ref, bf16[608,512]{1,0:T(8,128)(2,1)S(1)} %get-tuple-element.51.own_ref.refs_0_.refs_8_, ...), custom_call_target="tpu_custom_call" | custom-call | flops 134217728 | bytes 2097152 | tf_op jit(solution)/shard_map/adapter/pallas_call | solution.py:650
  49.1 3.9 %attend.3 = (bf16[64,1024]{1,0:T(8,128)(2,1)}, bf16[256,1024]{1,0:T(8,128)(2,1)}) custom-call(s32[3]{0:T(128)S(1)} %pad_add_fusion.refs_0_, bf16[4,512,512]{2,1,0:T(8,128)(2,1)S(1)} %norm_rows.1.x_ref.refs_1_, f32[512,128]{1,0:T(8,128)S(1)} %pad_maximum_fusion.5.refs_2_, f32[512,128]{1,0:T(8,128)S(1)} %pad_maximum_fusion.6.refs_3_, f32[1,128]{1,0:T(1,128)S(1)} %bitcast.20, ...), custom_call_target="tpu_custom_call" | custom-call | flops 1073741824 | bytes 1048576 | tf_op jit(solution)/shard_map/attend/pallas_call | solution.py:664
  53.0 0.1 collective-permute-done.10
  53.1 0.9 %collective-permute-done.13.refs_10_ = bf16[256,512]{1,0:T(8,128)(2,1)S(1)} collective-permute-done((bf16[256,512]{1,0:T(8,128)(2,1)S(1)}, bf16[256,512]{1,0:T(8,128)(2,1)S(1)}, u32[]{:S(2)}, u32[]{:S(2)}) %collective-permute-start.13) | collective-permute-done | bytes 262176 | tf_op jit(solution)/shard_map/ppermute | solution.py:239
  54.0 0.1 pad_maximum_fusion.2
  54.1 0.1 collective-permute-start.16
  54.2 0.6 collective-permute-start.17
  54.7 0.5 collective-permute-start.15
  55.3 1.9 %collective-permute-done.17.refs_13_ = bf16[512,512]{1,0:T(8,128)(2,1)S(1)} collective-permute-done((bf16[512,512]{1,0:T(8,128)(2,1)S(1)}, bf16[512,512]{1,0:T(8,128)(2,1)S(1)}, u32[]{:S(2)}, u32[]{:S(2)}) %collective-permute-start.17) | collective-permute-done | bytes 524320 | tf_op jit(solution)/shard_map/ppermute | solution.py:239
  57.2 5.4 %attend.4 = (bf16[64,1024]{1,0:T(8,128)(2,1)}, bf16[256,1024]{1,0:T(8,128)(2,1)}) custom-call(s32[3]{0:T(128)S(1)} %pad_add_fusion.refs_0_, bf16[4,512,512]{2,1,0:T(8,128)(2,1)S(1)} %norm_rows.1.x_ref.refs_1_, f32[512,128]{1,0:T(8,128)S(1)} %pad_maximum_fusion.5.refs_2_, ...), custom_call_target="tpu_custom_call", output_to_operand_aliasing={{0}: (14, {}), {1}: (15, {})} | custom-call | flops 2147483648 | bytes 2097152 | tf_op jit(solution)/shard_map/attend/pallas_call | solution.py:664
  62.6 0.2 collective-permute-start.18
  62.8 1.4 %collective-permute-done.18.refs_13_ = bf16[256,512]{1,0:T(8,128)(2,1)S(1)} collective-permute-done((bf16[256,512]{1,0:T(8,128)(2,1)S(1)}, bf16[256,512]{1,0:T(8,128)(2,1)S(1)}, u32[]{:S(2)}, u32[]{:S(2)}) %collective-permute-start.18) | collective-permute-done | bytes 262176 | tf_op jit(solution)/shard_map/ppermute | solution.py:239
  64.2 3.9 %attend.5 = (bf16[64,1024]{1,0:T(8,128)(2,1)}, bf16[256,1024]{1,0:T(8,128)(2,1)}) custom-call(s32[3]{0:T(128)S(1)} %pad_add_fusion.refs_0_, bf16[4,512,512]{2,1,0:T(8,128)(2,1)S(1)} %norm_rows.1.x_ref.refs_1_, f32[512,128]{1,0:T(8,128)S(1)} %pad_maximum_fusion.5.refs_2_, ...), custom_call_target="tpu_custom_call", output_to_operand_aliasing={{0}: (14, {}), {1}: (15, {})} | custom-call | flops 1073741824 | bytes 1048576 | tf_op jit(solution)/shard_map/attend/pallas_call | solution.py:664
  (34 shorter events, 0.4 us)
Async XLA Ops:
  0.6 10.4 %copy-start = (s32[1,4]{1,0:T(1,128)S(1)}, s32[1,4]{1,0:T(1,128)}, u32[]{:S(2)}) copy-start(s32[1,4]{1,0:T(1,128)} %param.28) | copy-start | bytes 52
  2.0 18.9 %collective-permute-start = (bf16[608,512]{1,0:T(8,128)(2,1)S(1)}, bf16[608,512]{1,0:T(8,128)(2,1)S(1)}, u32[]{:S(2)}, u32[]{:S(2)}) collective-permute-start(bf16[608,512]{1,0:T(8,128)(2,1)S(1)} %get-tuple-element.51.own_ref.refs_0_.refs_8_), channel_id=1, source_target_pairs={{0,8},{1,17},{2,10},{3,19},{4,12},{5,21},{6,14},{7,23},{8,0},{9,25... | collective-permute-start | bytes 1867784 | tf_op jit(solution)/shard_map/ppermute | solution.py:239
  5.0 15.9 %collective-permute-start.1 = (bf16[608,512]{1,0:T(8,128)(2,1)S(1)}, bf16[608,512]{1,0:T(8,128)(2,1)S(1)}, u32[]{:S(2)}, u32[]{:S(2)}) collective-permute-start(bf16[608,512]{1,0:T(8,128)(2,1)S(1)} %get-tuple-element.51.own_ref.refs_0_.refs_8_), channel_id=1, source_target_pairs={{0,16},{1,9},{2,18},{3,11},{4,20},{5,13},{6,22},{7,15},{8,24},{9,1... | collective-permute-start | bytes 1867784 | tf_op jit(solution)/shard_map/ppermute | solution.py:239
  6.5 11.1 %collective-permute-start.2 = (bf16[256,512]{1,0:T(8,128)(2,1)S(1)}, bf16[256,512]{1,0:T(8,128)(2,1)S(1)}, u32[]{:S(2)}, u32[]{:S(2)}) collective-permute-start(bf16[256,512]{1,0:T(8,128)(2,1)S(1)} %get-tuple-element.44), channel_id=1, source_target_pairs={{0,2},{1,3},{2,4},{3,5},{4,6},{5,7},{6,0},{7,1},{8,10},{9,11},{10,... | collective-permute-start | bytes 786440 | tf_op jit(solution)/shard_map/ppermute | solution.py:239
  8.1 12.8 %collective-permute-start.3 = (bf16[256,512]{1,0:T(8,128)(2,1)S(1)}, bf16[256,512]{1,0:T(8,128)(2,1)S(1)}, u32[]{:S(2)}, u32[]{:S(2)}) collective-permute-start(bf16[256,512]{1,0:T(8,128)(2,1)S(1)} %get-tuple-element.44), channel_id=1, source_target_pairs={{0,6},{1,7},{2,0},{3,1},{4,2},{5,3},{6,4},{7,5},{8,14},{9,15},{10,... | collective-permute-start | bytes 786440 | tf_op jit(solution)/shard_map/ppermute | solution.py:239
  21.1 20.0 %collective-permute-start.8 = (bf16[1056,512]{1,0:T(8,128)(2,1)S(1)}, bf16[1056,512]{1,0:T(8,128)(2,1)S(1)}, u32[]{:S(2)}, u32[]{:S(2)}) collective-permute-start(bf16[1056,512]{1,0:T(8,128)(2,1)S(1)} %pad_maximum_fusion.1), channel_id=1, source_target_pairs={{0,1},{1,0},{2,3},{3,2},{4,5},{5,4},{6,7},{7,6},{8,9},{9,8},{10,11... | collective-permute-start | bytes 3244040 | tf_op jit(solution)/shard_map/ppermute | solution.py:239
  21.2 16.2 %collective-permute-start.5 = (bf16[512,512]{1,0:T(8,128)(2,1)S(1)}, bf16[512,512]{1,0:T(8,128)(2,1)S(1)}, u32[]{:S(2)}, u32[]{:S(2)}) collective-permute-start(bf16[512,512]{1,0:T(8,128)(2,1)S(1)} %pad_maximum_fusion.3), channel_id=1, source_target_pairs={{0,2},{1,3},{2,4},{3,5},{4,6},{5,7},{6,0},{7,1},{8,10},{9,11},{10,... | collective-permute-start | bytes 1572872 | tf_op jit(solution)/shard_map/ppermute | solution.py:239
  22.4 18.7 %collective-permute-start.4 = (bf16[608,512]{1,0:T(8,128)(2,1)S(1)}, bf16[608,512]{1,0:T(8,128)(2,1)S(1)}, u32[]{:S(2)}, u32[]{:S(2)}) collective-permute-start(bf16[608,512]{1,0:T(8,128)(2,1)S(1)} %collective-permute-done.side_ref.refs_1_.refs_9_), channel_id=1, source_target_pairs={{0,16},{1,9},{2,18},{3,11},{4,20},{5,13},{6,22},{7,15},{8,24},{9,1... | collective-permute-start | bytes 1867784 | tf_op jit(solution)/shard_map/ppermute | solution.py:239
  23.0 18.1 %collective-permute-start.7 = (bf16[512,512]{1,0:T(8,128)(2,1)S(1)}, bf16[512,512]{1,0:T(8,128)(2,1)S(1)}, u32[]{:S(2)}, u32[]{:S(2)}) collective-permute-start(bf16[512,512]{1,0:T(8,128)(2,1)S(1)} %constant_dynamic-update-slice_fusion.refs_8_), channel_id=1, source_target_pairs={{0,16},{1,9},{2,18},{3,11},{4,20},{5,13},{6,22},{7,15},{8,24},{9,1... | collective-permute-start | bytes 1572872 | tf_op jit(solution)/shard_map/ppermute | solution.py:239
  24.6 12.9 %collective-permute-start.6 = (bf16[256,512]{1,0:T(8,128)(2,1)S(1)}, bf16[256,512]{1,0:T(8,128)(2,1)S(1)}, u32[]{:S(2)}, u32[]{:S(2)}) collective-permute-start(bf16[256,512]{1,0:T(8,128)(2,1)S(1)} %collective-permute-done.3), channel_id=1, source_target_pairs={{0,8},{1,17},{2,10},{3,19},{4,12},{5,21},{6,14},{7,23},{8,0},{9,25... | collective-permute-start | bytes 786440 | tf_op jit(solution)/shard_map/ppermute | solution.py:239
  41.1 5.9 %copy-start.1 = (bf16[1,1,256,2048]{3,2,1,0:T(8,128)(2,1)S(1)}, bf16[1,1,256,2048]{3,2,1,0:T(8,128)(2,1)}, u32[]{:S(2)}) copy-start(bf16[1,1,256,2048]{3,2,1,0:T(8,128)(2,1)} %param.16) | copy-start | bytes 3145732
  41.1 5.9 %copy-start.2 = (f32[2048]{0:T(1024)S(1)}, f32[2048]{0:T(1024)}, u32[]{:S(2)}) copy-start(f32[2048]{0:T(1024)} %param.17) | copy-start | bytes 24580
  41.2 12.7 %collective-permute-start.14 = (bf16[1536,512]{1,0:T(8,128)(2,1)S(1)}, bf16[1536,512]{1,0:T(8,128)(2,1)S(1)}, u32[]{:S(2)}, u32[]{:S(2)}) collective-permute-start(bf16[1536,512]{1,0:T(8,128)(2,1)S(1)} %pad_maximum_fusion), channel_id=1, source_target_pairs={{0,1},{1,0},{2,3},{3,2},{4,5},{5,4},{6,7},{7,6},{8,9},{9,8},{10,11... | collective-permute-start | bytes 4718600 | tf_op jit(solution)/shard_map/ppermute | solution.py:239
  41.4 4.2 %collective-permute-start.9 = (bf16[352,512]{1,0:T(8,128)(2,1)S(1)}, bf16[352,512]{1,0:T(8,128)(2,1)S(1)}, u32[]{:S(2)}, u32[]{:S(2)}) collective-permute-start(bf16[352,512]{1,0:T(8,128)(2,1)S(1)} %slice.30), channel_id=1, source_target_pairs={{0,1},{1,0},{2,3},{3,2},{4,5},{5,4},{6,7},{7,6},{8,9},{9,8},{10,11... | collective-permute-start | bytes 1081352 | tf_op jit(solution)/shard_map/ppermute | solution.py:239
  41.9 11.2 %collective-permute-start.11 = (bf16[256,512]{1,0:T(8,128)(2,1)S(1)}, bf16[256,512]{1,0:T(8,128)(2,1)S(1)}, u32[]{:S(2)}, u32[]{:S(2)}) collective-permute-start(bf16[256,512]{1,0:T(8,128)(2,1)S(1)} %collective-permute-done.6), channel_id=1, source_target_pairs={{0,16},{1,9},{2,18},{3,11},{4,20},{5,13},{6,22},{7,15},{8,24},{9,1... | collective-permute-start | bytes 786440 | tf_op jit(solution)/shard_map/ppermute | solution.py:239
  42.5 10.6 %collective-permute-start.10 = (bf16[256,512]{1,0:T(8,128)(2,1)S(1)}, bf16[256,512]{1,0:T(8,128)(2,1)S(1)}, u32[]{:S(2)}, u32[]{:S(2)}) collective-permute-start(bf16[256,512]{1,0:T(8,128)(2,1)S(1)} %slice.31), channel_id=1, source_target_pairs={{0,2},{1,3},{2,4},{3,5},{4,6},{5,7},{6,0},{7,1},{8,10},{9,11},{10,... | collective-permute-start | bytes 786440 | tf_op jit(solution)/shard_map/ppermute | solution.py:239
  44.1 9.0 %collective-permute-start.12 = (bf16[256,512]{1,0:T(8,128)(2,1)S(1)}, bf16[256,512]{1,0:T(8,128)(2,1)S(1)}, u32[]{:S(2)}, u32[]{:S(2)}) collective-permute-start(bf16[256,512]{1,0:T(8,128)(2,1)S(1)} %get-tuple-element.68.refs_8_), channel_id=1, source_target_pairs={{0,8},{1,17},{2,10},{3,19},{4,12},{5,21},{6,14},{7,23},{8,0},{9,25... | collective-permute-start | bytes 786440 | tf_op jit(solution)/shard_map/ppermute | solution.py:239
  45.6 8.4 %collective-permute-start.13 = (bf16[256,512]{1,0:T(8,128)(2,1)S(1)}, bf16[256,512]{1,0:T(8,128)(2,1)S(1)}, u32[]{:S(2)}, u32[]{:S(2)}) collective-permute-start(bf16[256,512]{1,0:T(8,128)(2,1)S(1)} %get-tuple-element.68.refs_8_), channel_id=1, source_target_pairs={{0,16},{1,9},{2,18},{3,11},{4,20},{5,13},{6,22},{7,15},{8,24},{9,1... | collective-permute-start | bytes 786440 | tf_op jit(solution)/shard_map/ppermute | solution.py:239
  48.0 1.2 %copy-start.3 = (f32[128]{0:T(128)S(1)}, f32[128]{0:T(128)}, u32[]{:S(2)}) copy-start(f32[128]{0:T(128)} %param.21) | copy-start | bytes 1540
  48.0 1.2 %copy-start.4 = (f32[128]{0:T(128)S(1)}, f32[128]{0:T(128)}, u32[]{:S(2)}) copy-start(f32[128]{0:T(128)} %param.22) | copy-start | bytes 1540
  54.1 8.6 %collective-permute-start.16 = (bf16[768,512]{1,0:T(8,128)(2,1)S(1)}, bf16[768,512]{1,0:T(8,128)(2,1)S(1)}, u32[]{:S(2)}, u32[]{:S(2)}) collective-permute-start(bf16[768,512]{1,0:T(8,128)(2,1)S(1)} %pad_maximum_fusion.2), channel_id=1, source_target_pairs={{0,1},{1,0},{2,3},{3,2},{4,5},{5,4},{6,7},{7,6},{8,9},{9,8},{10,11... | collective-permute-start | bytes 2359304 | tf_op jit(solution)/shard_map/ppermute | solution.py:239
  54.2 3.0 %collective-permute-start.17 = (bf16[512,512]{1,0:T(8,128)(2,1)S(1)}, bf16[512,512]{1,0:T(8,128)(2,1)S(1)}, u32[]{:S(2)}, u32[]{:S(2)}) collective-permute-start(bf16[512,512]{1,0:T(8,128)(2,1)S(1)} %constant_dynamic-update-slice_fusion.2.refs_11_), channel_id=1, source_target_pairs={{0,1},{1,0},{2,3},{3,2},{4,5},{5,4},{6,7},{7,6},{8,9},{9,8},{10,11... | collective-permute-start | bytes 1572872 | tf_op jit(solution)/shard_map/ppermute | solution.py:239
  54.7 7.9 %collective-permute-start.15 = (bf16[256,512]{1,0:T(8,128)(2,1)S(1)}, bf16[256,512]{1,0:T(8,128)(2,1)S(1)}, u32[]{:S(2)}, u32[]{:S(2)}) collective-permute-start(bf16[256,512]{1,0:T(8,128)(2,1)S(1)} %collective-permute-done.12.refs_9_), channel_id=1, source_target_pairs={{0,16},{1,9},{2,18},{3,11},{4,20},{5,13},{6,22},{7,15},{8,24},{9,1... | collective-permute-start | bytes 786440 | tf_op jit(solution)/shard_map/ppermute | solution.py:239
  62.6 1.6 %collective-permute-start.18 = (bf16[256,512]{1,0:T(8,128)(2,1)S(1)}, bf16[256,512]{1,0:T(8,128)(2,1)S(1)}, u32[]{:S(2)}, u32[]{:S(2)}) collective-permute-start(bf16[256,512]{1,0:T(8,128)(2,1)S(1)} %collective-permute-done.15.refs_11_), channel_id=1, source_target_pairs={{0,1},{1,0},{2,3},{3,2},{4,5},{5,4},{6,7},{7,6},{8,9},{9,8},{10,11... | collective-permute-start | bytes 786440 | tf_op jit(solution)/shard_map/ppermute | solution.py:239

commit v3 on v2

--- a/solution.py
+++ b/solution.py
@@ -232,6 +232,9 @@
 second_hop = pairs(lambda x, y, z, c: (x, 1 - y, z, c) if c == 0 else (1 - x, y, z, c))
 ring_hop = pairs(lambda x, y, z, c: (x, y, (z + 1) % 4, c))
 ring_back = pairs(lambda x, y, z, c: (x, y, (z + 3) % 4, c))
+second_hop_across = pairs(
+    lambda x, y, z, c: (x, 1 - y, z, 1 - c) if c == 0 else (1 - x, y, z, 1 - c)
+)
 core_swap = pairs(lambda x, y, z, c: (x, y, z, 1 - c))
 
 
@@ -413,9 +416,9 @@
 
     kv_raw = project(x_ref, slice(None), stacked(0))
     q_raw = project(x_ref, slice(first_query, None), stacked(head))
-    prompt_total = info_ref[0]
-    member_ok = info_ref[1]
-    suffix_total = info_ref[2]
+    prompt_total = info_ref[0:1, 0:1]
+    member_ok = info_ref[1:2, 0:1]
+    suffix_total = info_ref[2:3, 0:1]
 
     def key_positions(rows):
         column = lax.broadcasted_iota(jnp.int32, (rows, prompt_keys), 1)
@@ -605,6 +608,7 @@
             suffix_len[0, 0],
         ]
     )
+    info = jnp.broadcast_to(info[:, None], (3, head))
 
     def swapped(*blocks, rows=None):
         return permute(jnp.concatenate([block[:rows] for block in blocks], axis=0), core_swap)
@@ -667,7 +671,7 @@
                 jax.ShapeDtypeStruct((pr_rows, q_cols), bf16),
                 jax.ShapeDtypeStruct((suf_rows, q_cols), bf16),
             ),
-            in_specs=[in_smem] + [in_vmem] * 13 + [in_any] * len(results),
+            in_specs=[in_vmem] * 14 + [in_any] * len(results),
             out_specs=[in_any] * 2,
             scratch_shapes=[
                 pltpu.VMEM((pr_rows, 2 * head * count), bf16),
@@ -692,18 +696,19 @@
         )
 
     results = attend((0,), own_blocks, ())
-    one_corner, three_corner, step_two, two_side, two_other, far_near, *results = together(
-        one_corner, three_corner, step_two, two_side, two_other, far_near, *results
+    one_corner, three_corner, two_side, far_near, *results = together(
+        one_corner, three_corner, two_side, far_near, *results
     )
     far_corner = jnp.concatenate([one_corner, three_corner], axis=0)
 
     two_corner = permute(two_side, second_hop)
     far_blocks = (far, far_side, far_other, far_corner, far_near, swapped(far_corner))
     two_near = swapped(step_two, two_other, two_side)
-    two_corner, two_near, *results = together(
-        two_corner, two_near, *attend((1, 3), far_blocks, results)
-    )
-    two_blocks = (step_two, two_side, two_other, two_corner, two_near, swapped(two_corner))
+    two_across = permute(two_side, second_hop_across)
+    two_corner, two_across, two_near, *results = together(
+        two_corner, two_across, two_near, *attend((1, 3), far_blocks, results)
+    )
+    two_blocks = (step_two, two_side, two_other, two_corner, two_near, two_across)
     prompt_res, suffix_res = attend((2,), two_blocks, results)
     return prompt_res[None], suffix_res[None, None]
 

time: 68.5 us -> 67.1 us (0.980)
  Pallas kernels: 16.7 us -> 15.2 us
  waiting for transfers between devices: 23.8 us -> 22.9 us
  starting transfers between devices: 20.1 us -> 20.8 us
    pallas_call x3, Pallas kernels: 13.2 us -> 11.8 us  [attend(): pl.pallas_call(functools.partial(attend_kernel, steps=steps, first=not re...]
    ppermute x19, waiting for transfers between devices: 23.8 us -> 22.9 us  [permute(): return lax.ppermute(value, axes, hop)]
    ppermute x19, starting transfers between devices: 20.1 us -> 20.8 us  [permute(): return lax.ppermute(value, axes, hop)]
  transfers between devices with their start and end apart: 19 -> 19, of which waited for: 8 -> 8; matrix products, arithmetic and copies ran while one was open for 6% -> 6% of each run, Pallas kernels for 17% -> 16%
where the time goes in v3:
time: 67.1 us; the launch traced here: 66.7 us
  waiting for transfers between devices  22.9 us (34%)
  starting transfers between devices  20.8 us (31%)
  Pallas kernels  15.2 us (23%)
  other arithmetic  3.69 us (5%)
  between operations  3.06 us (5%)
  local copies, waits for them, and re-layouts  1.01 us (2%)
    ppermute x19, waiting for transfers between devices, permute(): return lax.ppermute(value, axes, hop)  22.9 us
    ppermute x19, starting transfers between devices, permute(): return lax.ppermute(value, axes, hop)  20.8 us
    pallas_call x3, Pallas kernels, attend(): pl.pallas_call(functools.partial(attend_kernel, steps=steps, first=not re...  11.8 us
    reduce_sum x1, other arithmetic, shards_torus(): jnp.sum(jnp.where(member == jnp.arange(holder_slot.shape[0]), holder_slot...  2.02 us
  transfers between devices with their start and end apart: 19, of which 8 were waited for; matrix products, arithmetic and copies ran while one was open for 6% of the time, Pallas kernels for 16%

profile of v3, /device:TPU:0, one launch (start us, length us, event | category | flops | bytes accessed | tf_op | source)
XLA Modules:
  0.0 66.7 jit_solution(1969649463276091450)
XLA Ops:
  0.6 0.0 copy-start
  0.6 1.3 %pack.1 = (bf16[608,512]{1,0:T(8,128)(2,1)S(1)}, bf16[256,512]{1,0:T(8,128)(2,1)S(1)}) custom-call(bf16[64,512]{1,0:T(8,128)(2,1)} %bitcast.29, bf16[64,512]{1,0:T(8,128)(2,1)} %bitcast.30, bf16[512,128]{1,0:T(8,128)(2,1)} %query_ref.1, bf16[2,16,2048]{2,1,0:T(8,128)(2,1)} %down_ref.1, bf16[2,16,1024]{2,1,0:T(8,128)(2,1)} %up_ref.1, bf16[64,2048]{1,0:T(8,128)(2,1)} %bitcast.27), custom_call_target="tpu_custom_call" | custom-call | tf_op jit(solution)/shard_map/pack/pallas_call | solution.py:566
  2.0 3.0 %collective-permute-start = (bf16[608,512]{1,0:T(8,128)(2,1)S(1)}, bf16[608,512]{1,0:T(8,128)(2,1)S(1)}, u32[]{:S(2)}, u32[]{:S(2)}) collective-permute-start(bf16[608,512]{1,0:T(8,128)(2,1)S(1)} %get-tuple-element.50.own_ref.refs_0_.refs_8_), channel_id=1, source_target_pairs={{0,8},{1,17},{2,10},{3,19},{4,12},{5,21},{6,14},{7,23},{8,0},{9,25... | collective-permute-start | bytes 1867784 | tf_op jit(solution)/shard_map/ppermute | solution.py:242
  5.0 1.5 %collective-permute-start.1 = (bf16[608,512]{1,0:T(8,128)(2,1)S(1)}, bf16[608,512]{1,0:T(8,128)(2,1)S(1)}, u32[]{:S(2)}, u32[]{:S(2)}) collective-permute-start(bf16[608,512]{1,0:T(8,128)(2,1)S(1)} %get-tuple-element.50.own_ref.refs_0_.refs_8_), channel_id=1, source_target_pairs={{0,16},{1,9},{2,18},{3,11},{4,20},{5,13},{6,22},{7,15},{8,24},{9,1... | collective-permute-start | bytes 1867784 | tf_op jit(solution)/shard_map/ppermute | solution.py:242
  6.5 1.6 %collective-permute-start.2 = (bf16[256,512]{1,0:T(8,128)(2,1)S(1)}, bf16[256,512]{1,0:T(8,128)(2,1)S(1)}, u32[]{:S(2)}, u32[]{:S(2)}) collective-permute-start(bf16[256,512]{1,0:T(8,128)(2,1)S(1)} %get-tuple-element.43), channel_id=1, source_target_pairs={{0,2},{1,3},{2,4},{3,5},{4,6},{5,7},{6,0},{7,1},{8,10},{9,11},{10,... | collective-permute-start | bytes 786440 | tf_op jit(solution)/shard_map/ppermute | solution.py:242
  8.1 2.2 %collective-permute-start.3 = (bf16[256,512]{1,0:T(8,128)(2,1)S(1)}, bf16[256,512]{1,0:T(8,128)(2,1)S(1)}, u32[]{:S(2)}, u32[]{:S(2)}) collective-permute-start(bf16[256,512]{1,0:T(8,128)(2,1)S(1)} %get-tuple-element.43), channel_id=1, source_target_pairs={{0,6},{1,7},{2,0},{3,1},{4,2},{5,3},{6,4},{7,5},{8,14},{9,15},{10,... | collective-permute-start | bytes 786440 | tf_op jit(solution)/shard_map/ppermute | solution.py:242
  11.0 0.6 constant_dynamic-slice_fusion
  11.6 2.0 %fusion.1 = s32[]{:T(128)} fusion(s32[8]{0:T(128)} %param.29, s32[]{:T(128)} %bitcast.4), kind=kLoop, calls=%fused_computation.16 | loop fusion | flops 23 | bytes 40 | tf_op jit(solution)/shard_map/reduce_sum | solution.py:601
  13.6 0.1 concatenate.35
  15.0 1.0 %fusion = (f32[512,64]{1,0:T(8,128)S(1)}, f32[512,64]{1,0:T(8,128)S(1)}, f32[512,64]{1,0:T(8,128)S(1)}) fusion(f32[64]{0:T(128)S(1)} %multiply_power_fusion, f32[512]{0:T(512)S(1)} %convert_element_type.15), kind=kLoop, calls=%fused_computation.9 | loop fusion | flops 65536 | bytes 395520 | tf_op jit(solution)/shard_map/neg | solution.py:599
  16.0 0.1 pad_add_fusion
  16.1 0.1 pad_maximum_fusion.5.refs_2_
  16.3 0.1 pad_maximum_fusion.6.refs_3_
  16.4 1.2 %collective-permute-done.2 = bf16[256,512]{1,0:T(8,128)(2,1)S(1)} collective-permute-done((bf16[256,512]{1,0:T(8,128)(2,1)S(1)}, bf16[256,512]{1,0:T(8,128)(2,1)S(1)}, u32[]{:S(2)}, u32[]{:S(2)}) %collective-permute-start.2) | collective-permute-done | bytes 262176 | tf_op jit(solution)/shard_map/ppermute | solution.py:242
  17.6 3.3 %collective-permute-done.3 = bf16[256,512]{1,0:T(8,128)(2,1)S(1)} collective-permute-done((bf16[256,512]{1,0:T(8,128)(2,1)S(1)}, bf16[256,512]{1,0:T(8,128)(2,1)S(1)}, u32[]{:S(2)}, u32[]{:S(2)}) %collective-permute-start.3) | collective-permute-done | bytes 262176 | tf_op jit(solution)/shard_map/ppermute | solution.py:242
  20.9 0.1 broadcast_in_dim.36.refs_0_
  21.1 0.1 pad_maximum_fusion.1
  21.1 0.1 collective-permute-start.8
  21.3 1.2 %collective-permute-start.5 = (bf16[512,512]{1,0:T(8,128)(2,1)S(1)}, bf16[512,512]{1,0:T(8,128)(2,1)S(1)}, u32[]{:S(2)}, u32[]{:S(2)}) collective-permute-start(bf16[512,512]{1,0:T(8,128)(2,1)S(1)} %pad_maximum_fusion.3), channel_id=1, source_target_pairs={{0,2},{1,3},{2,4},{3,5},{4,6},{5,7},{6,0},{7,1},{8,10},{9,11},{10,... | collective-permute-start | bytes 1572872 | tf_op jit(solution)/shard_map/ppermute | solution.py:242
  22.5 0.5 collective-permute-start.4
  23.1 1.6 %collective-permute-start.7 = (bf16[512,512]{1,0:T(8,128)(2,1)S(1)}, bf16[512,512]{1,0:T(8,128)(2,1)S(1)}, u32[]{:S(2)}, u32[]{:S(2)}) collective-permute-start(bf16[512,512]{1,0:T(8,128)(2,1)S(1)} %constant_dynamic-update-slice_fusion.refs_8_), channel_id=1, source_target_pairs={{0,16},{1,9},{2,18},{3,11},{4,20},{5,13},{6,22},{7,15},{8,24},{9,1... | collective-permute-start | bytes 1572872 | tf_op jit(solution)/shard_map/ppermute | solution.py:242
  24.7 1.4 %collective-permute-start.6 = (bf16[256,512]{1,0:T(8,128)(2,1)S(1)}, bf16[256,512]{1,0:T(8,128)(2,1)S(1)}, u32[]{:S(2)}, u32[]{:S(2)}) collective-permute-start(bf16[256,512]{1,0:T(8,128)(2,1)S(1)} %collective-permute-done.3), channel_id=1, source_target_pairs={{0,8},{1,17},{2,10},{3,19},{4,12},{5,21},{6,14},{7,23},{8,0},{9,25... | collective-permute-start | bytes 786440 | tf_op jit(solution)/shard_map/ppermute | solution.py:242
  26.0 11.4 %collective-permute-done.5 = bf16[512,512]{1,0:T(8,128)(2,1)S(1)} collective-permute-done((bf16[512,512]{1,0:T(8,128)(2,1)S(1)}, bf16[512,512]{1,0:T(8,128)(2,1)S(1)}, u32[]{:S(2)}, u32[]{:S(2)}) %collective-permute-start.5) | collective-permute-done | bytes 524320 | tf_op jit(solution)/shard_map/ppermute | solution.py:242
  37.5 3.7 %collective-permute-done.7.refs_10_ = bf16[512,512]{1,0:T(8,128)(2,1)S(1)} collective-permute-done((bf16[512,512]{1,0:T(8,128)(2,1)S(1)}, bf16[512,512]{1,0:T(8,128)(2,1)S(1)}, u32[]{:S(2)}, u32[]{:S(2)}) %collective-permute-start.7) | collective-permute-done | bytes 524320 | tf_op jit(solution)/shard_map/ppermute | solution.py:242
  41.2 0.0 copy-start.2
  41.2 0.1 pad_maximum_fusion
  41.3 0.1 collective-permute-start.13
  41.4 0.6 collective-permute-start.9
  42.0 0.6 collective-permute-start.11
  42.6 1.6 %collective-permute-start.10 = (bf16[256,512]{1,0:T(8,128)(2,1)S(1)}, bf16[256,512]{1,0:T(8,128)(2,1)S(1)}, u32[]{:S(2)}, u32[]{:S(2)}) collective-permute-start(bf16[256,512]{1,0:T(8,128)(2,1)S(1)} %slice.31), channel_id=1, source_target_pairs={{0,2},{1,3},{2,4},{3,5},{4,6},{5,7},{6,0},{7,1},{8,10},{9,11},{10,... | collective-permute-start | bytes 786440 | tf_op jit(solution)/shard_map/ppermute | solution.py:242
  44.2 1.5 %collective-permute-start.12 = (bf16[256,512]{1,0:T(8,128)(2,1)S(1)}, bf16[256,512]{1,0:T(8,128)(2,1)S(1)}, u32[]{:S(2)}, u32[]{:S(2)}) collective-permute-start(bf16[256,512]{1,0:T(8,128)(2,1)S(1)} %get-tuple-element.60.refs_8_), channel_id=1, source_target_pairs={{0,8},{1,17},{2,10},{3,19},{4,12},{5,21},{6,14},{7,23},{8,0},{9,25... | collective-permute-start | bytes 786440 | tf_op jit(solution)/shard_map/ppermute | solution.py:242
  45.7 1.4 %collective-permute-start.14 = (bf16[256,512]{1,0:T(8,128)(2,1)S(1)}, bf16[256,512]{1,0:T(8,128)(2,1)S(1)}, u32[]{:S(2)}, u32[]{:S(2)}) collective-permute-start(bf16[256,512]{1,0:T(8,128)(2,1)S(1)} %get-tuple-element.60.refs_8_), channel_id=1, source_target_pairs={{0,16},{1,9},{2,18},{3,11},{4,20},{5,13},{6,22},{7,15},{8,24},{9,1... | collective-permute-start | bytes 786440 | tf_op jit(solution)/shard_map/ppermute | solution.py:242
  47.1 1.0 %norm_rows.1.x_ref.refs_1_ = bf16[4,512,512]{2,1,0:T(8,128)(2,1)S(1)} custom-call(bf16[608,512]{1,0:T(8,128)(2,1)S(1)} %get-tuple-element.50.own_ref.refs_0_.refs_8_, bf16[608,512]{1,0:T(8,128)(2,1)S(1)} %collective-permute-done.side_ref.refs_1_.refs_9_, bf16[608,512]{1,0:T(8,128)(2,1)S(1)} %collective-permute-done.1.other_ref.refs_2_.refs_10_, ...), custom_call_target="tpu_custom_call" | custom-call | bytes 4194304 | tf_op jit(solution)/shard_map/norm_rows/pallas_call | solution.py:646
  48.0 0.0 copy-start.3
  48.0 0.0 copy-start.4
  48.0 1.1 %adapter.1 = (bf16[256,128]{1,0:T(8,128)(2,1)S(1)}, bf16[128,1024]{1,0:T(8,128)(2,1)S(1)}) custom-call(bf16[4,512,512]{2,1,0:T(8,128)(2,1)S(1)} %norm_rows.1.x_ref.refs_1_, s32[1]{0:T(128)} %bitcast.5.slot_ref, bf16[608,512]{1,0:T(8,128)(2,1)S(1)} %get-tuple-element.50.own_ref.refs_0_.refs_8_, ...), custom_call_target="tpu_custom_call" | custom-call | flops 134217728 | bytes 2097152 | tf_op jit(solution)/shard_map/adapter/pallas_call | solution.py:654
  49.2 3.4 %attend.3 = (bf16[64,1024]{1,0:T(8,128)(2,1)}, bf16[256,1024]{1,0:T(8,128)(2,1)}) custom-call(s32[3,128]{1,0:T(4,128)S(1)} %broadcast_in_dim.36.refs_0_, bf16[4,512,512]{2,1,0:T(8,128)(2,1)S(1)} %norm_rows.1.x_ref.refs_1_, f32[512,128]{1,0:T(8,128)S(1)} %pad_maximum_fusion.5.refs_2_, f32[512,128]{1,0:T(8,128)S(1)} %pad_maximum_fusion.6.refs_3_, ...), custom_call_target="tpu_custom_call" | custom-call | flops 1073741824 | bytes 1048576 | tf_op jit(solution)/shard_map/attend/pallas_call | solution.py:668
  52.7 0.5 collective-permute-done.10
  53.2 0.8 %collective-permute-done.14.refs_10_ = bf16[256,512]{1,0:T(8,128)(2,1)S(1)} collective-permute-done((bf16[256,512]{1,0:T(8,128)(2,1)S(1)}, bf16[256,512]{1,0:T(8,128)(2,1)S(1)}, u32[]{:S(2)}, u32[]{:S(2)}) %collective-permute-start.14) | collective-permute-done | bytes 262176 | tf_op jit(solution)/shard_map/ppermute | solution.py:242
  54.1 0.1 pad_maximum_fusion.2
  54.1 0.1 collective-permute-start.17
  54.2 0.6 collective-permute-start.18
  54.8 0.5 collective-permute-start.15
  55.3 0.9 %collective-permute-start.16 = (bf16[256,512]{1,0:T(8,128)(2,1)S(1)}, bf16[256,512]{1,0:T(8,128)(2,1)S(1)}, u32[]{:S(2)}, u32[]{:S(2)}) collective-permute-start(bf16[256,512]{1,0:T(8,128)(2,1)S(1)} %collective-permute-done.12.refs_9_), channel_id=1, source_target_pairs={{0,17},{1,8},{2,19},{3,10},{4,21},{5,12},{6,23},{7,14},{8,25},{9,0... | collective-permute-start | bytes 786440 | tf_op jit(solution)/shard_map/ppermute | solution.py:242
  56.2 1.0 %collective-permute-done.18.refs_13_ = bf16[512,512]{1,0:T(8,128)(2,1)S(1)} collective-permute-done((bf16[512,512]{1,0:T(8,128)(2,1)S(1)}, bf16[512,512]{1,0:T(8,128)(2,1)S(1)}, u32[]{:S(2)}, u32[]{:S(2)}) %collective-permute-start.18) | collective-permute-done | bytes 524320 | tf_op jit(solution)/shard_map/ppermute | solution.py:242
  57.2 4.9 %attend.4 = (bf16[64,1024]{1,0:T(8,128)(2,1)}, bf16[256,1024]{1,0:T(8,128)(2,1)}) custom-call(s32[3,128]{1,0:T(4,128)S(1)} %broadcast_in_dim.36.refs_0_, bf16[4,512,512]{2,1,0:T(8,128)(2,1)S(1)} %norm_rows.1.x_ref.refs_1_, f32[512,128]{1,0:T(8,128)S(1)} %pad_maximum_fusion.5.refs_2_, ...), custom_call_target="tpu_custom_call", output_to_operand_aliasing={{0}: (14, {}), {1}: (15, {})} | custom-call | flops 2147483648 | bytes 2097152 | tf_op jit(solution)/shard_map/attend/pallas_call | solution.py:668
  62.1 0.9 %collective-permute-done.16.refs_13_ = bf16[256,512]{1,0:T(8,128)(2,1)S(1)} collective-permute-done((bf16[256,512]{1,0:T(8,128)(2,1)S(1)}, bf16[256,512]{1,0:T(8,128)(2,1)S(1)}, u32[]{:S(2)}, u32[]{:S(2)}) %collective-permute-start.16) | collective-permute-done | bytes 262176 | tf_op jit(solution)/shard_map/ppermute | solution.py:242
  63.1 3.4 %attend.5 = (bf16[64,1024]{1,0:T(8,128)(2,1)}, bf16[256,1024]{1,0:T(8,128)(2,1)}) custom-call(s32[3,128]{1,0:T(4,128)S(1)} %broadcast_in_dim.36.refs_0_, bf16[4,512,512]{2,1,0:T(8,128)(2,1)S(1)} %norm_rows.1.x_ref.refs_1_, f32[512,128]{1,0:T(8,128)S(1)} %pad_maximum_fusion.5.refs_2_, ...), custom_call_target="tpu_custom_call", output_to_operand_aliasing={{0}: (14, {}), {1}: (15, {})} | custom-call | flops 1073741824 | bytes 1048576 | tf_op jit(solution)/shard_map/attend/pallas_call | solution.py:668
  (35 shorter events, 0.4 us)
Async XLA Ops:
  0.6 10.4 %copy-start = (s32[1,4]{1,0:T(1,128)S(1)}, s32[1,4]{1,0:T(1,128)}, u32[]{:S(2)}) copy-start(s32[1,4]{1,0:T(1,128)} %param.28) | copy-start | bytes 52
  2.0 18.9 %collective-permute-start = (bf16[608,512]{1,0:T(8,128)(2,1)S(1)}, bf16[608,512]{1,0:T(8,128)(2,1)S(1)}, u32[]{:S(2)}, u32[]{:S(2)}) collective-permute-start(bf16[608,512]{1,0:T(8,128)(2,1)S(1)} %get-tuple-element.50.own_ref.refs_0_.refs_8_), channel_id=1, source_target_pairs={{0,8},{1,17},{2,10},{3,19},{4,12},{5,21},{6,14},{7,23},{8,0},{9,25... | collective-permute-start | bytes 1867784 | tf_op jit(solution)/shard_map/ppermute | solution.py:242
  5.0 15.9 %collective-permute-start.1 = (bf16[608,512]{1,0:T(8,128)(2,1)S(1)}, bf16[608,512]{1,0:T(8,128)(2,1)S(1)}, u32[]{:S(2)}, u32[]{:S(2)}) collective-permute-start(bf16[608,512]{1,0:T(8,128)(2,1)S(1)} %get-tuple-element.50.own_ref.refs_0_.refs_8_), channel_id=1, source_target_pairs={{0,16},{1,9},{2,18},{3,11},{4,20},{5,13},{6,22},{7,15},{8,24},{9,1... | collective-permute-start | bytes 1867784 | tf_op jit(solution)/shard_map/ppermute | solution.py:242
  6.5 11.1 %collective-permute-start.2 = (bf16[256,512]{1,0:T(8,128)(2,1)S(1)}, bf16[256,512]{1,0:T(8,128)(2,1)S(1)}, u32[]{:S(2)}, u32[]{:S(2)}) collective-permute-start(bf16[256,512]{1,0:T(8,128)(2,1)S(1)} %get-tuple-element.43), channel_id=1, source_target_pairs={{0,2},{1,3},{2,4},{3,5},{4,6},{5,7},{6,0},{7,1},{8,10},{9,11},{10,... | collective-permute-start | bytes 786440 | tf_op jit(solution)/shard_map/ppermute | solution.py:242
  8.1 12.8 %collective-permute-start.3 = (bf16[256,512]{1,0:T(8,128)(2,1)S(1)}, bf16[256,512]{1,0:T(8,128)(2,1)S(1)}, u32[]{:S(2)}, u32[]{:S(2)}) collective-permute-start(bf16[256,512]{1,0:T(8,128)(2,1)S(1)} %get-tuple-element.43), channel_id=1, source_target_pairs={{0,6},{1,7},{2,0},{3,1},{4,2},{5,3},{6,4},{7,5},{8,14},{9,15},{10,... | collective-permute-start | bytes 786440 | tf_op jit(solution)/shard_map/ppermute | solution.py:242
  21.1 20.0 %collective-permute-start.8 = (bf16[1056,512]{1,0:T(8,128)(2,1)S(1)}, bf16[1056,512]{1,0:T(8,128)(2,1)S(1)}, u32[]{:S(2)}, u32[]{:S(2)}) collective-permute-start(bf16[1056,512]{1,0:T(8,128)(2,1)S(1)} %pad_maximum_fusion.1), channel_id=1, source_target_pairs={{0,1},{1,0},{2,3},{3,2},{4,5},{5,4},{6,7},{7,6},{8,9},{9,8},{10,11... | collective-permute-start | bytes 3244040 | tf_op jit(solution)/shard_map/ppermute | solution.py:242
  21.3 16.2 %collective-permute-start.5 = (bf16[512,512]{1,0:T(8,128)(2,1)S(1)}, bf16[512,512]{1,0:T(8,128)(2,1)S(1)}, u32[]{:S(2)}, u32[]{:S(2)}) collective-permute-start(bf16[512,512]{1,0:T(8,128)(2,1)S(1)} %pad_maximum_fusion.3), channel_id=1, source_target_pairs={{0,2},{1,3},{2,4},{3,5},{4,6},{5,7},{6,0},{7,1},{8,10},{9,11},{10,... | collective-permute-start | bytes 1572872 | tf_op jit(solution)/shard_map/ppermute | solution.py:242
  22.5 18.7 %collective-permute-start.4 = (bf16[608,512]{1,0:T(8,128)(2,1)S(1)}, bf16[608,512]{1,0:T(8,128)(2,1)S(1)}, u32[]{:S(2)}, u32[]{:S(2)}) collective-permute-start(bf16[608,512]{1,0:T(8,128)(2,1)S(1)} %collective-permute-done.side_ref.refs_1_.refs_9_), channel_id=1, source_target_pairs={{0,16},{1,9},{2,18},{3,11},{4,20},{5,13},{6,22},{7,15},{8,24},{9,1... | collective-permute-start | bytes 1867784 | tf_op jit(solution)/shard_map/ppermute | solution.py:242
  23.1 18.1 %collective-permute-start.7 = (bf16[512,512]{1,0:T(8,128)(2,1)S(1)}, bf16[512,512]{1,0:T(8,128)(2,1)S(1)}, u32[]{:S(2)}, u32[]{:S(2)}) collective-permute-start(bf16[512,512]{1,0:T(8,128)(2,1)S(1)} %constant_dynamic-update-slice_fusion.refs_8_), channel_id=1, source_target_pairs={{0,16},{1,9},{2,18},{3,11},{4,20},{5,13},{6,22},{7,15},{8,24},{9,1... | collective-permute-start | bytes 1572872 | tf_op jit(solution)/shard_map/ppermute | solution.py:242
  24.7 12.9 %collective-permute-start.6 = (bf16[256,512]{1,0:T(8,128)(2,1)S(1)}, bf16[256,512]{1,0:T(8,128)(2,1)S(1)}, u32[]{:S(2)}, u32[]{:S(2)}) collective-permute-start(bf16[256,512]{1,0:T(8,128)(2,1)S(1)} %collective-permute-done.3), channel_id=1, source_target_pairs={{0,8},{1,17},{2,10},{3,19},{4,12},{5,21},{6,14},{7,23},{8,0},{9,25... | collective-permute-start | bytes 786440 | tf_op jit(solution)/shard_map/ppermute | solution.py:242
  41.2 5.9 %copy-start.1 = (bf16[1,1,256,2048]{3,2,1,0:T(8,128)(2,1)S(1)}, bf16[1,1,256,2048]{3,2,1,0:T(8,128)(2,1)}, u32[]{:S(2)}) copy-start(bf16[1,1,256,2048]{3,2,1,0:T(8,128)(2,1)} %param.16) | copy-start | bytes 3145732
  41.2 5.9 %copy-start.2 = (f32[2048]{0:T(1024)S(1)}, f32[2048]{0:T(1024)}, u32[]{:S(2)}) copy-start(f32[2048]{0:T(1024)} %param.17) | copy-start | bytes 24580
  41.3 11.9 %collective-permute-start.13 = (bf16[1536,512]{1,0:T(8,128)(2,1)S(1)}, bf16[1536,512]{1,0:T(8,128)(2,1)S(1)}, u32[]{:S(2)}, u32[]{:S(2)}) collective-permute-start(bf16[1536,512]{1,0:T(8,128)(2,1)S(1)} %pad_maximum_fusion), channel_id=1, source_target_pairs={{0,1},{1,0},{2,3},{3,2},{4,5},{5,4},{6,7},{7,6},{8,9},{9,8},{10,11... | collective-permute-start | bytes 4718600 | tf_op jit(solution)/shard_map/ppermute | solution.py:242
  41.4 4.2 %collective-permute-start.9 = (bf16[352,512]{1,0:T(8,128)(2,1)S(1)}, bf16[352,512]{1,0:T(8,128)(2,1)S(1)}, u32[]{:S(2)}, u32[]{:S(2)}) collective-permute-start(bf16[352,512]{1,0:T(8,128)(2,1)S(1)} %slice.30), channel_id=1, source_target_pairs={{0,1},{1,0},{2,3},{3,2},{4,5},{5,4},{6,7},{7,6},{8,9},{9,8},{10,11... | collective-permute-start | bytes 1081352 | tf_op jit(solution)/shard_map/ppermute | solution.py:242
  42.0 11.2 %collective-permute-start.11 = (bf16[256,512]{1,0:T(8,128)(2,1)S(1)}, bf16[256,512]{1,0:T(8,128)(2,1)S(1)}, u32[]{:S(2)}, u32[]{:S(2)}) collective-permute-start(bf16[256,512]{1,0:T(8,128)(2,1)S(1)} %collective-permute-done.6), channel_id=1, source_target_pairs={{0,16},{1,9},{2,18},{3,11},{4,20},{5,13},{6,22},{7,15},{8,24},{9,1... | collective-permute-start | bytes 786440 | tf_op jit(solution)/shard_map/ppermute | solution.py:242
  42.6 10.6 %collective-permute-start.10 = (bf16[256,512]{1,0:T(8,128)(2,1)S(1)}, bf16[256,512]{1,0:T(8,128)(2,1)S(1)}, u32[]{:S(2)}, u32[]{:S(2)}) collective-permute-start(bf16[256,512]{1,0:T(8,128)(2,1)S(1)} %slice.31), channel_id=1, source_target_pairs={{0,2},{1,3},{2,4},{3,5},{4,6},{5,7},{6,0},{7,1},{8,10},{9,11},{10,... | collective-permute-start | bytes 786440 | tf_op jit(solution)/shard_map/ppermute | solution.py:242
  44.2 9.0 %collective-permute-start.12 = (bf16[256,512]{1,0:T(8,128)(2,1)S(1)}, bf16[256,512]{1,0:T(8,128)(2,1)S(1)}, u32[]{:S(2)}, u32[]{:S(2)}) collective-permute-start(bf16[256,512]{1,0:T(8,128)(2,1)S(1)} %get-tuple-element.60.refs_8_), channel_id=1, source_target_pairs={{0,8},{1,17},{2,10},{3,19},{4,12},{5,21},{6,14},{7,23},{8,0},{9,25... | collective-permute-start | bytes 786440 | tf_op jit(solution)/shard_map/ppermute | solution.py:242
  45.7 8.4 %collective-permute-start.14 = (bf16[256,512]{1,0:T(8,128)(2,1)S(1)}, bf16[256,512]{1,0:T(8,128)(2,1)S(1)}, u32[]{:S(2)}, u32[]{:S(2)}) collective-permute-start(bf16[256,512]{1,0:T(8,128)(2,1)S(1)} %get-tuple-element.60.refs_8_), channel_id=1, source_target_pairs={{0,16},{1,9},{2,18},{3,11},{4,20},{5,13},{6,22},{7,15},{8,24},{9,1... | collective-permute-start | bytes 786440 | tf_op jit(solution)/shard_map/ppermute | solution.py:242
  48.0 1.2 %copy-start.3 = (f32[128]{0:T(128)S(1)}, f32[128]{0:T(128)}, u32[]{:S(2)}) copy-start(f32[128]{0:T(128)} %param.21) | copy-start | bytes 1540
  48.0 1.2 %copy-start.4 = (f32[128]{0:T(128)S(1)}, f32[128]{0:T(128)}, u32[]{:S(2)}) copy-start(f32[128]{0:T(128)} %param.22) | copy-start | bytes 1540
  54.1 9.0 %collective-permute-start.17 = (bf16[768,512]{1,0:T(8,128)(2,1)S(1)}, bf16[768,512]{1,0:T(8,128)(2,1)S(1)}, u32[]{:S(2)}, u32[]{:S(2)}) collective-permute-start(bf16[768,512]{1,0:T(8,128)(2,1)S(1)} %pad_maximum_fusion.2), channel_id=1, source_target_pairs={{0,1},{1,0},{2,3},{3,2},{4,5},{5,4},{6,7},{7,6},{8,9},{9,8},{10,11... | collective-permute-start | bytes 2359304 | tf_op jit(solution)/shard_map/ppermute | solution.py:242
  54.2 3.0 %collective-permute-start.18 = (bf16[512,512]{1,0:T(8,128)(2,1)S(1)}, bf16[512,512]{1,0:T(8,128)(2,1)S(1)}, u32[]{:S(2)}, u32[]{:S(2)}) collective-permute-start(bf16[512,512]{1,0:T(8,128)(2,1)S(1)} %constant_dynamic-update-slice_fusion.2.refs_11_), channel_id=1, source_target_pairs={{0,1},{1,0},{2,3},{3,2},{4,5},{5,4},{6,7},{7,6},{8,9},{9,8},{10,11... | collective-permute-start | bytes 1572872 | tf_op jit(solution)/shard_map/ppermute | solution.py:242
  54.8 7.4 %collective-permute-start.15 = (bf16[256,512]{1,0:T(8,128)(2,1)S(1)}, bf16[256,512]{1,0:T(8,128)(2,1)S(1)}, u32[]{:S(2)}, u32[]{:S(2)}) collective-permute-start(bf16[256,512]{1,0:T(8,128)(2,1)S(1)} %collective-permute-done.12.refs_9_), channel_id=1, source_target_pairs={{0,16},{1,9},{2,18},{3,11},{4,20},{5,13},{6,22},{7,15},{8,24},{9,1... | collective-permute-start | bytes 786440 | tf_op jit(solution)/shard_map/ppermute | solution.py:242
  55.3 7.8 %collective-permute-start.16 = (bf16[256,512]{1,0:T(8,128)(2,1)S(1)}, bf16[256,512]{1,0:T(8,128)(2,1)S(1)}, u32[]{:S(2)}, u32[]{:S(2)}) collective-permute-start(bf16[256,512]{1,0:T(8,128)(2,1)S(1)} %collective-permute-done.12.refs_9_), channel_id=1, source_target_pairs={{0,17},{1,8},{2,19},{3,10},{4,21},{5,12},{6,23},{7,14},{8,25},{9,0... | collective-permute-start | bytes 786440 | tf_op jit(solution)/shard_map/ppermute | solution.py:242

commit v4 on v3

--- a/solution.py
+++ b/solution.py
@@ -622,8 +622,8 @@
     )
 
     own_corner = permute(own_side, second_hop)
-    along = permute(jnp.concatenate([step_one, own_side[: 2 * head]], axis=0), ring_hop)
-    step_two, one_side = along[: 2 * head], along[2 * head :]
+    step_two = permute(step_one, ring_hop)
+    one_side = permute(own_side[: 2 * head], ring_hop)
     three_side = permute(step_three, first_hop)
     far = jnp.concatenate([step_one, step_three], axis=0)
     far_other = permute(far, second_hop)

time: 67.1 us -> 65.4 us (0.975)
  waiting for transfers between devices: 22.9 us -> 19.7 us
  starting transfers between devices: 20.8 us -> 22.3 us
    ppermute x19 -> x20, waiting for transfers between devices: 22.9 us -> 19.7 us  [permute(): return lax.ppermute(value, axes, hop)]
    ppermute x19 -> x20, starting transfers between devices: 20.8 us -> 22.3 us  [permute(): return lax.ppermute(value, axes, hop)]
  transfers between devices with their start and end apart: 19 -> 20, of which waited for: 8 -> 9; matrix products, arithmetic and copies ran while one was open for 6% -> 7% of each run, Pallas kernels for 16% -> 16%
where the time goes in v4:
time: 65.4 us; the launch traced here: 64.9 us
  starting transfers between devices  22.3 us (34%)
  waiting for transfers between devices  19.7 us (30%)
  Pallas kernels  15.2 us (23%)
  other arithmetic  3.65 us (6%)
  between operations  3.03 us (5%)
  local copies, waits for them, and re-layouts  0.98 us (1%)
    ppermute x20, starting transfers between devices, permute(): return lax.ppermute(value, axes, hop)  22.3 us
    ppermute x20, waiting for transfers between devices, permute(): return lax.ppermute(value, axes, hop)  19.7 us
    pallas_call x3, Pallas kernels, attend(): pl.pallas_call(functools.partial(attend_kernel, steps=steps, first=not re...  11.8 us
    reduce_sum x1, other arithmetic, shards_torus(): jnp.sum(jnp.where(member == jnp.arange(holder_slot.shape[0]), holder_slot...  2.02 us
    pallas_call x1, Pallas kernels, shards_torus(): pl.pallas_call(pack_kernel, out_shape=(jax.ShapeDtypeStruct((tail + slice...  1.32 us
  transfers between devices with their start and end apart: 20, of which 9 were waited for; matrix products, arithmetic and copies ran while one was open for 7% of the time, Pallas kernels for 16%

profile of v4, /device:TPU:0, one launch (start us, length us, event | category | flops | bytes accessed | tf_op | source)
XLA Modules:
  0.0 64.9 jit_solution(1034718550724122026)
XLA Ops:
  0.6 0.0 copy-start
  0.6 1.3 %pack.1 = (bf16[608,512]{1,0:T(8,128)(2,1)S(1)}, bf16[256,512]{1,0:T(8,128)(2,1)S(1)}) custom-call(bf16[64,512]{1,0:T(8,128)(2,1)} %bitcast.29, bf16[64,512]{1,0:T(8,128)(2,1)} %bitcast.30, bf16[512,128]{1,0:T(8,128)(2,1)} %query_ref.1, bf16[2,16,2048]{2,1,0:T(8,128)(2,1)} %down_ref.1, bf16[2,16,1024]{2,1,0:T(8,128)(2,1)} %up_ref.1, bf16[64,2048]{1,0:T(8,128)(2,1)} %bitcast.27), custom_call_target="tpu_custom_call" | custom-call | tf_op jit(solution)/shard_map/pack/pallas_call | solution.py:566
  2.0 3.0 %collective-permute-start = (bf16[608,512]{1,0:T(8,128)(2,1)S(1)}, bf16[608,512]{1,0:T(8,128)(2,1)S(1)}, u32[]{:S(2)}, u32[]{:S(2)}) collective-permute-start(bf16[608,512]{1,0:T(8,128)(2,1)S(1)} %get-tuple-element.50.own_ref.refs_0_.refs_8_), channel_id=1, source_target_pairs={{0,8},{1,17},{2,10},{3,19},{4,12},{5,21},{6,14},{7,23},{8,0},{9,25... | collective-permute-start | bytes 1867784 | tf_op jit(solution)/shard_map/ppermute | solution.py:242
  5.0 1.5 %collective-permute-start.1 = (bf16[608,512]{1,0:T(8,128)(2,1)S(1)}, bf16[608,512]{1,0:T(8,128)(2,1)S(1)}, u32[]{:S(2)}, u32[]{:S(2)}) collective-permute-start(bf16[608,512]{1,0:T(8,128)(2,1)S(1)} %get-tuple-element.50.own_ref.refs_0_.refs_8_), channel_id=1, source_target_pairs={{0,16},{1,9},{2,18},{3,11},{4,20},{5,13},{6,22},{7,15},{8,24},{9,1... | collective-permute-start | bytes 1867784 | tf_op jit(solution)/shard_map/ppermute | solution.py:242
  6.5 1.6 %collective-permute-start.2 = (bf16[256,512]{1,0:T(8,128)(2,1)S(1)}, bf16[256,512]{1,0:T(8,128)(2,1)S(1)}, u32[]{:S(2)}, u32[]{:S(2)}) collective-permute-start(bf16[256,512]{1,0:T(8,128)(2,1)S(1)} %get-tuple-element.43), channel_id=1, source_target_pairs={{0,2},{1,3},{2,4},{3,5},{4,6},{5,7},{6,0},{7,1},{8,10},{9,11},{10,... | collective-permute-start | bytes 786440 | tf_op jit(solution)/shard_map/ppermute | solution.py:242
  8.1 2.2 %collective-permute-start.3 = (bf16[256,512]{1,0:T(8,128)(2,1)S(1)}, bf16[256,512]{1,0:T(8,128)(2,1)S(1)}, u32[]{:S(2)}, u32[]{:S(2)}) collective-permute-start(bf16[256,512]{1,0:T(8,128)(2,1)S(1)} %get-tuple-element.43), channel_id=1, source_target_pairs={{0,6},{1,7},{2,0},{3,1},{4,2},{5,3},{6,4},{7,5},{8,14},{9,15},{10,... | collective-permute-start | bytes 786440 | tf_op jit(solution)/shard_map/ppermute | solution.py:242
  11.0 0.6 constant_dynamic-slice_fusion
  11.6 2.0 %fusion.1 = s32[]{:T(128)} fusion(s32[8]{0:T(128)} %param.29, s32[]{:T(128)} %bitcast.4), kind=kLoop, calls=%fused_computation.15 | loop fusion | flops 23 | bytes 40 | tf_op jit(solution)/shard_map/reduce_sum | solution.py:601
  13.6 0.1 concatenate.32
  15.0 1.0 %fusion = (f32[512,64]{1,0:T(8,128)S(1)}, f32[512,64]{1,0:T(8,128)S(1)}, f32[512,64]{1,0:T(8,128)S(1)}) fusion(f32[64]{0:T(128)S(1)} %multiply_power_fusion, f32[512]{0:T(512)S(1)} %convert_element_type.15), kind=kLoop, calls=%fused_computation.8 | loop fusion | flops 65536 | bytes 395520 | tf_op jit(solution)/shard_map/neg | solution.py:599
  16.0 0.1 pad_add_fusion
  16.1 0.1 pad_maximum_fusion.4.refs_2_
  16.3 0.1 pad_maximum_fusion.5.refs_3_
  16.4 1.2 %collective-permute-done.2 = bf16[256,512]{1,0:T(8,128)(2,1)S(1)} collective-permute-done((bf16[256,512]{1,0:T(8,128)(2,1)S(1)}, bf16[256,512]{1,0:T(8,128)(2,1)S(1)}, u32[]{:S(2)}, u32[]{:S(2)}) %collective-permute-start.2) | collective-permute-done | bytes 262176 | tf_op jit(solution)/shard_map/ppermute | solution.py:242
  17.6 3.3 %collective-permute-done.3 = bf16[256,512]{1,0:T(8,128)(2,1)S(1)} collective-permute-done((bf16[256,512]{1,0:T(8,128)(2,1)S(1)}, bf16[256,512]{1,0:T(8,128)(2,1)S(1)}, u32[]{:S(2)}, u32[]{:S(2)}) %collective-permute-start.3) | collective-permute-done | bytes 262176 | tf_op jit(solution)/shard_map/ppermute | solution.py:242
  20.9 0.1 broadcast_in_dim.36.refs_0_
  21.1 0.1 pad_maximum_fusion.1
  21.1 0.1 collective-permute-start.9
  21.2 0.6 collective-permute-start.4
  21.8 1.2 %collective-permute-start.6 = (bf16[256,512]{1,0:T(8,128)(2,1)S(1)}, bf16[256,512]{1,0:T(8,128)(2,1)S(1)}, u32[]{:S(2)}, u32[]{:S(2)}) collective-permute-start(bf16[256,512]{1,0:T(8,128)(2,1)S(1)} %slice.18), channel_id=1, source_target_pairs={{0,2},{1,3},{2,4},{3,5},{4,6},{5,7},{6,0},{7,1},{8,10},{9,11},{10,... | collective-permute-start | bytes 786440 | tf_op jit(solution)/shard_map/ppermute | solution.py:242
  23.1 1.5 %collective-permute-start.8 = (bf16[512,512]{1,0:T(8,128)(2,1)S(1)}, bf16[512,512]{1,0:T(8,128)(2,1)S(1)}, u32[]{:S(2)}, u32[]{:S(2)}) collective-permute-start(bf16[512,512]{1,0:T(8,128)(2,1)S(1)} %constant_dynamic-update-slice_fusion.refs_8_), channel_id=1, source_target_pairs={{0,16},{1,9},{2,18},{3,11},{4,20},{5,13},{6,22},{7,15},{8,24},{9,1... | collective-permute-start | bytes 1572872 | tf_op jit(solution)/shard_map/ppermute | solution.py:242
  24.7 1.4 %collective-permute-start.5 = (bf16[256,512]{1,0:T(8,128)(2,1)S(1)}, bf16[256,512]{1,0:T(8,128)(2,1)S(1)}, u32[]{:S(2)}, u32[]{:S(2)}) collective-permute-start(bf16[256,512]{1,0:T(8,128)(2,1)S(1)} %collective-permute-done.2), channel_id=1, source_target_pairs={{0,2},{1,3},{2,4},{3,5},{4,6},{5,7},{6,0},{7,1},{8,10},{9,11},{10,... | collective-permute-start | bytes 786440 | tf_op jit(solution)/shard_map/ppermute | solution.py:242
  26.1 6.7 %collective-permute-done.6 = bf16[256,512]{1,0:T(8,128)(2,1)S(1)} collective-permute-done((bf16[256,512]{1,0:T(8,128)(2,1)S(1)}, bf16[256,512]{1,0:T(8,128)(2,1)S(1)}, u32[]{:S(2)}, u32[]{:S(2)}) %collective-permute-start.6) | collective-permute-done | bytes 262176 | tf_op jit(solution)/shard_map/ppermute | solution.py:242
  32.8 1.1 %collective-permute-start.7 = (bf16[256,512]{1,0:T(8,128)(2,1)S(1)}, bf16[256,512]{1,0:T(8,128)(2,1)S(1)}, u32[]{:S(2)}, u32[]{:S(2)}) collective-permute-start(bf16[256,512]{1,0:T(8,128)(2,1)S(1)} %collective-permute-done.3), channel_id=1, source_target_pairs={{0,8},{1,17},{2,10},{3,19},{4,12},{5,21},{6,14},{7,23},{8,0},{9,25... | collective-permute-start | bytes 786440 | tf_op jit(solution)/shard_map/ppermute | solution.py:242
  33.8 4.2 %collective-permute-done.5.refs_8_ = bf16[256,512]{1,0:T(8,128)(2,1)S(1)} collective-permute-done((bf16[256,512]{1,0:T(8,128)(2,1)S(1)}, bf16[256,512]{1,0:T(8,128)(2,1)S(1)}, u32[]{:S(2)}, u32[]{:S(2)}) %collective-permute-start.5) | collective-permute-done | bytes 262176 | tf_op jit(solution)/shard_map/ppermute | solution.py:242
  38.1 1.3 %collective-permute-done.7 = bf16[256,512]{1,0:T(8,128)(2,1)S(1)} collective-permute-done((bf16[256,512]{1,0:T(8,128)(2,1)S(1)}, bf16[256,512]{1,0:T(8,128)(2,1)S(1)}, u32[]{:S(2)}, u32[]{:S(2)}) %collective-permute-start.7) | collective-permute-done | bytes 262176 | tf_op jit(solution)/shard_map/ppermute | solution.py:242
  39.4 0.1 pad_maximum_fusion
  39.5 0.4 collective-permute-start.14
  40.0 0.2 collective-permute-start.10
  40.2 1.4 %collective-permute-start.12 = (bf16[256,512]{1,0:T(8,128)(2,1)S(1)}, bf16[256,512]{1,0:T(8,128)(2,1)S(1)}, u32[]{:S(2)}, u32[]{:S(2)}) collective-permute-start(bf16[256,512]{1,0:T(8,128)(2,1)S(1)} %collective-permute-done.7), channel_id=1, source_target_pairs={{0,16},{1,9},{2,18},{3,11},{4,20},{5,13},{6,22},{7,15},{8,24},{9,1... | collective-permute-start | bytes 786440 | tf_op jit(solution)/shard_map/ppermute | solution.py:242
  41.6 0.9 %collective-permute-start.11 = (bf16[256,512]{1,0:T(8,128)(2,1)S(1)}, bf16[256,512]{1,0:T(8,128)(2,1)S(1)}, u32[]{:S(2)}, u32[]{:S(2)}) collective-permute-start(bf16[256,512]{1,0:T(8,128)(2,1)S(1)} %slice.23), channel_id=1, source_target_pairs={{0,2},{1,3},{2,4},{3,5},{4,6},{5,7},{6,0},{7,1},{8,10},{9,11},{10,... | collective-permute-start | bytes 786440 | tf_op jit(solution)/shard_map/ppermute | solution.py:242
  42.5 1.5 %collective-permute-start.13 = (bf16[256,512]{1,0:T(8,128)(2,1)S(1)}, bf16[256,512]{1,0:T(8,128)(2,1)S(1)}, u32[]{:S(2)}, u32[]{:S(2)}) collective-permute-start(bf16[256,512]{1,0:T(8,128)(2,1)S(1)} %collective-permute-done.5.refs_8_), channel_id=1, source_target_pairs={{0,8},{1,17},{2,10},{3,19},{4,12},{5,21},{6,14},{7,23},{8,0},{9,25... | collective-permute-start | bytes 786440 | tf_op jit(solution)/shard_map/ppermute | solution.py:242
  44.0 1.3 %collective-permute-start.15 = (bf16[256,512]{1,0:T(8,128)(2,1)S(1)}, bf16[256,512]{1,0:T(8,128)(2,1)S(1)}, u32[]{:S(2)}, u32[]{:S(2)}) collective-permute-start(bf16[256,512]{1,0:T(8,128)(2,1)S(1)} %collective-permute-done.5.refs_8_), channel_id=1, source_target_pairs={{0,16},{1,9},{2,18},{3,11},{4,20},{5,13},{6,22},{7,15},{8,24},{9,1... | collective-permute-start | bytes 786440 | tf_op jit(solution)/shard_map/ppermute | solution.py:242
  45.3 1.0 %norm_rows.1.x_ref.refs_1_ = bf16[4,512,512]{2,1,0:T(8,128)(2,1)S(1)} custom-call(bf16[608,512]{1,0:T(8,128)(2,1)S(1)} %get-tuple-element.50.own_ref.refs_0_.refs_8_, bf16[608,512]{1,0:T(8,128)(2,1)S(1)} %collective-permute-done.side_ref.refs_1_.refs_9_, bf16[608,512]{1,0:T(8,128)(2,1)S(1)} %collective-permute-done.1.other_ref.refs_2_.refs_10_, ...), custom_call_target="tpu_custom_call" | custom-call | bytes 4194304 | tf_op jit(solution)/shard_map/norm_rows/pallas_call | solution.py:646
  46.3 0.0 copy-start.4
  46.3 1.1 %adapter.1 = (bf16[256,128]{1,0:T(8,128)(2,1)S(1)}, bf16[128,1024]{1,0:T(8,128)(2,1)S(1)}) custom-call(bf16[4,512,512]{2,1,0:T(8,128)(2,1)S(1)} %norm_rows.1.x_ref.refs_1_, s32[1]{0:T(128)} %bitcast.5.slot_ref, bf16[608,512]{1,0:T(8,128)(2,1)S(1)} %get-tuple-element.50.own_ref.refs_0_.refs_8_, ...), custom_call_target="tpu_custom_call" | custom-call | flops 134217728 | bytes 2097152 | tf_op jit(solution)/shard_map/adapter/pallas_call | solution.py:654
  47.5 3.4 %attend.3 = (bf16[64,1024]{1,0:T(8,128)(2,1)}, bf16[256,1024]{1,0:T(8,128)(2,1)}) custom-call(s32[3,128]{1,0:T(4,128)S(1)} %broadcast_in_dim.36.refs_0_, bf16[4,512,512]{2,1,0:T(8,128)(2,1)S(1)} %norm_rows.1.x_ref.refs_1_, f32[512,128]{1,0:T(8,128)S(1)} %pad_maximum_fusion.4.refs_2_, f32[512,128]{1,0:T(8,128)S(1)} %pad_maximum_fusion.5.refs_3_, ...), custom_call_target="tpu_custom_call" | custom-call | flops 1073741824 | bytes 1048576 | tf_op jit(solution)/shard_map/attend/pallas_call | solution.py:668
  50.9 0.6 collective-permute-done.11
  51.6 0.7 %collective-permute-done.15.refs_10_ = bf16[256,512]{1,0:T(8,128)(2,1)S(1)} collective-permute-done((bf16[256,512]{1,0:T(8,128)(2,1)S(1)}, bf16[256,512]{1,0:T(8,128)(2,1)S(1)}, u32[]{:S(2)}, u32[]{:S(2)}) %collective-permute-start.15) | collective-permute-done | bytes 262176 | tf_op jit(solution)/shard_map/ppermute | solution.py:242
  52.3 0.1 pad_maximum_fusion.2
  52.3 0.1 collective-permute-start.18
  52.4 0.6 collective-permute-start.19
  53.0 1.3 %collective-permute-start.16 = (bf16[256,512]{1,0:T(8,128)(2,1)S(1)}, bf16[256,512]{1,0:T(8,128)(2,1)S(1)}, u32[]{:S(2)}, u32[]{:S(2)}) collective-permute-start(bf16[256,512]{1,0:T(8,128)(2,1)S(1)} %collective-permute-done.13.refs_9_), channel_id=1, source_target_pairs={{0,16},{1,9},{2,18},{3,11},{4,20},{5,13},{6,22},{7,15},{8,24},{9,1... | collective-permute-start | bytes 786440 | tf_op jit(solution)/shard_map/ppermute | solution.py:242
  54.4 0.3 collective-permute-start.17
  54.7 0.7 %collective-permute-done.19.refs_13_ = bf16[512,512]{1,0:T(8,128)(2,1)S(1)} collective-permute-done((bf16[512,512]{1,0:T(8,128)(2,1)S(1)}, bf16[512,512]{1,0:T(8,128)(2,1)S(1)}, u32[]{:S(2)}, u32[]{:S(2)}) %collective-permute-start.19) | collective-permute-done | bytes 524320 | tf_op jit(solution)/shard_map/ppermute | solution.py:242
  55.4 4.9 %attend.4 = (bf16[64,1024]{1,0:T(8,128)(2,1)}, bf16[256,1024]{1,0:T(8,128)(2,1)}) custom-call(s32[3,128]{1,0:T(4,128)S(1)} %broadcast_in_dim.36.refs_0_, bf16[4,512,512]{2,1,0:T(8,128)(2,1)S(1)} %norm_rows.1.x_ref.refs_1_, f32[512,128]{1,0:T(8,128)S(1)} %pad_maximum_fusion.4.refs_2_, ...), custom_call_target="tpu_custom_call", output_to_operand_aliasing={{0}: (14, {}), {1}: (15, {})} | custom-call | flops 2147483648 | bytes 2097152 | tf_op jit(solution)/shard_map/attend/pallas_call | solution.py:668
  60.4 0.9 %collective-permute-done.17.refs_13_ = bf16[256,512]{1,0:T(8,128)(2,1)S(1)} collective-permute-done((bf16[256,512]{1,0:T(8,128)(2,1)S(1)}, bf16[256,512]{1,0:T(8,128)(2,1)S(1)}, u32[]{:S(2)}, u32[]{:S(2)}) %collective-permute-start.17) | collective-permute-done | bytes 262176 | tf_op jit(solution)/shard_map/ppermute | solution.py:242
  61.3 3.4 %attend.5 = (bf16[64,1024]{1,0:T(8,128)(2,1)}, bf16[256,1024]{1,0:T(8,128)(2,1)}) custom-call(s32[3,128]{1,0:T(4,128)S(1)} %broadcast_in_dim.36.refs_0_, bf16[4,512,512]{2,1,0:T(8,128)(2,1)S(1)} %norm_rows.1.x_ref.refs_1_, f32[512,128]{1,0:T(8,128)S(1)} %pad_maximum_fusion.4.refs_2_, ...), custom_call_target="tpu_custom_call", output_to_operand_aliasing={{0}: (14, {}), {1}: (15, {})} | custom-call | flops 1073741824 | bytes 1048576 | tf_op jit(solution)/shard_map/attend/pallas_call | solution.py:668
  (35 shorter events, 0.3 us)
Async XLA Ops:
  0.6 10.4 %copy-start = (s32[1,4]{1,0:T(1,128)S(1)}, s32[1,4]{1,0:T(1,128)}, u32[]{:S(2)}) copy-start(s32[1,4]{1,0:T(1,128)} %param.28) | copy-start | bytes 52
  2.0 18.9 %collective-permute-start = (bf16[608,512]{1,0:T(8,128)(2,1)S(1)}, bf16[608,512]{1,0:T(8,128)(2,1)S(1)}, u32[]{:S(2)}, u32[]{:S(2)}) collective-permute-start(bf16[608,512]{1,0:T(8,128)(2,1)S(1)} %get-tuple-element.50.own_ref.refs_0_.refs_8_), channel_id=1, source_target_pairs={{0,8},{1,17},{2,10},{3,19},{4,12},{5,21},{6,14},{7,23},{8,0},{9,25... | collective-permute-start | bytes 1867784 | tf_op jit(solution)/shard_map/ppermute | solution.py:242
  5.0 15.9 %collective-permute-start.1 = (bf16[608,512]{1,0:T(8,128)(2,1)S(1)}, bf16[608,512]{1,0:T(8,128)(2,1)S(1)}, u32[]{:S(2)}, u32[]{:S(2)}) collective-permute-start(bf16[608,512]{1,0:T(8,128)(2,1)S(1)} %get-tuple-element.50.own_ref.refs_0_.refs_8_), channel_id=1, source_target_pairs={{0,16},{1,9},{2,18},{3,11},{4,20},{5,13},{6,22},{7,15},{8,24},{9,1... | collective-permute-start | bytes 1867784 | tf_op jit(solution)/shard_map/ppermute | solution.py:242
  6.5 11.1 %collective-permute-start.2 = (bf16[256,512]{1,0:T(8,128)(2,1)S(1)}, bf16[256,512]{1,0:T(8,128)(2,1)S(1)}, u32[]{:S(2)}, u32[]{:S(2)}) collective-permute-start(bf16[256,512]{1,0:T(8,128)(2,1)S(1)} %get-tuple-element.43), channel_id=1, source_target_pairs={{0,2},{1,3},{2,4},{3,5},{4,6},{5,7},{6,0},{7,1},{8,10},{9,11},{10,... | collective-permute-start | bytes 786440 | tf_op jit(solution)/shard_map/ppermute | solution.py:242
  8.1 12.8 %collective-permute-start.3 = (bf16[256,512]{1,0:T(8,128)(2,1)S(1)}, bf16[256,512]{1,0:T(8,128)(2,1)S(1)}, u32[]{:S(2)}, u32[]{:S(2)}) collective-permute-start(bf16[256,512]{1,0:T(8,128)(2,1)S(1)} %get-tuple-element.43), channel_id=1, source_target_pairs={{0,6},{1,7},{2,0},{3,1},{4,2},{5,3},{6,4},{7,5},{8,14},{9,15},{10,... | collective-permute-start | bytes 786440 | tf_op jit(solution)/shard_map/ppermute | solution.py:242
  21.1 18.3 %collective-permute-start.9 = (bf16[1056,512]{1,0:T(8,128)(2,1)S(1)}, bf16[1056,512]{1,0:T(8,128)(2,1)S(1)}, u32[]{:S(2)}, u32[]{:S(2)}) collective-permute-start(bf16[1056,512]{1,0:T(8,128)(2,1)S(1)} %pad_maximum_fusion.1), channel_id=1, source_target_pairs={{0,1},{1,0},{2,3},{3,2},{4,5},{5,4},{6,7},{7,6},{8,9},{9,8},{10,11... | collective-permute-start | bytes 3244040 | tf_op jit(solution)/shard_map/ppermute | solution.py:242
  21.2 18.2 %collective-permute-start.4 = (bf16[608,512]{1,0:T(8,128)(2,1)S(1)}, bf16[608,512]{1,0:T(8,128)(2,1)S(1)}, u32[]{:S(2)}, u32[]{:S(2)}) collective-permute-start(bf16[608,512]{1,0:T(8,128)(2,1)S(1)} %collective-permute-done.side_ref.refs_1_.refs_9_), channel_id=1, source_target_pairs={{0,16},{1,9},{2,18},{3,11},{4,20},{5,13},{6,22},{7,15},{8,24},{9,1... | collective-permute-start | bytes 1867784 | tf_op jit(solution)/shard_map/ppermute | solution.py:242
  21.8 10.9 %collective-permute-start.6 = (bf16[256,512]{1,0:T(8,128)(2,1)S(1)}, bf16[256,512]{1,0:T(8,128)(2,1)S(1)}, u32[]{:S(2)}, u32[]{:S(2)}) collective-permute-start(bf16[256,512]{1,0:T(8,128)(2,1)S(1)} %slice.18), channel_id=1, source_target_pairs={{0,2},{1,3},{2,4},{3,5},{4,6},{5,7},{6,0},{7,1},{8,10},{9,11},{10,... | collective-permute-start | bytes 786440 | tf_op jit(solution)/shard_map/ppermute | solution.py:242
  23.1 22.2 %copy-start.1 = (bf16[1,1,256,2048]{3,2,1,0:T(8,128)(2,1)S(1)}, bf16[1,1,256,2048]{3,2,1,0:T(8,128)(2,1)}, u32[]{:S(2)}) copy-start(bf16[1,1,256,2048]{3,2,1,0:T(8,128)(2,1)} %param.16) | copy-start | bytes 3145732
  23.1 22.2 %copy-start.2 = (f32[2048]{0:T(1024)S(1)}, f32[2048]{0:T(1024)}, u32[]{:S(2)}) copy-start(f32[2048]{0:T(1024)} %param.17) | copy-start | bytes 24580
  23.1 16.3 %collective-permute-start.8 = (bf16[512,512]{1,0:T(8,128)(2,1)S(1)}, bf16[512,512]{1,0:T(8,128)(2,1)S(1)}, u32[]{:S(2)}, u32[]{:S(2)}) collective-permute-start(bf16[512,512]{1,0:T(8,128)(2,1)S(1)} %constant_dynamic-update-slice_fusion.refs_8_), channel_id=1, source_target_pairs={{0,16},{1,9},{2,18},{3,11},{4,20},{5,13},{6,22},{7,15},{8,24},{9,1... | collective-permute-start | bytes 1572872 | tf_op jit(solution)/shard_map/ppermute | solution.py:242
  24.7 13.4 %collective-permute-start.5 = (bf16[256,512]{1,0:T(8,128)(2,1)S(1)}, bf16[256,512]{1,0:T(8,128)(2,1)S(1)}, u32[]{:S(2)}, u32[]{:S(2)}) collective-permute-start(bf16[256,512]{1,0:T(8,128)(2,1)S(1)} %collective-permute-done.2), channel_id=1, source_target_pairs={{0,2},{1,3},{2,4},{3,5},{4,6},{5,7},{6,0},{7,1},{8,10},{9,11},{10,... | collective-permute-start | bytes 786440 | tf_op jit(solution)/shard_map/ppermute | solution.py:242
  32.8 6.7 %collective-permute-start.7 = (bf16[256,512]{1,0:T(8,128)(2,1)S(1)}, bf16[256,512]{1,0:T(8,128)(2,1)S(1)}, u32[]{:S(2)}, u32[]{:S(2)}) collective-permute-start(bf16[256,512]{1,0:T(8,128)(2,1)S(1)} %collective-permute-done.3), channel_id=1, source_target_pairs={{0,8},{1,17},{2,10},{3,19},{4,12},{5,21},{6,14},{7,23},{8,0},{9,25... | collective-permute-start | bytes 786440 | tf_op jit(solution)/shard_map/ppermute | solution.py:242
  39.5 12.0 %collective-permute-start.14 = (bf16[1536,512]{1,0:T(8,128)(2,1)S(1)}, bf16[1536,512]{1,0:T(8,128)(2,1)S(1)}, u32[]{:S(2)}, u32[]{:S(2)}) collective-permute-start(bf16[1536,512]{1,0:T(8,128)(2,1)S(1)} %pad_maximum_fusion), channel_id=1, source_target_pairs={{0,1},{1,0},{2,3},{3,2},{4,5},{5,4},{6,7},{7,6},{8,9},{9,8},{10,11... | collective-permute-start | bytes 4718600 | tf_op jit(solution)/shard_map/ppermute | solution.py:242
  40.0 4.0 %collective-permute-start.10 = (bf16[352,512]{1,0:T(8,128)(2,1)S(1)}, bf16[352,512]{1,0:T(8,128)(2,1)S(1)}, u32[]{:S(2)}, u32[]{:S(2)}) collective-permute-start(bf16[352,512]{1,0:T(8,128)(2,1)S(1)} %slice.22), channel_id=1, source_target_pairs={{0,1},{1,0},{2,3},{3,2},{4,5},{5,4},{6,7},{7,6},{8,9},{9,8},{10,11... | collective-permute-start | bytes 1081352 | tf_op jit(solution)/shard_map/ppermute | solution.py:242
  40.2 11.3 %collective-permute-start.12 = (bf16[256,512]{1,0:T(8,128)(2,1)S(1)}, bf16[256,512]{1,0:T(8,128)(2,1)S(1)}, u32[]{:S(2)}, u32[]{:S(2)}) collective-permute-start(bf16[256,512]{1,0:T(8,128)(2,1)S(1)} %collective-permute-done.7), channel_id=1, source_target_pairs={{0,16},{1,9},{2,18},{3,11},{4,20},{5,13},{6,22},{7,15},{8,24},{9,1... | collective-permute-start | bytes 786440 | tf_op jit(solution)/shard_map/ppermute | solution.py:242
  41.6 9.9 %collective-permute-start.11 = (bf16[256,512]{1,0:T(8,128)(2,1)S(1)}, bf16[256,512]{1,0:T(8,128)(2,1)S(1)}, u32[]{:S(2)}, u32[]{:S(2)}) collective-permute-start(bf16[256,512]{1,0:T(8,128)(2,1)S(1)} %slice.23), channel_id=1, source_target_pairs={{0,2},{1,3},{2,4},{3,5},{4,6},{5,7},{6,0},{7,1},{8,10},{9,11},{10,... | collective-permute-start | bytes 786440 | tf_op jit(solution)/shard_map/ppermute | solution.py:242
  42.5 9.0 %collective-permute-start.13 = (bf16[256,512]{1,0:T(8,128)(2,1)S(1)}, bf16[256,512]{1,0:T(8,128)(2,1)S(1)}, u32[]{:S(2)}, u32[]{:S(2)}) collective-permute-start(bf16[256,512]{1,0:T(8,128)(2,1)S(1)} %collective-permute-done.5.refs_8_), channel_id=1, source_target_pairs={{0,8},{1,17},{2,10},{3,19},{4,12},{5,21},{6,14},{7,23},{8,0},{9,25... | collective-permute-start | bytes 786440 | tf_op jit(solution)/shard_map/ppermute | solution.py:242
  44.0 8.3 %collective-permute-start.15 = (bf16[256,512]{1,0:T(8,128)(2,1)S(1)}, bf16[256,512]{1,0:T(8,128)(2,1)S(1)}, u32[]{:S(2)}, u32[]{:S(2)}) collective-permute-start(bf16[256,512]{1,0:T(8,128)(2,1)S(1)} %collective-permute-done.5.refs_8_), channel_id=1, source_target_pairs={{0,16},{1,9},{2,18},{3,11},{4,20},{5,13},{6,22},{7,15},{8,24},{9,1... | collective-permute-start | bytes 786440 | tf_op jit(solution)/shard_map/ppermute | solution.py:242
  46.3 1.2 %copy-start.3 = (f32[128]{0:T(128)S(1)}, f32[128]{0:T(128)}, u32[]{:S(2)}) copy-start(f32[128]{0:T(128)} %param.21) | copy-start | bytes 1540
  46.3 1.2 %copy-start.4 = (f32[128]{0:T(128)S(1)}, f32[128]{0:T(128)}, u32[]{:S(2)}) copy-start(f32[128]{0:T(128)} %param.22) | copy-start | bytes 1540
  52.3 9.0 %collective-permute-start.18 = (bf16[768,512]{1,0:T(8,128)(2,1)S(1)}, bf16[768,512]{1,0:T(8,128)(2,1)S(1)}, u32[]{:S(2)}, u32[]{:S(2)}) collective-permute-start(bf16[768,512]{1,0:T(8,128)(2,1)S(1)} %pad_maximum_fusion.2), channel_id=1, source_target_pairs={{0,1},{1,0},{2,3},{3,2},{4,5},{5,4},{6,7},{7,6},{8,9},{9,8},{10,11... | collective-permute-start | bytes 2359304 | tf_op jit(solution)/shard_map/ppermute | solution.py:242
  52.4 3.0 %collective-permute-start.19 = (bf16[512,512]{1,0:T(8,128)(2,1)S(1)}, bf16[512,512]{1,0:T(8,128)(2,1)S(1)}, u32[]{:S(2)}, u32[]{:S(2)}) collective-permute-start(bf16[512,512]{1,0:T(8,128)(2,1)S(1)} %constant_dynamic-update-slice_fusion.2.refs_11_), channel_id=1, source_target_pairs={{0,1},{1,0},{2,3},{3,2},{4,5},{5,4},{6,7},{7,6},{8,9},{9,8},{10,11... | collective-permute-start | bytes 1572872 | tf_op jit(solution)/shard_map/ppermute | solution.py:242
  53.0 7.4 %collective-permute-start.16 = (bf16[256,512]{1,0:T(8,128)(2,1)S(1)}, bf16[256,512]{1,0:T(8,128)(2,1)S(1)}, u32[]{:S(2)}, u32[]{:S(2)}) collective-permute-start(bf16[256,512]{1,0:T(8,128)(2,1)S(1)} %collective-permute-done.13.refs_9_), channel_id=1, source_target_pairs={{0,16},{1,9},{2,18},{3,11},{4,20},{5,13},{6,22},{7,15},{8,24},{9,1... | collective-permute-start | bytes 786440 | tf_op jit(solution)/shard_map/ppermute | solution.py:242
  54.4 6.9 %collective-permute-start.17 = (bf16[256,512]{1,0:T(8,128)(2,1)S(1)}, bf16[256,512]{1,0:T(8,128)(2,1)S(1)}, u32[]{:S(2)}, u32[]{:S(2)}) collective-permute-start(bf16[256,512]{1,0:T(8,128)(2,1)S(1)} %collective-permute-done.13.refs_9_), channel_id=1, source_target_pairs={{0,17},{1,8},{2,19},{3,10},{4,21},{5,12},{6,23},{7,14},{8,25},{9,0... | collective-permute-start | bytes 786440 | tf_op jit(solution)/shard_map/ppermute | solution.py:242
